TPU v7x, 256 devices: a whole 4x4x8 slice. The times are simulated.
256 devices in a mesh: gx: 8 (over y, x_hi), gy: 32 (over z, x_lo, core).
Axes of the slice: x: 4 (x_hi: 2, x_lo: 2; x = x_hi * 2 + x_lo), y: 4, z: 8, core: 2. Of those that a mesh axis runs over, the one named last changes fastest.
Arguments:
- positions: float32 [3, 64, 64, 512], P(None, 'gx', 'gy'), may hold values from 0 to 1
- charges: float32 [64, 64, 512], P('gx', 'gy'), may hold values from -0.24 to 0.24
- counts: int32 [64, 64, 8], P('gx', 'gy'), may hold values from 16 to 64, as said below
- up_ops: float32 [3, 296, 296], replicated, may hold values from -0.375 to 0.375
- m2l_ops: float32 [3, 8, 296, 296], replicated, may hold values from -0.125 to 0.125
- down_ops: float32 [2, 2, 296, 296], replicated, may hold values from -0.375 to 0.375
- box_lists: int32 [224, 8], replicated, may hold values from 0 to 127, as said below
Outputs:
- potential: float32 [64, 64, 512], P('gx', 'gy')
Inputs may be any that keep to these rules, and one draw needn't show every extreme that they name: `counts`: each leaf holds its particles in its first slots; in every column of 8 leaves along z some leaf is full. `box_lists`: rows o to o + 8 * (32 / 2^h) - 1 belong to level h; entry k of box b there is (b + s) modulo the level's box count, with a shift s of 1 or more that depends on the level and k only; entry 0 has s equal to half the level's box count.
All inputs are finite; a program needn't handle non-finite values.
Results may differ from a plain program's by a relative error of at most 0.0003.
Values sent between devices are 32-bit elements; how exact they have to be, the bound alone decides.
No kernel may reach another device: no remote copies, remote signals or barrier semaphores. Data moves between devices by JAX's collectives and lax.ppermute only.
A program may use at most 64 MiB of HBM per device.

v0:
```python
import jax
import jax.numpy as jnp
import numpy as np
from jax import lax
from jax.sharding import PartitionSpec as P

CXL = 8
CYL = 2
LZ = 8
PPL = 64
P_ORD = 8
LEV = 3


SOFTENING = 0.01
SURFACE_REACH = 1.05
PRECISE = lax.Precision.HIGHEST


def extended(cells, sides, width):
    for axis, dim in sides:
        count = lax.axis_size(axis)
        ends = count - 1
        head = lax.slice_in_dim(cells, 0, width, axis=dim)
        tail = lax.slice_in_dim(cells, cells.shape[dim] - width, cells.shape[dim], axis=dim)
        cells = jnp.concatenate(
            [
                lax.ppermute(tail, axis, [(i, (i + 1) % count) for i in range(ends)]),
                cells,
                lax.ppermute(head, axis, [((i + 1) % count, i) for i in range(ends)]),
            ],
            axis=dim,
        )
    return cells


def surface_points(order):
    lattice = np.linspace(-1.0, 1.0, order)
    points_list = []
    for first in range(order):
        for second in range(order):
            for third in range(order):
                if first in (0, order - 1) or second in (0, order - 1) or third in (0, order - 1):
                    points_list.append((lattice[first], lattice[second], lattice[third]))
    return jnp.asarray(np.array(points_list).T, dtype=jnp.float32)


def kernel(gap_x, gap_y, gap_z):
    return lax.rsqrt(gap_x * gap_x + gap_y * gap_y + gap_z * gap_z + SOFTENING)


def live_charges(charges, counts):
    size_x, size_y = (counts.shape[0], counts.shape[1])
    filled = jnp.broadcast_to(counts[..., None], (size_x, size_y, LZ, PPL)).reshape(
        size_x, size_y, LZ * PPL
    )
    within = jnp.arange(LZ * PPL, dtype=jnp.int32) % PPL
    occupied = within[None, None, :] < filled
    return (jnp.where(occupied, charges, 0.0), occupied)


def absolute(positions, anchor_x, anchor_y):
    size_x, size_y, slots = (positions.shape[1], positions.shape[2], positions.shape[3])
    along_x = anchor_x + jnp.arange(size_x).astype(jnp.float32)
    along_y = anchor_y + jnp.arange(size_y).astype(jnp.float32)
    along_z = (jnp.arange(slots) // PPL).astype(jnp.float32)
    return jnp.stack(
        [
            positions[0] + along_x[:, None, None],
            positions[1] + along_y[None, :, None],
            positions[2] + along_z[None, None, :],
        ]
    )


def near_field(padded, width_y):
    count_x = padded.shape[1] - 2
    blocks = padded.reshape(4, count_x + 2, width_y + 2, LZ, PPL)
    blocks = jnp.pad(blocks, ((0, 0), (0, 0), (0, 0), (1, 1), (0, 0)))
    rows_in = jnp.arange(PPL)[:, None]
    cols_in = jnp.arange(27 * PPL)[None, :]
    itself = cols_in == rows_in + 13 * PPL

    def one_column(column):
        window = lax.dynamic_slice_in_dim(blocks, column, 3, axis=1)
        target = window[:, 1, 1:-1, 1:-1, :]
        pieces = []
        for shift_x in range(3):
            for shift_y in range(3):
                for shift_z in range(3):
                    source = window[
                        :, shift_x, shift_y : shift_y + width_y, shift_z : shift_z + LZ, :
                    ]
                    pieces.append(
                        jnp.stack(
                            [
                                source[0] + (shift_x - 1.0),
                                source[1] + (shift_y - 1.0),
                                source[2] + (shift_z - 1.0),
                                source[3],
                            ]
                        )
                    )
        sources = jnp.concatenate(pieces, axis=-1)
        gap_x = target[0][..., :, None] - sources[0][..., None, :]
        gap_y = target[1][..., :, None] - sources[1][..., None, :]
        gap_z = target[2][..., :, None] - sources[2][..., None, :]
        strength = jnp.where(itself, 0.0, kernel(gap_x, gap_y, gap_z))
        return jnp.sum(strength * sources[3][..., None, :], axis=-1).reshape(width_y, LZ * PPL)

    return lax.map(one_column, jnp.arange(count_x))


def box_surface(unit_cube, height, column_x, group_y):
    span_y = CYL * 2**height
    centre = [(column_x + 0.5) * CXL, (group_y + 0.5) * span_y, 0.5 * LZ]
    halves = [0.5 * CXL, 0.5 * span_y, 0.5 * LZ]
    return jnp.stack(
        [
            centre[axis_id] + SURFACE_REACH * halves[axis_id] * unit_cube[axis_id]
            for axis_id in range(3)
        ]
    )


def check_terms(coords, weights, surfaces):
    per_level = []
    for surface in surfaces:
        strength = kernel(
            surface[0][:, None] - coords[0][None, :],
            surface[1][:, None] - coords[1][None, :],
            surface[2][:, None] - coords[2][None, :],
        )
        per_level.append(jnp.dot(strength, weights, precision=PRECISE))
    return jnp.stack(per_level)


def far_values(coords, surface, panel_now):
    strength = kernel(
        coords[0][:, None] - surface[0][None, :],
        coords[1][:, None] - surface[1][None, :],
        coords[2][:, None] - surface[2][None, :],
    )
    return jnp.dot(strength, panel_now, precision=PRECISE)


def box_multipoles(checks, height, up_ops):
    count_x, count_y = (checks.shape[0], checks.shape[1])
    summed = (
        checks[:, :, height - 1, :]
        .reshape(count_x, count_y >> height, 2**height, checks.shape[3])
        .sum(axis=2)
    )
    return jnp.dot(summed.reshape(-1, checks.shape[3]), up_ops[height - 1], precision=PRECISE)


def per_device(positions, charges, counts, up_ops, m2l_ops, down_ops, box_lists):
    unit_cube = surface_points(P_ORD)
    width_x, width_y = (positions.shape[1], positions.shape[2])
    index_x = lax.axis_index("gx")
    index_y = lax.axis_index("gy")
    devices_x = lax.axis_size("gx")
    devices_y = lax.axis_size("gy")
    weights, occupied = live_charges(charges, counts)
    local_rows = jnp.concatenate([positions, weights[None]], axis=0)
    padded = extended(local_rows, (("gx", 1), ("gy", 2)), 1)
    near_part = near_field(padded, width_y)
    coords = absolute(
        positions, (index_x * width_x).astype(jnp.float32), (index_y * width_y).astype(jnp.float32)
    )
    flat_coords = coords.reshape(3, -1)
    flat_weights = weights.reshape(-1)
    column_x = index_x.astype(jnp.float32)
    surfaces = [
        box_surface(unit_cube, height, column_x, (index_y >> height).astype(jnp.float32))
        for height in range(1, LEV + 1)
    ]
    own_checks = check_terms(flat_coords, flat_weights, surfaces)
    gathered = lax.all_gather(own_checks[None], ("gx", "gy"), axis=0, tiled=True)
    checks = gathered.reshape(devices_x, devices_y, own_checks.shape[0], own_checks.shape[1])
    multipoles = [box_multipoles(checks, height, up_ops) for height in range(1, LEV + 1)]
    panel_above = None
    for height in range(LEV, 0, -1):
        across = devices_y >> height
        group_y = index_y >> height
        box_id = index_x * across + group_y
        offset = devices_x * (devices_y - (devices_y >> height - 1))
        list_row = lax.dynamic_slice_in_dim(box_lists, offset + box_id, 1, 0)[0]
        chooser = (
            list_row[:, None] == jnp.arange(devices_x * across, dtype=jnp.int32)[None, :]
        ).astype(jnp.float32)
        sources = jnp.dot(chooser, multipoles[height - 1], precision=PRECISE)
        panel_now = jnp.einsum("kf,kfe->e", sources, m2l_ops[height - 1], precision=PRECISE)
        if panel_above is not None:
            side_bit = group_y % 2
            matrix = jnp.where(side_bit == 0, down_ops[height - 1, 0], down_ops[height - 1, 1])
            panel_now = panel_now + jnp.dot(panel_above, matrix, precision=PRECISE)
        panel_above = panel_now
    far_part = far_values(flat_coords, surfaces[0], panel_above).reshape(weights.shape)
    return jnp.where(occupied, near_part + far_part, 0.0)


def solution(mesh):
    return jax.shard_map(
        per_device,
        mesh=mesh,
        in_specs=(
            P(None, "gx", "gy", None),
            P("gx", "gy", None),
            P("gx", "gy", None),
            P(),
            P(),
            P(),
            P(),
        ),
        out_specs=P("gx", "gy", None),
        check_vma=False,
    )
```

profile of v0, /device:TPU:1, one launch (start us, length us, event | category | flops | bytes accessed | tf_op | source)
XLA Modules:
  0.0 515.1 jit_solution(16584847775598698696)
XLA Ops:
  0.0 0.8 broadcast_in_dim.23
  0.9 0.8 broadcast_select_fusion
  1.7 0.7 pad_maximum_fusion.30
  2.4 5.5 %collective-permute-start = (f32[4,1,2,512]{3,2,1,0:T(2,128)S(1)}, f32[4,1,2,512]{3,2,1,0:T(2,128)S(1)}, u32[]{:S(2)}, u32[]{:S(2)}) collective-permute-start(f32[4,1,2,512]{3,2,1,0:T(2,128)S(1)} %get-tuple-element.205), channel_id=1, source_target_pairs={{0,32},{32,64},{64,96},{96,128},{128,160},{160,192},{192,224},{1,3... | collective-permute-start | bytes 49160 | tf_op jit(solution)/shard_map/ppermute | solution.py:28
  7.9 1.3 collective-permute-start.1
  9.4 0.9 add_bitcast_fusion.2
  10.6 0.7 add_reduce_fusion.2
  11.3 0.7 add_reduce_fusion
  12.0 11.5 %fusion.172 = f32[1,296]{1,0:T(1,128)S(1)} fusion(f32[8192,1]{0,1:T(1,128)S(1)} %reshape.1001, f32[296]{0:T(512)S(1)} %get-tuple-element.213, f32[8192]{0:T(1024)S(1)} %add.1013, f32[296]{0:T(512)} %constant.132, f32[8192]{0:T(1024)S(1)} %add.1009, f32[8192]{0:T(1024)S(1)} %add.1006, f32[296]{0:T(512)S(1)} %get-tuple-element.214), kind=kOutput, calls=%fused_computation.313 | convolution fusion | flops 50921472 | bytes 135808 | tf_op jit(solution)/shard_map/dot_general | solution.py:134
  23.5 11.0 %fusion.186 = f32[1,296]{1,0:T(1,128)S(1)} fusion(f32[8192,1]{0,1:T(1,128)S(1)} %reshape.1001, f32[8192]{0:T(1024)S(1)} %add.1013, f32[296]{0:T(512)S(1)} %copy-done.5, f32[8192]{0:T(1024)S(1)} %add.1009, f32[296]{0:T(512)S(1)} %add_reduce_fusion.2, f32[8192]{0:T(1024)S(1)} %add.1006, f32[296]{0:T(512)S(1)} %get-tuple-element.214), kind=kOutput, calls=%fused_computation.327 | convolution fusion | flops 50921472 | bytes 135808 | tf_op jit(solution)/shard_map/dot_general | solution.py:134
  34.6 22.4 %fusion.179 = f32[1,296]{1,0:T(1,128)S(1)} fusion(f32[8192,1]{0,1:T(1,128)S(1)} %reshape.1001, f32[296]{0:T(512)S(1)} %add_reduce_fusion.1, f32[8192]{0:T(1024)S(1)} %add.1013, f32[296]{0:T(512)S(1)} %copy-done.5, f32[8192]{0:T(1024)S(1)} %add.1009, f32[8192]{0:T(1024)S(1)} %add.1006, f32[296]{0:T(512)S(1)} %get-tuple-element.214), kind=kOutput, calls=%fused_computation.320 | convolution fusion | flops 50921472 | bytes 135808 | tf_op jit(solution)/shard_map/dot_general | solution.py:134
  57.0 355.4 %all-gather.1 = f32[256,3,296]{2,1,0:T(4,128)S(1)} all-gather(f32[1,3,296]{2,1,0:T(4,128)S(1)} %maximum_bitcast_fusion), channel_id=2, replica_groups=mesh['gx'=8,'gy'=32] {'gx','gy'}, dimensions={0}, use_global_device_ids=true | all-gather | bytes 912864 | tf_op jit(solution)/shard_map/all_gather | solution.py:179
  412.4 2.5 slice_reduce_fusion
  416.7 3.9 fusion.238
  420.8 3.9 fusion.241
  424.7 1.5 convolution_reduce_fusion.1
  427.0 1.1 fusion.250
  428.3 4.1 fusion.235
  432.4 1.5 convolution_reduce_fusion
  434.0 8.2 %fusion.170 = f32[1,8192]{1,0:T(1,128)S(1)} fusion(f32[296,1]{0,1:T(1,128)S(1)} %reshape.1017, f32[296]{0:T(512)S(1)} %copy-done.4, f32[8192]{0:T(1024)S(1)} %bitcast.343, f32[296]{0:T(512)S(1)} %add_reduce_fusion.2, f32[8192]{0:T(1024)S(1)} %bitcast.341, f32[296]{0:T(512)S(1)} %get-tuple-element.214, f32[8192]{0:T(1024)S(1)} %bitcast.340), kind=kOutput, calls=%fused_computation.312 | convolution fusion | flops 50921472 | bytes 135808 | tf_op jit(solution)/shard_map/dot_general | solution.py:144
  442.5 1.9 collective-permute-start.2
  444.4 2.7 collective-permute-start.3
  447.1 3.1 collective-permute-done.3
  450.9 63.2 %while.12 = (s32[]{:T(128)}, f32[8,2,512]{2,1,0:T(2,128)S(1)}, s32[8]{0:T(128)S(1)}, f32[4,10,4,10,64]{4,3,2,1,0:T(8,128)S(1)}, s32[64]{0:T(128)S(1)}) while((s32[]{:T(128)}, f32[8,2,512]{2,1,0:T(2,128)S(1)}, s32[8]{0:T(128)S(1)}, f32[4,10,4,10,64]{4,3,2,1,0:T(8,128)S(1)}, s32[64]{0:T(128)S(1)}) %tuple.207), condition=%wide.region_2.3_spmd.clone.clone, body=%wide.region_0.2_spmd.clone.sunk.clone | while | flops 21730312 | bytes 4248003 | solution.py:111
  454.8 3.9 multiply_reduce_fusion.3
  462.7 3.9 multiply_reduce_fusion.3
  470.6 3.9 multiply_reduce_fusion.3
  478.5 3.9 multiply_reduce_fusion.3
  486.4 3.9 multiply_reduce_fusion.3
  494.3 3.9 multiply_reduce_fusion.3
  502.2 3.9 multiply_reduce_fusion.3
  510.1 3.9 multiply_reduce_fusion.3
  (232 shorter events, 19.4 us)
Async XLA Ops:
  2.4 439.9 %collective-permute-start = (f32[4,1,2,512]{3,2,1,0:T(2,128)S(1)}, f32[4,1,2,512]{3,2,1,0:T(2,128)S(1)}, u32[]{:S(2)}, u32[]{:S(2)}) collective-permute-start(f32[4,1,2,512]{3,2,1,0:T(2,128)S(1)} %get-tuple-element.205), channel_id=1, source_target_pairs={{0,32},{32,64},{64,96},{96,128},{128,160},{160,192},{192,224},{1,3... | collective-permute-start | bytes 49160 | tf_op jit(solution)/shard_map/ppermute | solution.py:28
  7.9 434.4 %collective-permute-start.1 = (f32[4,1,2,512]{3,2,1,0:T(2,128)S(1)}, f32[4,1,2,512]{3,2,1,0:T(2,128)S(1)}, u32[]{:S(2)}, u32[]{:S(2)}) collective-permute-start(f32[4,1,2,512]{3,2,1,0:T(2,128)S(1)} %get-tuple-element.206), channel_id=1, source_target_pairs={{32,0},{64,32},{96,64},{128,96},{160,128},{192,160},{224,192},{33,... | collective-permute-start | bytes 49160 | tf_op jit(solution)/shard_map/ppermute | solution.py:30
  12.0 11.5 %copy-start.5 = (f32[296]{0:T(512)S(1)}, f32[296]{0:T(512)}, u32[]{:S(2)}) copy-start(f32[296]{0:T(512)} %constant.132) | copy-start | bytes 3556
  23.5 11.0 %copy-start.3 = (f32[1,296]{1,0:T(1,128)S(1)}, f32[1,296]{1,0:T(1,128)}, u32[]{:S(2)}) copy-start(f32[1,296]{1,0:T(1,128)} %constant.133) | copy-start | bytes 3556
  34.5 380.9 %copy-start.1 = (f32[3,296,296]{2,1,0:T(8,128)S(1)}, f32[3,296,296]{2,1,0:T(8,128)}, u32[]{:S(2)}) copy-start(f32[3,296,296]{2,1,0:T(8,128)} %param.13) | copy-start | bytes 3154180
  34.5 381.7 %copy-start.2 = (s32[224,8]{0,1:T(8,128)S(1)}, s32[224,8]{0,1:T(8,128)}, u32[]{:S(2)}) copy-start(s32[224,8]{0,1:T(8,128)} %param.16) | copy-start | bytes 21508
  412.4 21.6 %copy-start.4 = (f32[296]{0:T(512)S(1)}, f32[296]{0:T(512)}, u32[]{:S(2)}) copy-start(f32[296]{0:T(512)} %constant.135) | copy-start | bytes 3556
  434.0 8.3 %copy-start = (f32[3,8,2,512]{3,2,1,0:T(2,128)S(1)}, f32[3,8,2,512]{3,2,1,0:T(2,128)}, u32[]{:S(2)}) copy-start(f32[3,8,2,512]{3,2,1,0:T(2,128)} %param.10) | copy-start | bytes 294916
  442.5 4.6 collective-permute-start.2
  444.4 5.8 %collective-permute-start.3 = (f32[4,10,1,512]{3,2,1,0:T(1,128)S(1)}, f32[4,10,1,512]{3,2,1,0:T(1,128)S(1)}, u32[]{:S(2)}, u32[]{:S(2)}) collective-permute-start(f32[4,10,1,512]{3,2,1,0:T(1,128)S(1)} %get-tuple-element.204), channel_id=1, source_target_pairs={{1,0},{2,1},{3,2},{4,3},{5,4},{6,5},{7,6},{8,7},{9,8},{10,9},{11,1... | collective-permute-start | bytes 245768 | tf_op jit(solution)/shard_map/ppermute | solution.py:30
where the time goes:
time: 525 us; the launch traced here: 515 us
  blocking collectives  355 us (68%)
  matrix products  70.6 us (13%)
  other arithmetic  43.1 us (8%)
  loops' own time  17.7 us (3%)
  local copies, waits for them, and re-layouts  12.9 us (2%)
  starting transfers between devices  11.3 us (2%)
    all_gather x1, blocking collectives, per_device(): lax.all_gather(own_checks[None], ('gx', 'gy'), axis=0, tiled=True)  355 us
    dot_general x3, matrix products, check_terms(): per_level.append(jnp.dot(strength, weights, precision=PRECISE))  44.9 us
    reduce_sum x8, other arithmetic, one_column(): jnp.sum(strength * sources[3][..., None, :], axis=-1)  31 us
    another operation x1, loops' own time, near_field(): return lax.map(one_column, jnp.arange(count_x))  17.7 us
    dot_general x3, matrix products, per_device(): jnp.einsum('kf,kfe->e', sources, m2l_ops[height - 1], precision=PRECISE)  11.9 us
  transfers between devices with their start and end apart: 4, of which 1 were waited for; matrix products, arithmetic and copies ran while one was open for 15% of the time, Pallas kernels for 0%

commit v1 on v0

v1 whole, which is shorter than its diff:
```python
import functools
import jax
import jax.numpy as jnp
import numpy as np
from jax import lax
from jax.experimental import pallas as pl
from jax.experimental.pallas import tpu as pltpu
from jax.sharding import PartitionSpec as P

CXL = 8
CYL = 2
LZ = 8
PPL = 64
P_ORD = 8
K = 8
LEV = 3
NE = 296
SLOTS = LZ * PPL
LANES = 128
ROWS = CXL * CYL * SLOTS // LANES
SOFTENING = 0.01
SURFACE_REACH = 1.05
PRECISE = lax.Precision.HIGHEST
LATTICE = np.linspace(-1.0, 1.0, P_ORD)
CHUNKS = ((0, 128), (128, 256), (256, NE))
INNER = range(1, P_ORD - 1)
ENDS = (0, P_ORD - 1)
A_TILES = [(a, b) for a in ENDS for b in range(P_ORD)]
B_TILES = [(a, b) for b in ENDS for a in INNER]
C_TILES = [(b, c) for c in ENDS for b in INNER]


def first_row(a, b):
    if a == 0:
        return 8 * b
    if a == P_ORD - 1:
        return 232 + 8 * b
    return 64 + 28 * (a - 1) + (0 if b == 0 else 20)


def strided_rows(b, c):
    return pl.ds(64 + 8 + 2 * (b - 1) + (1 if c else 0), P_ORD - 2, stride=28)


def wide(row):
    return jnp.broadcast_to(row, (8, LANES))


def lattice_x(a):
    return float(0.5 * CXL + SURFACE_REACH * 0.5 * CXL * LATTICE[a])


def lattice_z(c):
    return float(0.5 * LZ + SURFACE_REACH * 0.5 * LZ * LATTICE[c])


def along_sublanes(half):
    steps = lax.broadcasted_iota(jnp.int32, (8, LANES), 0).astype(jnp.float32)
    return half - SURFACE_REACH * half + steps * (SURFACE_REACH * half * 2.0 / (P_ORD - 1))


def square(value):
    return value * value


def a_squares(x8, z8, y_parts):
    along_z = square(along_sublanes(0.5 * LZ) - z8) + SOFTENING
    for a in ENDS:
        base = square(lattice_x(a) - x8) + along_z
        for b in range(P_ORD):
            yield base + y_parts[b]


def bc_squares(x8, z8, y_parts):
    along_z = square(along_sublanes(0.5 * LZ) - z8) + SOFTENING
    bases = [square(lattice_x(a) - x8) + along_z for a in INNER]
    for b in ENDS:
        for base in bases:
            yield base + y_parts[b]
    along_x = square(along_sublanes(0.5 * CXL) - x8) + SOFTENING
    for c in ENDS:
        base = along_x + square(lattice_z(c) - z8)
        for b in INNER:
            yield base + y_parts[b]


def row_of(p_ref, r):
    return [wide(p_ref[c, pl.ds(r, 1), :]) for c in range(4)]


def send_kernel(
    span_x, span_y, meta_ref, sy_ref, p_ref, up_hbm, m2l_hbm, down_hbm, out_ref,
    up_ref, m2l_ref, down_ref, check_ref, row_ref, column_ref, panel_ref, sems,
):
    copies = [pltpu.make_async_copy(up_hbm, up_ref, sems.at[0])]
    copies += [
        pltpu.make_async_copy(m2l_hbm.at[h], m2l_ref.at[h], sems.at[1 + h]) for h in range(LEV)
    ]
    copies.append(pltpu.make_async_copy(down_hbm, down_ref, sems.at[1 + LEV]))
    for copy in copies:
        copy.start()
    row_ref[...] = jnp.zeros((8, 384), jnp.float32)

    for h in range(LEV):
        ys = [sy_ref[8 * h + b] for b in range(P_ORD)]
        for squares, tiles in ((a_squares, A_TILES), (bc_squares, B_TILES + C_TILES)):

            def gather(r, sums):
                x8, y8, z8, w8 = row_of(p_ref, r)
                y_parts = [square(ys[b] - y8) for b in range(P_ORD)]
                return [
                    total + w8 * lax.rsqrt(d2)
                    for total, d2 in zip(sums, squares(x8, z8, y_parts))
                ]

            sums = lax.fori_loop(
                0, ROWS, gather, [jnp.zeros((8, LANES), jnp.float32) for _ in tiles], unroll=2
            )
            for n, (total, tile) in enumerate(zip(sums, tiles)):
                filled = jnp.broadcast_to(jnp.sum(total, axis=1, keepdims=True), (8, LANES))
                if squares is bc_squares and n >= len(B_TILES):
                    check_ref[h, strided_rows(*tile), :] = filled[1:7]
                else:
                    check_ref[h, pl.ds(first_row(*tile), 8), :] = filled

    copies[0].wait()
    for h in range(LEV):
        for low, high in CHUNKS:
            total = jnp.zeros((8, high - low), jnp.float32)
            for i in range(0, NE, 8):
                total += check_ref[h, i : i + 8, : high - low] * up_ref[h, i : i + 8, low:high]
            row_ref[h : h + 1, low:high] = jnp.sum(total, axis=0, keepdims=True)
    flipped = jnp.transpose(row_ref[...])
    for h in range(LEV):
        column_ref[h] = jnp.broadcast_to(flipped[:NE, h : h + 1], (NE, LANES))

    for h in range(LEV):
        copies[1 + h].wait()

        def translate(k, carry):
            for low, high in CHUNKS:
                total = jnp.zeros((8, high - low), jnp.float32)
                for i in range(0, NE, 8):
                    total += (
                        column_ref[h, i : i + 8, : high - low]
                        * m2l_ref[h, k, i : i + 8, low:high]
                    )
                panel_ref[h, k, :, low:high] = total
            return carry

        lax.fori_loop(0, K, translate, 0)

    copies[1 + LEV].wait()
    panels = [jnp.sum(panel_ref[h], axis=1) for h in range(LEV)]
    top = panels[2]
    middle = jnp.concatenate(
        [panels[1]]
        + [
            jnp.dot(top, down_ref[1, side], precision=PRECISE, preferred_element_type=jnp.float32)
            for side in range(2)
        ],
        axis=0,
    )
    lower = [
        jnp.dot(middle, down_ref[0, side], precision=PRECISE, preferred_element_type=jnp.float32)
        for side in range(2)
    ]
    out_ref[...] = jnp.zeros(out_ref.shape, jnp.float32)
    sub = lax.broadcasted_iota(jnp.int32, (8, NE), 0)
    index_x = meta_ref[0]
    index_y = meta_ref[1]

    def spread(row):
        return jnp.broadcast_to(row, (8, NE))

    for h in range(1, LEV + 1):
        across = span_y >> h
        bits = across.bit_length() - 1
        own_box = (index_x << bits) + (index_y >> h)
        for k in range(K):
            box = (own_box - meta_ref[2 + (h - 1) * K + k]) & (span_x * across - 1)
            place_y = (box & (across - 1)) << h
            tile = (box >> bits) * (span_y // 8) + (place_y >> 3)
            inside = place_y & 7
            if h == 1:
                value = spread(panels[0][k : k + 1])
            else:
                first = 0 if h == 2 else 8
                value = jnp.where(
                    (sub // 2) % 2 == 0,
                    spread(lower[0][first + k : first + k + 1]),
                    spread(lower[1][first + k : first + k + 1]),
                )
                if h == 3:
                    upper = jnp.where(
                        (sub // 2) % 2 == 0,
                        spread(lower[0][16 + k : 17 + k]),
                        spread(lower[1][16 + k : 17 + k]),
                    )
                    value = jnp.where(sub < 4, value, upper)
            if h < 3:
                value = jnp.where((sub >= inside) & (sub < inside + 2**h), value, 0.0)
            out_ref[tile] = out_ref[tile] + value


def send_panels(meta, sy, points, up_ops, m2l_ops, down_ops, span_x, span_y):
    return pl.pallas_call(
        functools.partial(send_kernel, span_x, span_y),
        out_shape=jax.ShapeDtypeStruct((span_x * span_y // 8, 8, NE), jnp.float32),
        in_specs=[
            pl.BlockSpec(memory_space=pltpu.SMEM),
            pl.BlockSpec(memory_space=pltpu.SMEM),
            pl.BlockSpec(memory_space=pltpu.VMEM),
            pl.BlockSpec(memory_space=pl.ANY),
            pl.BlockSpec(memory_space=pl.ANY),
            pl.BlockSpec(memory_space=pl.ANY),
        ],
        out_specs=pl.BlockSpec(memory_space=pltpu.VMEM),
        scratch_shapes=[
            pltpu.VMEM((LEV, NE, NE), jnp.float32),
            pltpu.VMEM((LEV, K, NE, NE), jnp.float32),
            pltpu.VMEM((LEV - 1, 2, NE, NE), jnp.float32),
            pltpu.VMEM((LEV, NE, LANES), jnp.float32),
            pltpu.VMEM((8, 384), jnp.float32),
            pltpu.VMEM((LEV, NE, LANES), jnp.float32),
            pltpu.VMEM((LEV, K, 8, NE), jnp.float32),
            pltpu.SemaphoreType.DMA((LEV + 2,)),
        ],
        compiler_params=pltpu.CompilerParams(vmem_limit_bytes=40 * 2**20),
        name="send_panels",
    )(meta, sy, points, up_ops, m2l_ops, down_ops)


def far_kernel(
    sy_ref, p_ref, held_ref, low_ref, high_ref, parts_ref, out_ref, row_ref, column_ref, tile_ref,
    near_ref,
):
    row_ref[...] = jnp.zeros((8, 384), jnp.float32)
    near_ref[: ROWS // 2, :] = low_ref[...]
    near_ref[ROWS // 2 :, :] = high_ref[...]
    row_ref[0:1, :NE] = jnp.sum(parts_ref[...], axis=0, keepdims=True)
    flipped = jnp.transpose(row_ref[...])
    column_ref[...] = jnp.broadcast_to(flipped[:NE, 0:1], (NE, LANES))
    for n, tile in enumerate(A_TILES + B_TILES):
        tile_ref[n] = column_ref[pl.ds(first_row(*tile), 8), :]
    for n, tile in enumerate(C_TILES):
        n += len(A_TILES + B_TILES)
        tile_ref[n] = jnp.zeros((8, LANES), jnp.float32)
        tile_ref[n, 1:7, :] = column_ref[strided_rows(*tile), :]
    ys = [sy_ref[b] for b in range(P_ORD)]

    def spread(r, carry):
        x8, y8, z8, w8 = row_of(p_ref, r)
        y_parts = [square(ys[b] - y8) for b in range(P_ORD)]
        totals = [jnp.zeros((8, LANES), jnp.float32) for _ in range(4)]
        n = 0
        for squares in (a_squares, bc_squares):
            for d2 in squares(x8, z8, y_parts):
                totals[n % 4] += tile_ref[n] * lax.rsqrt(d2)
                n += 1
        far = jnp.sum(totals[0] + totals[1] + (totals[2] + totals[3]), axis=0, keepdims=True)
        here = pl.ds(r, 1)
        value = near_ref[here, :] + far
        out_ref[here, :] = jnp.where(held_ref[here, :] > 0, value, 0.0)
        return carry

    lax.fori_loop(0, ROWS, spread, 0, unroll=2)


def far_and_sum(sy, points, held, low, high, parts):
    return pl.pallas_call(
        far_kernel,
        out_shape=jax.ShapeDtypeStruct((ROWS, LANES), jnp.float32),
        in_specs=[pl.BlockSpec(memory_space=pltpu.SMEM)]
        + [pl.BlockSpec(memory_space=pltpu.VMEM)] * 5,
        out_specs=pl.BlockSpec(memory_space=pltpu.VMEM),
        scratch_shapes=[
            pltpu.VMEM((8, 384), jnp.float32),
            pltpu.VMEM((NE, LANES), jnp.float32),
            pltpu.VMEM((40, 8, LANES), jnp.float32),
            pltpu.VMEM((ROWS, LANES), jnp.float32),
        ],
        compiler_params=pltpu.CompilerParams(vmem_limit_bytes=16 * 2**20),
        name="far_and_sum",
    )(sy, points, held, low, high, parts)


PAD_Z = LZ + 2
STEP = 4


def near_kernel(first_x, count_x, fill_ref, source_ref, column_ref, out_ref, sum_ref):
    lanes = lax.broadcasted_iota(jnp.int32, (8, LANES), 1)
    lower_half = lanes < PPL
    ones = jnp.ones((8, LANES), jnp.bfloat16)
    own = lax.rsqrt(jnp.full((1, LANES), SOFTENING, jnp.float32))

    def one_leaf_pair(leaf, carry):
        x = leaf // LZ
        z = leaf % LZ
        held = jnp.maximum(
            fill_ref[(first_x + x) * 2 * LZ + z], fill_ref[((first_x + x) * 2 + 1) * LZ + z]
        )

        def add_tiles(step, inner):
            targets = []
            for u in range(STEP):
                start = pl.multiple_of(8 * (STEP * step + u), 8)
                block = column_ref[first_x + x, pl.ds(start, 8), :]

                def pick(c, y):
                    lane = jnp.full((8, LANES), (c * 2 + y) * LZ, jnp.int32) + z
                    return jnp.take_along_axis(block, lane, axis=1)

                low = [pick(c, 0) for c in range(3)]
                high = [pick(c, 1) for c in range(3)]
                mixed = [jnp.where(lower_half, l, h) for l, h in zip(low, high)]
                targets.append((low, high, mixed))
            sums = [[None] * 3 for _ in range(STEP)]
            for shift_x in range(3):
                for shift_z in range(3):
                    row = (first_x + x + shift_x) * PAD_Z + z + shift_z
                    for side in range(2):
                        source = [
                            wide(source_ref[4 * side + c, pl.ds(row, 1), :]) for c in range(4)
                        ]
                        for u in range(STEP):
                            for n in (0, 1) if side == 0 else (2,):
                                tx, ty, tz = targets[u][n]
                                d2 = square(tx - source[0]) + SOFTENING
                                d2 += square(ty - source[1])
                                d2 += square(tz - source[2])
                                value = source[3] * lax.rsqrt(d2)
                                old = sums[u][n]
                                sums[u][n] = value if old is None else old + value
            for u in range(STEP):
                low, high, mixed = sums[u]
                start = pl.multiple_of(8 * (STEP * step + u), 8)
                sum_ref[leaf, pl.ds(start, 8), :] = low + jnp.where(lower_half, mixed, 0.0)
                sum_ref[leaf, pl.ds(PPL + start, 8), :] = high + jnp.where(lower_half, 0.0, mixed)
            return inner

        lax.fori_loop(0, (held + 8 * STEP - 1) // (8 * STEP), add_tiles, 0)
        return carry

    lax.fori_loop(0, count_x * LZ, one_leaf_pair, 0)

    def finish(group, carry):
        rows = []
        for n in range(8):
            rest = sum_ref[8 * group + n]
            total = None
            for _ in range(3):
                part = rest.astype(jnp.bfloat16)
                rest = rest - part.astype(jnp.float32)
                term = lax.dot_general(
                    ones, part, (((1,), (1,)), ((), ())), preferred_element_type=jnp.float32
                )
                total = term if total is None else total + term
            own_row = (first_x + group + 1) * PAD_Z + n + 1
            rows.append(total[0:1] - source_ref[3, pl.ds(own_row, 1), :] * own)
        out_ref[pl.ds(pl.multiple_of(8 * group, 8), 8), :] = jnp.concatenate(rows, axis=0)
        return carry

    lax.fori_loop(0, count_x, finish, 0)


def near_sums(first_x, count_x, fill, sources, columns):
    return pl.pallas_call(
        functools.partial(near_kernel, first_x, count_x),
        out_shape=jax.ShapeDtypeStruct((count_x * LZ, LANES), jnp.float32),
        in_specs=[pl.BlockSpec(memory_space=pltpu.SMEM)]
        + [pl.BlockSpec(memory_space=pltpu.VMEM)] * 2,
        out_specs=pl.BlockSpec(memory_space=pltpu.VMEM),
        scratch_shapes=[pltpu.VMEM((count_x * LZ, LANES, LANES), jnp.float32)],
        compiler_params=pltpu.CompilerParams(vmem_limit_bytes=24 * 2**20),
        name="near_sums",
    )(fill, sources, columns)


def extended(cells, sides, width):
    for axis, dim in sides:
        count = lax.axis_size(axis)
        ends = count - 1
        head = lax.slice_in_dim(cells, 0, width, axis=dim)
        tail = lax.slice_in_dim(cells, cells.shape[dim] - width, cells.shape[dim], axis=dim)
        cells = jnp.concatenate(
            [
                lax.ppermute(tail, axis, [(i, (i + 1) % count) for i in range(ends)]),
                cells,
                lax.ppermute(head, axis, [((i + 1) % count, i) for i in range(ends)]),
            ],
            axis=dim,
        )
    return cells


def live_charges(charges, counts):
    size_x, size_y = (counts.shape[0], counts.shape[1])
    filled = jnp.broadcast_to(counts[..., None], (size_x, size_y, LZ, PPL)).reshape(
        size_x, size_y, SLOTS
    )
    within = jnp.arange(SLOTS, dtype=jnp.int32) % PPL
    occupied = within[None, None, :] < filled
    return (jnp.where(occupied, charges, 0.0), occupied)


def placed(rows, start_x, start_y):
    size_x, size_y = rows.shape[1:3]
    along_x = (start_x + jnp.arange(size_x)).astype(jnp.float32)
    along_y = (start_y + jnp.arange(size_y)).astype(jnp.float32)
    along_z = (jnp.arange(SLOTS) // PPL).astype(jnp.float32)
    return jnp.stack(
        [
            rows[0] + along_x[:, None, None],
            rows[1] + along_y[None, :, None],
            rows[2] + along_z[None, None, :],
            rows[3],
        ]
    )


def leaf_pairs(cells):
    lead, size_x = cells.shape[:2]
    split = cells.reshape(lead, size_x, 2, LZ, PPL).transpose(0, 1, 3, 2, 4)
    return split.reshape(lead, size_x, LZ, LANES)


def per_device(positions, charges, counts, up_ops, m2l_ops, down_ops, box_lists):
    index_x = lax.axis_index("gx")
    index_y = lax.axis_index("gy")
    devices_x = lax.axis_size("gx")
    devices_y = lax.axis_size("gy")
    weights, occupied = live_charges(charges, counts)
    local_rows = jnp.concatenate([positions, weights[None]], axis=0)
    padded = extended(local_rows, (("gx", 1), ("gy", 2)), 1)

    own = placed(local_rows, 0, 0)
    points = leaf_pairs(own).reshape(4, ROWS, LANES)
    held = leaf_pairs(occupied.astype(jnp.float32)[None]).reshape(ROWS, LANES)
    offsets = [devices_x * (devices_y - (devices_y >> h - 1)) for h in range(1, LEV + 1)]
    meta = jnp.concatenate([jnp.stack([index_x, index_y])] + [box_lists[o] for o in offsets])
    lattice = jnp.asarray(LATTICE, dtype=jnp.float32)
    sy = jnp.concatenate(
        [
            ((index_y >> h) * CYL * 2**h - index_y * CYL).astype(jnp.float32)
            + (0.5 * CYL * 2**h) * (1.0 + SURFACE_REACH * lattice)
            for h in range(1, LEV + 1)
        ]
    )
    sent = send_panels(meta, sy, points, up_ops, m2l_ops, down_ops, devices_x, devices_y)
    along_x = lax.all_to_all(
        sent.reshape(devices_x, devices_y, NE), "gx", split_axis=0, concat_axis=0, tiled=True
    )
    middle = jnp.sum(along_x, axis=0).reshape(devices_y, 1, NE)
    parts = lax.all_to_all(middle, "gy", split_axis=0, concat_axis=0, tiled=True)

    around = placed(padded, -1, -1)
    sources = jnp.concatenate(
        [leaf_pairs(around[:, :, 1:3]), leaf_pairs(jnp.stack([around[:, :, 0], around[:, :, 3]], 2))]
    )
    sources = jnp.pad(sources, ((0, 0), (0, 0), (1, 1), (0, 0)))
    sources = sources.reshape(8, (CXL + 2) * PAD_Z, LANES)
    columns = own[:3].reshape(3, CXL, CYL, LZ, PPL).transpose(1, 4, 0, 2, 3)
    columns = columns.reshape(CXL, PPL, 3 * CYL * LZ)
    columns = jnp.pad(columns, ((0, 0), (0, 0), (0, LANES - columns.shape[2])))
    fill = counts.reshape(-1)
    half = CXL // 2
    near = [near_sums(0, half, fill, sources, columns)]
    near.append(near_sums(half, half, fill, sources, columns))
    total = far_and_sum(sy, points, held, near[0], near[1], parts.reshape(devices_y, NE))
    total = total.reshape(CXL, LZ, CYL, PPL).transpose(0, 2, 1, 3)
    return total.reshape(CXL, CYL, SLOTS)


def solution(mesh):
    return jax.shard_map(
        per_device,
        mesh=mesh,
        in_specs=(
            P(None, "gx", "gy", None),
            P("gx", "gy", None),
            P("gx", "gy", None),
            P(),
            P(),
            P(),
            P(),
        ),
        out_specs=P("gx", "gy", None),
        check_vma=False,
    )
```

time: 525 us -> 103 us (0.20)
  the two profiles are of different devices: /device:TPU:1 before, /device:TPU:11 now
where the time goes in v1:
time: 103 us; the launch traced here: 102 us
  Pallas kernels  55.8 us (54%)
  starting transfers between devices  30.6 us (30%)
  local copies, waits for them, and re-layouts  7.04 us (7%)
  waiting for transfers between devices  4.72 us (5%)
  other arithmetic  3.56 us (3%)
    pallas_call x2, Pallas kernels, near_sums(): pl.pallas_call(functools.partial(near_kernel, first_x, count_x), out_shap...  39.4 us
    pallas_call x1, Pallas kernels, send_panels(): pl.pallas_call(functools.partial(send_kernel, span_x, span_y), out_shape=...  13.1 us
    ppermute x2, starting transfers between devices, extended(): lax.ppermute(tail, axis, [(i, (i + 1) % count) for i in range(ends)])  9.85 us
    all_to_all x1, starting transfers between devices, per_device(): lax.all_to_all(middle, 'gy', split_axis=0, concat_axis=0, tiled=True)  9.69 us
    ppermute x2, starting transfers between devices, extended(): lax.ppermute(head, axis, [((i + 1) % count, i) for i in range(ends)])  5.85 us
    all_to_all x1, starting transfers between devices, per_device(): lax.all_to_all(sent.reshape(devices_x, devices_y, NE), 'gx', split_axis=0...  5.16 us
    ppermute x2, waiting for transfers between devices, extended(): lax.ppermute(head, axis, [((i + 1) % count, i) for i in range(ends)])  4.71 us
    pallas_call x1, Pallas kernels, far_and_sum(): pl.pallas_call(far_kernel, out_shape=jax.ShapeDtypeStruct((ROWS, LANES),...  3.25 us
  transfers between devices with their start and end apart: 6, of which 1 were waited for; matrix products, arithmetic and copies ran while one was open for 5% of the time, Pallas kernels for 51%

profile of v1, /device:TPU:11, one launch (start us, length us, event | category | flops | bytes accessed | tf_op | source)
XLA Modules:
  0.0 102.1 jit_solution(10631259305865772320)
XLA Ops:
  0.0 0.9 broadcast_in_dim.10
  1.0 0.8 compare_select_fusion
  1.8 0.7 pad_maximum_fusion.5
  2.6 3.8 %collective-permute-start = (f32[4,1,2,512]{3,2,1,0:T(2,128)S(1)}, f32[4,1,2,512]{3,2,1,0:T(2,128)S(1)}, u32[]{:S(2)}, u32[]{:S(2)}) collective-permute-start(f32[4,1,2,512]{3,2,1,0:T(2,128)S(1)} %get-tuple-element.14), channel_id=1, source_target_pairs={{0,32},{32,64},{64,96},{96,128},{128,160},{160,192},{192,224},{1,3... | collective-permute-start | bytes 49160 | tf_op jit(solution)/shard_map/ppermute | solution.py:389
  6.3 3.9 %collective-permute-start.1 = (f32[4,1,2,512]{3,2,1,0:T(2,128)S(1)}, f32[4,1,2,512]{3,2,1,0:T(2,128)S(1)}, u32[]{:S(2)}, u32[]{:S(2)}) collective-permute-start(f32[4,1,2,512]{3,2,1,0:T(2,128)S(1)} %get-tuple-element.15), channel_id=1, source_target_pairs={{32,0},{64,32},{96,64},{128,96},{160,128},{192,160},{224,192},{33,... | collective-permute-start | bytes 49160 | tf_op jit(solution)/shard_map/ppermute | solution.py:391
  10.4 0.9 slice_add_fusion.5
  11.8 0.1 maximum_bitcast_fusion
  11.9 0.2 reshape_reshape.8.p_ref
  12.1 0.2 slice_reduce_fusion
  12.5 1.3 %copy-done.1 = f32[3,296,296]{2,1,0:T(8,128)S(1)} copy-done((f32[3,296,296]{2,1,0:T(8,128)S(1)}, f32[3,296,296]{2,1,0:T(8,128)}, u32[]{:S(2)}) %copy-start.1) | copy-done | bytes 1051416
  13.9 13.1 %send_panels.1 = f32[32,8,296]{2,1,0:T(8,128)} custom-call(s32[26]{0:T(128)S(1)} %concatenate.25.meta_ref, f32[24]{0:T(128)S(1)} %pad_maximum_fusion.6.sy_ref, f32[4,64,128]{2,1,0:T(8,128)S(1)} %reshape_reshape.8.p_ref, f32[3,296,296]{2,1,0:T(8,128)S(1)} %copy-done.1, f32[3,8,296,296]{3,2,1,0:T(8,128)} %m2l_hbm.1, f32[2,2,296,296]{3,2,1,0:T(8,128)S(1)} %copy-done), custom_call_target="tpu_custom_call" | custom-call | tf_op jit(solution)/shard_map/send_panels/pallas_call | solution.py:207
  27.0 5.2 %all-to-all-start = ((f32[8,32,296]{2,1,0:T(8,128)}), f32[8,32,296]{2,1,0:T(8,128)S(1)}, u32[]{:S(2)}, u32[]{:S(2)}) async-start(f32[8,32,296]{2,1,0:T(8,128)} %bitcast.10), calls=%async_computation | async-start | bytes 786432 | tf_op jit(solution)/shard_map/all_to_all | solution.py:452
  32.3 0.1 fusion.2
  32.6 0.2 reshape.107
  33.1 0.1 fusion.14
  33.3 6.1 %collective-permute-start.2 = (f32[4,10,1,512]{3,2,1,0:T(1,128)S(1)}, f32[4,10,1,512]{3,2,1,0:T(1,128)S(1)}, u32[]{:S(2)}, u32[]{:S(2)}) collective-permute-start(f32[4,10,1,512]{3,2,1,0:T(1,128)S(1)} %get-tuple-element.12), channel_id=1, source_target_pairs={{0,1},{1,2},{2,3},{3,4},{4,5},{5,6},{6,7},{7,8},{8,9},{9,10},{10,1... | collective-permute-start | bytes 245768 | tf_op jit(solution)/shard_map/ppermute | solution.py:389
  39.4 1.9 %collective-permute-start.3 = (f32[4,10,1,512]{3,2,1,0:T(1,128)S(1)}, f32[4,10,1,512]{3,2,1,0:T(1,128)S(1)}, u32[]{:S(2)}, u32[]{:S(2)}) collective-permute-start(f32[4,10,1,512]{3,2,1,0:T(1,128)S(1)} %get-tuple-element.13), channel_id=1, source_target_pairs={{1,0},{2,1},{3,2},{4,3},{5,4},{6,5},{7,6},{8,7},{9,8},{10,9},{11,1... | collective-permute-start | bytes 245768 | tf_op jit(solution)/shard_map/ppermute | solution.py:391
  41.3 4.7 %collective-permute-done.3 = f32[4,10,1,512]{3,2,1,0:T(1,128)S(1)} collective-permute-done((f32[4,10,1,512]{3,2,1,0:T(1,128)S(1)}, f32[4,10,1,512]{3,2,1,0:T(1,128)S(1)}, u32[]{:S(2)}, u32[]{:S(2)}) %collective-permute-start.3) | collective-permute-done | bytes 81952 | tf_op jit(solution)/shard_map/ppermute | solution.py:391
  46.0 0.2 pad_maximum_fusion
  46.6 0.2 reshape.102
  46.8 0.2 copy.47
  46.9 0.2 reshape.103
  47.2 0.1 fusion.1
  47.3 0.2 reshape.104
  47.6 0.2 copy.46
  47.7 0.2 reshape.105
  48.0 0.7 reshape.110
  48.7 9.7 %all-to-all-start.1 = ((f32[32,1,296]{2,1,0:T(1,128)}), f32[32,1,296]{2,1,0:T(1,128)S(1)}, u32[]{:S(2)}, u32[]{:S(2)}) async-start(f32[32,1,296]{2,1,0:T(1,128)} %reshape.110), calls=%async_computation.1 | async-start | bytes 98304 | tf_op jit(solution)/shard_map/all_to_all | solution.py:456
  58.6 19.7 %near_sums.3.high_ref = f32[32,128]{1,0:T(8,128)S(1)} custom-call(s32[128]{0:T(128)S(1)} %reshape.101.fill_ref, f32[8,100,128]{2,1,0:T(8,128)S(1)} %copy.39.source_ref, f32[8,64,128]{2,1,0:T(8,128)S(1)} %pad.9.column_ref), custom_call_target="tpu_custom_call" | custom-call | tf_op jit(solution)/shard_map/near_sums/pallas_call | solution.py:369
  78.3 19.7 %near_sums.2.low_ref = f32[32,128]{1,0:T(8,128)S(1)} custom-call(s32[128]{0:T(128)S(1)} %reshape.101.fill_ref, f32[8,100,128]{2,1,0:T(8,128)S(1)} %copy.39.source_ref, f32[8,64,128]{2,1,0:T(8,128)S(1)} %pad.9.column_ref), custom_call_target="tpu_custom_call" | custom-call | tf_op jit(solution)/shard_map/near_sums/pallas_call | solution.py:369
  98.0 3.2 %far_and_sum.1 = f32[64,128]{1,0:T(8,128)S(1)} custom-call(f32[24]{0:T(128)S(1)} %pad_maximum_fusion.6.sy_ref, f32[4,64,128]{2,1,0:T(8,128)S(1)} %reshape_reshape.8.p_ref, f32[64,128]{1,0:T(8,128)S(1)} %reshape.114.held_ref, f32[32,128]{1,0:T(8,128)S(1)} %near_sums.2.low_ref, f32[32,128]{1,0:T(8,128)S(1)} %near_sums.3.high_ref, f32[32,296]{1,0:T(8,128)S(1)} %bitcast.32), custom_call_target="tpu_custom_call" | custom-call | tf_op jit(solution)/shard_map/far_and_sum/pallas_call | solution.py:271
  101.4 0.7 reshape.113
  (57 shorter events, 2.0 us)
Async XLA Ops:
  0.0 12.3 %copy-start.7 = (f32[8]{0:T(128)S(1)}, f32[8]{0:T(128)}, u32[]{:S(2)}) copy-start(f32[8]{0:T(128)} %constant.84) | copy-start | bytes 100
  0.0 12.3 %copy-start.5 = (f32[8]{0:T(128)S(1)}, f32[8]{0:T(128)}, u32[]{:S(2)}) copy-start(f32[8]{0:T(128)} %constant.85) | copy-start | bytes 100
  0.0 12.3 %copy-start.6 = (f32[8]{0:T(128)S(1)}, f32[8]{0:T(128)}, u32[]{:S(2)}) copy-start(f32[8]{0:T(128)} %constant.86) | copy-start | bytes 100
  0.0 12.1 %copy-start.4 = (s32[224,8]{0,1:T(8,128)S(1)}, s32[224,8]{0,1:T(8,128)}, u32[]{:S(2)}) copy-start(s32[224,8]{0,1:T(8,128)} %param.14) | copy-start | bytes 21508
  0.0 12.5 %copy-start = (f32[2,2,296,296]{3,2,1,0:T(8,128)S(1)}, f32[2,2,296,296]{3,2,1,0:T(8,128)}, u32[]{:S(2)}) copy-start(f32[2,2,296,296]{3,2,1,0:T(8,128)} %down_hbm.1) | copy-start | bytes 4205572
  2.6 30.4 %collective-permute-start = (f32[4,1,2,512]{3,2,1,0:T(2,128)S(1)}, f32[4,1,2,512]{3,2,1,0:T(2,128)S(1)}, u32[]{:S(2)}, u32[]{:S(2)}) collective-permute-start(f32[4,1,2,512]{3,2,1,0:T(2,128)S(1)} %get-tuple-element.14), channel_id=1, source_target_pairs={{0,32},{32,64},{64,96},{96,128},{128,160},{160,192},{192,224},{1,3... | collective-permute-start | bytes 49160 | tf_op jit(solution)/shard_map/ppermute | solution.py:389
  6.3 26.7 %collective-permute-start.1 = (f32[4,1,2,512]{3,2,1,0:T(2,128)S(1)}, f32[4,1,2,512]{3,2,1,0:T(2,128)S(1)}, u32[]{:S(2)}, u32[]{:S(2)}) collective-permute-start(f32[4,1,2,512]{3,2,1,0:T(2,128)S(1)} %get-tuple-element.15), channel_id=1, source_target_pairs={{32,0},{64,32},{96,64},{128,96},{160,128},{192,160},{224,192},{33,... | collective-permute-start | bytes 49160 | tf_op jit(solution)/shard_map/ppermute | solution.py:391
  12.5 1.3 %copy-start.1 = (f32[3,296,296]{2,1,0:T(8,128)S(1)}, f32[3,296,296]{2,1,0:T(8,128)}, u32[]{:S(2)}) copy-start(f32[3,296,296]{2,1,0:T(8,128)} %up_hbm.1) | copy-start | bytes 3154180
  13.9 18.3 %copy-start.3 = (s32[8,2,8]{2,1,0:T(2,128)S(1)}, s32[8,2,8]{2,1,0:T(2,128)}, u32[]{:S(2)}) copy-start(s32[8,2,8]{2,1,0:T(2,128)} %param.10) | copy-start | bytes 1540
  27.0 6.1 %copy-start.2 = (f32[3,8,2,512]{3,2,1,0:T(2,128)S(1)}, f32[3,8,2,512]{3,2,1,0:T(2,128)}, u32[]{:S(2)}) copy-start(f32[3,8,2,512]{3,2,1,0:T(2,128)} %param.8) | copy-start | bytes 294916
  27.0 21.0 %all-to-all-start = ((f32[8,32,296]{2,1,0:T(8,128)}), f32[8,32,296]{2,1,0:T(8,128)S(1)}, u32[]{:S(2)}, u32[]{:S(2)}) async-start(f32[8,32,296]{2,1,0:T(8,128)} %bitcast.10), calls=%async_computation | async-start | bytes 786432 | tf_op jit(solution)/shard_map/all_to_all | solution.py:452
  33.3 8.1 %collective-permute-start.2 = (f32[4,10,1,512]{3,2,1,0:T(1,128)S(1)}, f32[4,10,1,512]{3,2,1,0:T(1,128)S(1)}, u32[]{:S(2)}, u32[]{:S(2)}) collective-permute-start(f32[4,10,1,512]{3,2,1,0:T(1,128)S(1)} %get-tuple-element.12), channel_id=1, source_target_pairs={{0,1},{1,2},{2,3},{3,4},{4,5},{5,6},{6,7},{7,8},{8,9},{9,10},{10,1... | collective-permute-start | bytes 245768 | tf_op jit(solution)/shard_map/ppermute | solution.py:389
  39.4 6.7 %collective-permute-start.3 = (f32[4,10,1,512]{3,2,1,0:T(1,128)S(1)}, f32[4,10,1,512]{3,2,1,0:T(1,128)S(1)}, u32[]{:S(2)}, u32[]{:S(2)}) collective-permute-start(f32[4,10,1,512]{3,2,1,0:T(1,128)S(1)} %get-tuple-element.13), channel_id=1, source_target_pairs={{1,0},{2,1},{3,2},{4,3},{5,4},{6,5},{7,6},{8,7},{9,8},{10,9},{11,1... | collective-permute-start | bytes 245768 | tf_op jit(solution)/shard_map/ppermute | solution.py:391
  48.7 49.3 %all-to-all-start.1 = ((f32[32,1,296]{2,1,0:T(1,128)}), f32[32,1,296]{2,1,0:T(1,128)S(1)}, u32[]{:S(2)}, u32[]{:S(2)}) async-start(f32[32,1,296]{2,1,0:T(1,128)} %reshape.110), calls=%async_computation.1 | async-start | bytes 98304 | tf_op jit(solution)/shard_map/all_to_all | solution.py:456

commit v2 on v1

--- a/solution.py
+++ b/solution.py
@@ -166,54 +166,35 @@
         for side in range(2)
     ]
     out_ref[...] = jnp.zeros(out_ref.shape, jnp.float32)
-    sub = lax.broadcasted_iota(jnp.int32, (8, NE), 0)
     index_x = meta_ref[0]
     index_y = meta_ref[1]
-
-    def spread(row):
-        return jnp.broadcast_to(row, (8, NE))
-
     for h in range(1, LEV + 1):
         across = span_y >> h
         bits = across.bit_length() - 1
         own_box = (index_x << bits) + (index_y >> h)
         for k in range(K):
             box = (own_box - meta_ref[2 + (h - 1) * K + k]) & (span_x * across - 1)
-            place_y = (box & (across - 1)) << h
-            tile = (box >> bits) * (span_y // 8) + (place_y >> 3)
-            inside = place_y & 7
-            if h == 1:
-                value = spread(panels[0][k : k + 1])
-            else:
-                first = 0 if h == 2 else 8
-                value = jnp.where(
-                    (sub // 2) % 2 == 0,
-                    spread(lower[0][first + k : first + k + 1]),
-                    spread(lower[1][first + k : first + k + 1]),
-                )
-                if h == 3:
-                    upper = jnp.where(
-                        (sub // 2) % 2 == 0,
-                        spread(lower[0][16 + k : 17 + k]),
-                        spread(lower[1][16 + k : 17 + k]),
-                    )
-                    value = jnp.where(sub < 4, value, upper)
-            if h < 3:
-                value = jnp.where((sub >= inside) & (sub < inside + 2**h), value, 0.0)
-            out_ref[tile] = out_ref[tile] + value
+            first = (box >> bits) * span_y + ((box & (across - 1)) << h)
+            for j in range(2**h):
+                if h == 1:
+                    value = panels[0][k : k + 1]
+                else:
+                    start = 8 * (h - 2 + j // 4) + k
+                    value = lower[j // 2 % 2][start : start + 1]
+                out_ref[first + j] += value
 
 
 def send_panels(meta, sy, points, up_ops, m2l_ops, down_ops, span_x, span_y):
     return pl.pallas_call(
         functools.partial(send_kernel, span_x, span_y),
-        out_shape=jax.ShapeDtypeStruct((span_x * span_y // 8, 8, NE), jnp.float32),
+        out_shape=jax.ShapeDtypeStruct((span_x * span_y, 1, NE), jnp.float32),
         in_specs=[
             pl.BlockSpec(memory_space=pltpu.SMEM),
             pl.BlockSpec(memory_space=pltpu.SMEM),
             pl.BlockSpec(memory_space=pltpu.VMEM),
-            pl.BlockSpec(memory_space=pl.ANY),
-            pl.BlockSpec(memory_space=pl.ANY),
-            pl.BlockSpec(memory_space=pl.ANY),
+            pl.BlockSpec(memory_space=pltpu.HBM),
+            pl.BlockSpec(memory_space=pltpu.HBM),
+            pl.BlockSpec(memory_space=pltpu.HBM),
         ],
         out_specs=pl.BlockSpec(memory_space=pltpu.VMEM),
         scratch_shapes=[
@@ -226,19 +207,16 @@
             pltpu.VMEM((LEV, K, 8, NE), jnp.float32),
             pltpu.SemaphoreType.DMA((LEV + 2,)),
         ],
-        compiler_params=pltpu.CompilerParams(vmem_limit_bytes=40 * 2**20),
+        compiler_params=pltpu.CompilerParams(vmem_limit_bytes=18 * 2**20),
         name="send_panels",
     )(meta, sy, points, up_ops, m2l_ops, down_ops)
 
 
 def far_kernel(
-    sy_ref, p_ref, held_ref, low_ref, high_ref, parts_ref, out_ref, row_ref, column_ref, tile_ref,
-    near_ref,
+    sy_ref, p_ref, held_ref, near_ref, parts_ref, out_ref, row_ref, column_ref, tile_ref,
 ):
     row_ref[...] = jnp.zeros((8, 384), jnp.float32)
-    near_ref[: ROWS // 2, :] = low_ref[...]
-    near_ref[ROWS // 2 :, :] = high_ref[...]
-    row_ref[0:1, :NE] = jnp.sum(parts_ref[...], axis=0, keepdims=True)
+    row_ref[0:1, :NE] = jnp.sum(parts_ref[...], axis=0)
     flipped = jnp.transpose(row_ref[...])
     column_ref[...] = jnp.broadcast_to(flipped[:NE, 0:1], (NE, LANES))
     for n, tile in enumerate(A_TILES + B_TILES):
@@ -267,130 +245,163 @@
     lax.fori_loop(0, ROWS, spread, 0, unroll=2)
 
 
-def far_and_sum(sy, points, held, low, high, parts):
+def far_and_sum(sy, points, held, near, parts):
     return pl.pallas_call(
         far_kernel,
         out_shape=jax.ShapeDtypeStruct((ROWS, LANES), jnp.float32),
         in_specs=[pl.BlockSpec(memory_space=pltpu.SMEM)]
-        + [pl.BlockSpec(memory_space=pltpu.VMEM)] * 5,
+        + [pl.BlockSpec(memory_space=pltpu.VMEM)] * 4,
         out_specs=pl.BlockSpec(memory_space=pltpu.VMEM),
         scratch_shapes=[
             pltpu.VMEM((8, 384), jnp.float32),
             pltpu.VMEM((NE, LANES), jnp.float32),
             pltpu.VMEM((40, 8, LANES), jnp.float32),
-            pltpu.VMEM((ROWS, LANES), jnp.float32),
         ],
-        compiler_params=pltpu.CompilerParams(vmem_limit_bytes=16 * 2**20),
+        compiler_params=pltpu.CompilerParams(vmem_limit_bytes=4 * 2**20),
         name="far_and_sum",
-    )(sy, points, held, low, high, parts)
+    )(sy, points, held, near, parts)
 
 
 PAD_Z = LZ + 2
-STEP = 4
-
-
-def near_kernel(first_x, count_x, fill_ref, source_ref, column_ref, out_ref, sum_ref):
+PLANES = 5
+STEP = 2
+TILES = PPL // 8
+LEAVES = CXL * LZ
+COLUMNS = 3 * CYL * LZ
+
+
+def choices():
+    chosen = np.zeros((LZ, 2 * LANES, 3 * CYL * LANES), np.float32)
+    for z in range(LZ):
+        for n in range(3 * CYL):
+            for part in range(3):
+                chosen[z, part * COLUMNS + n * LZ + z, n * LANES : (n + 1) * LANES] = 1.0
+    return jnp.asarray(chosen, dtype=jnp.bfloat16)
+
+
+def near_kernel(fill_ref, source_ref, column_ref, choice_ref, out_ref, sum_ref, place_ref):
     lanes = lax.broadcasted_iota(jnp.int32, (8, LANES), 1)
+    slots = lax.broadcasted_iota(jnp.int32, (8, LANES), 0)
     lower_half = lanes < PPL
-    ones = jnp.ones((8, LANES), jnp.bfloat16)
-    own = lax.rsqrt(jnp.full((1, LANES), SOFTENING, jnp.float32))
+    rest = column_ref[...]
+    high_part = rest.astype(jnp.bfloat16)
+    rest = rest - high_part.astype(jnp.float32)
+    middle_part = rest.astype(jnp.bfloat16)
+    low_part = (rest - middle_part.astype(jnp.float32)).astype(jnp.bfloat16)
+    column = lax.broadcasted_iota(jnp.int32, rest.shape, 1)
+    split = jnp.where(
+        column < COLUMNS,
+        high_part.astype(jnp.float32),
+        jnp.where(
+            column < 2 * COLUMNS, middle_part.astype(jnp.float32), low_part.astype(jnp.float32)
+        ),
+    ).astype(jnp.bfloat16)
+    for z in range(LZ):
+        place_ref[z] = jnp.dot(split, choice_ref[z], preferred_element_type=jnp.float32)
+
+    def add_tiles(leaf, step):
+        x = leaf // LZ
+        z = leaf % LZ
+        targets = []
+        for u in range(STEP):
+            start = pl.multiple_of(x * PPL + 8 * (STEP * step + u), 8)
+            low, high = [
+                [
+                    place_ref[z, pl.ds(start, 8), LANES * (2 * c + y) : LANES * (2 * c + y + 1)]
+                    for c in range(3)
+                ]
+                for y in range(2)
+            ]
+            for place in (low, high):
+                place.append(square(place[0]) + square(place[1]) + square(place[2]))
+            mixed = [jnp.where(lower_half, l, h) for l, h in zip(low, high)]
+            targets.append((low, high, mixed))
+        sums = [[None] * 3 for _ in range(STEP)]
+        for shift_x in range(3):
+            for shift_z in range(3):
+                row = (x + shift_x) * PAD_Z + z + shift_z
+                for side in range(2):
+                    mx, my, mz, norm, weight = [
+                        wide(source_ref[PLANES * side + c, pl.ds(row, 1), :]) for c in range(PLANES)
+                    ]
+                    for u in range(STEP):
+                        for n in (0, 1) if side == 0 else (2,):
+                            tx, ty, tz, own_norm = targets[u][n]
+                            d2 = (own_norm + norm) + tx * mx + ty * my + tz * mz
+                            value = weight * lax.rsqrt(d2)
+                            if side == 0 and shift_x == 1 and shift_z == 1:
+                                itself = lanes == slots + (8 * (STEP * step + u) + PPL * n)
+                                value = jnp.where(itself, 0.0, value)
+                            old = sums[u][n]
+                            sums[u][n] = value if old is None else old + value
+        for u in range(STEP):
+            low, high, mixed = sums[u]
+            start = pl.multiple_of(8 * (STEP * step + u), 8)
+            sum_ref[leaf, pl.ds(start, 8), :] = low + jnp.where(lower_half, mixed, 0.0)
+            sum_ref[leaf, pl.ds(PPL + start, 8), :] = high + jnp.where(lower_half, 0.0, mixed)
 
     def one_leaf_pair(leaf, carry):
         x = leaf // LZ
         z = leaf % LZ
-        held = jnp.maximum(
-            fill_ref[(first_x + x) * 2 * LZ + z], fill_ref[((first_x + x) * 2 + 1) * LZ + z]
-        )
-
-        def add_tiles(step, inner):
-            targets = []
-            for u in range(STEP):
-                start = pl.multiple_of(8 * (STEP * step + u), 8)
-                block = column_ref[first_x + x, pl.ds(start, 8), :]
-
-                def pick(c, y):
-                    lane = jnp.full((8, LANES), (c * 2 + y) * LZ, jnp.int32) + z
-                    return jnp.take_along_axis(block, lane, axis=1)
-
-                low = [pick(c, 0) for c in range(3)]
-                high = [pick(c, 1) for c in range(3)]
-                mixed = [jnp.where(lower_half, l, h) for l, h in zip(low, high)]
-                targets.append((low, high, mixed))
-            sums = [[None] * 3 for _ in range(STEP)]
-            for shift_x in range(3):
-                for shift_z in range(3):
-                    row = (first_x + x + shift_x) * PAD_Z + z + shift_z
-                    for side in range(2):
-                        source = [
-                            wide(source_ref[4 * side + c, pl.ds(row, 1), :]) for c in range(4)
-                        ]
-                        for u in range(STEP):
-                            for n in (0, 1) if side == 0 else (2,):
-                                tx, ty, tz = targets[u][n]
-                                d2 = square(tx - source[0]) + SOFTENING
-                                d2 += square(ty - source[1])
-                                d2 += square(tz - source[2])
-                                value = source[3] * lax.rsqrt(d2)
-                                old = sums[u][n]
-                                sums[u][n] = value if old is None else old + value
-            for u in range(STEP):
-                low, high, mixed = sums[u]
-                start = pl.multiple_of(8 * (STEP * step + u), 8)
-                sum_ref[leaf, pl.ds(start, 8), :] = low + jnp.where(lower_half, mixed, 0.0)
-                sum_ref[leaf, pl.ds(PPL + start, 8), :] = high + jnp.where(lower_half, 0.0, mixed)
+        held = jnp.maximum(fill_ref[x * 2 * LZ + z], fill_ref[(x * 2 + 1) * LZ + z])
+
+        def more(step, inner):
+            add_tiles(leaf, step)
             return inner
 
-        lax.fori_loop(0, (held + 8 * STEP - 1) // (8 * STEP), add_tiles, 0)
+        lax.fori_loop(0, (held + 8 * STEP - 1) // (8 * STEP), more, 0)
         return carry
 
-    lax.fori_loop(0, count_x * LZ, one_leaf_pair, 0)
+    lax.fori_loop(0, LEAVES, one_leaf_pair, 0)
+    ones = jnp.ones((2 * LANES, LANES), jnp.bfloat16)
+    diagonal = lax.broadcasted_iota(jnp.int32, (LANES, LANES), 0) == lax.broadcasted_iota(
+        jnp.int32, (LANES, LANES), 1
+    )
 
     def finish(group, carry):
         rows = []
         for n in range(8):
-            rest = sum_ref[8 * group + n]
-            total = None
-            for _ in range(3):
-                part = rest.astype(jnp.bfloat16)
-                rest = rest - part.astype(jnp.float32)
-                term = lax.dot_general(
-                    ones, part, (((1,), (1,)), ((), ())), preferred_element_type=jnp.float32
-                )
-                total = term if total is None else total + term
-            own_row = (first_x + group + 1) * PAD_Z + n + 1
-            rows.append(total[0:1] - source_ref[3, pl.ds(own_row, 1), :] * own)
+            whole = sum_ref[8 * group + n]
+            coarse = whole.astype(jnp.bfloat16)
+            fine = (whole - coarse.astype(jnp.float32)).astype(jnp.bfloat16)
+            added = jnp.dot(
+                jnp.concatenate([coarse, fine], axis=1), ones, preferred_element_type=jnp.float32
+            )
+            rows.append(jnp.sum(jnp.where(diagonal, added, 0.0), axis=0, keepdims=True))
         out_ref[pl.ds(pl.multiple_of(8 * group, 8), 8), :] = jnp.concatenate(rows, axis=0)
         return carry
 
-    lax.fori_loop(0, count_x, finish, 0)
-
-
-def near_sums(first_x, count_x, fill, sources, columns):
+    lax.fori_loop(0, LEAVES // 8, finish, 0)
+
+
+def near_sums(fill, sources, columns):
     return pl.pallas_call(
-        functools.partial(near_kernel, first_x, count_x),
-        out_shape=jax.ShapeDtypeStruct((count_x * LZ, LANES), jnp.float32),
+        near_kernel,
+        out_shape=jax.ShapeDtypeStruct((LEAVES, LANES), jnp.float32),
         in_specs=[pl.BlockSpec(memory_space=pltpu.SMEM)]
-        + [pl.BlockSpec(memory_space=pltpu.VMEM)] * 2,
+        + [pl.BlockSpec(memory_space=pltpu.VMEM)] * 3,
         out_specs=pl.BlockSpec(memory_space=pltpu.VMEM),
-        scratch_shapes=[pltpu.VMEM((count_x * LZ, LANES, LANES), jnp.float32)],
-        compiler_params=pltpu.CompilerParams(vmem_limit_bytes=24 * 2**20),
+        scratch_shapes=[
+            pltpu.VMEM((LEAVES, LANES, LANES), jnp.float32),
+            pltpu.VMEM((LZ, CXL * PPL, 3 * CYL * LANES), jnp.float32),
+        ],
+        compiler_params=pltpu.CompilerParams(vmem_limit_bytes=20 * 2**20),
         name="near_sums",
-    )(fill, sources, columns)
+    )(fill, sources, columns, choices())
 
 
 def extended(cells, sides, width):
     for axis, dim in sides:
         count = lax.axis_size(axis)
-        ends = count - 1
+        even = lax.axis_index(axis) % 2 == 0
         head = lax.slice_in_dim(cells, 0, width, axis=dim)
         tail = lax.slice_in_dim(cells, cells.shape[dim] - width, cells.shape[dim], axis=dim)
+        first = [(i, i ^ 1) for i in range(count)]
+        second = [(i, i + 1 if i % 2 else i - 1) for i in range(1, count - 1)]
+        inside = lax.ppermute(jnp.where(even, tail, head), axis, first)
+        outside = lax.ppermute(jnp.where(even, head, tail), axis, second)
         cells = jnp.concatenate(
-            [
-                lax.ppermute(tail, axis, [(i, (i + 1) % count) for i in range(ends)]),
-                cells,
-                lax.ppermute(head, axis, [((i + 1) % count, i) for i in range(ends)]),
-            ],
-            axis=dim,
+            [jnp.where(even, outside, inside), cells, jnp.where(even, inside, outside)], axis=dim
         )
     return cells
 
@@ -405,11 +416,11 @@
     return (jnp.where(occupied, charges, 0.0), occupied)
 
 
-def placed(rows, start_x, start_y):
+def placed(rows, start_x, start_y, start_z):
     size_x, size_y = rows.shape[1:3]
     along_x = (start_x + jnp.arange(size_x)).astype(jnp.float32)
     along_y = (start_y + jnp.arange(size_y)).astype(jnp.float32)
-    along_z = (jnp.arange(SLOTS) // PPL).astype(jnp.float32)
+    along_z = (start_z + jnp.arange(SLOTS) // PPL).astype(jnp.float32)
     return jnp.stack(
         [
             rows[0] + along_x[:, None, None],
@@ -435,7 +446,7 @@
     local_rows = jnp.concatenate([positions, weights[None]], axis=0)
     padded = extended(local_rows, (("gx", 1), ("gy", 2)), 1)
 
-    own = placed(local_rows, 0, 0)
+    own = placed(local_rows, 0, 0, 0)
     points = leaf_pairs(own).reshape(4, ROWS, LANES)
     held = leaf_pairs(occupied.astype(jnp.float32)[None]).reshape(ROWS, LANES)
     offsets = [devices_x * (devices_y - (devices_y >> h - 1)) for h in range(1, LEV + 1)]
@@ -449,26 +460,25 @@
         ]
     )
     sent = send_panels(meta, sy, points, up_ops, m2l_ops, down_ops, devices_x, devices_y)
-    along_x = lax.all_to_all(
-        sent.reshape(devices_x, devices_y, NE), "gx", split_axis=0, concat_axis=0, tiled=True
-    )
-    middle = jnp.sum(along_x, axis=0).reshape(devices_y, 1, NE)
-    parts = lax.all_to_all(middle, "gy", split_axis=0, concat_axis=0, tiled=True)
-
-    around = placed(padded, -1, -1)
-    sources = jnp.concatenate(
-        [leaf_pairs(around[:, :, 1:3]), leaf_pairs(jnp.stack([around[:, :, 0], around[:, :, 3]], 2))]
-    )
-    sources = jnp.pad(sources, ((0, 0), (0, 0), (1, 1), (0, 0)))
-    sources = sources.reshape(8, (CXL + 2) * PAD_Z, LANES)
-    columns = own[:3].reshape(3, CXL, CYL, LZ, PPL).transpose(1, 4, 0, 2, 3)
-    columns = columns.reshape(CXL, PPL, 3 * CYL * LZ)
-    columns = jnp.pad(columns, ((0, 0), (0, 0), (0, LANES - columns.shape[2])))
+    parts = lax.all_to_all(sent, ("gx", "gy"), split_axis=0, concat_axis=0, tiled=True)
+
+    around = placed(padded, -1 - CXL // 2, -1 - CYL // 2, -(LZ // 2))
+    norm = jnp.sum(square(around[:3]), axis=0, keepdims=True) + SOFTENING
+    planes = jnp.concatenate([-2.0 * around[:3], norm, around[3:]])
+    sides = [planes[:, :, 1:3], jnp.stack([planes[:, :, 0], planes[:, :, 3]], axis=2)]
+    sources = jnp.concatenate([leaf_pairs(side) for side in sides])
+    sources = jnp.pad(sources, ((0, 0), (0, 0), (1, 1), (0, 0)), constant_values=0.0)
+    beyond = jnp.pad(jnp.zeros((LZ,), jnp.float32), (1, 1), constant_values=1.0)
+    is_norm = (jnp.arange(2 * PLANES) % PLANES == 3).astype(jnp.float32)
+    sources = sources + is_norm[:, None, None, None] * beyond[None, None, :, None]
+    sources = sources.reshape(2 * PLANES, (CXL + 2) * PAD_Z, LANES)
+    columns = placed(local_rows, -(CXL // 2), -(CYL // 2), -(LZ // 2))[:3]
+    columns = columns.reshape(3, CXL, CYL, LZ, PPL).transpose(1, 4, 0, 2, 3)
+    columns = columns.reshape(CXL * PPL, COLUMNS)
+    columns = jnp.concatenate([columns] * 3 + [jnp.zeros((CXL * PPL, 2 * LANES - 3 * COLUMNS))], 1)
     fill = counts.reshape(-1)
-    half = CXL // 2
-    near = [near_sums(0, half, fill, sources, columns)]
-    near.append(near_sums(half, half, fill, sources, columns))
-    total = far_and_sum(sy, points, held, near[0], near[1], parts.reshape(devices_y, NE))
+    near = near_sums(fill, sources, columns)
+    total = far_and_sum(sy, points, held, near, parts)
     total = total.reshape(CXL, LZ, CYL, PPL).transpose(0, 2, 1, 3)
     return total.reshape(CXL, CYL, SLOTS)
 

time: 103 us -> 116 us (1.13)
  the two profiles are of different devices: /device:TPU:11 before, /device:TPU:1 now
where the time goes in v2:
time: 116 us; the launch traced here: 115 us
  Pallas kernels  45.6 us (39%)
  local copies, waits for them, and re-layouts  29.5 us (25%)
  starting transfers between devices  25.7 us (22%)
  other arithmetic  10.5 us (9%)
  waiting for transfers between devices  2.97 us (3%)
    pallas_call x1, Pallas kernels, near_sums(): pl.pallas_call(near_kernel, out_shape=jax.ShapeDtypeStruct((LEAVES, LANES...  27.3 us
    all_to_all x1, starting transfers between devices, per_device(): lax.all_to_all(sent, ('gx', 'gy'), split_axis=0, concat_axis=0, tiled=True)  17.6 us
    pallas_call x1, Pallas kernels, send_panels(): pl.pallas_call(functools.partial(send_kernel, span_x, span_y), out_shape=...  14.7 us
    unnamed x33, local copies, waits for them, and re-layouts  11.3 us
    ppermute x2, starting transfers between devices, extended(): outside = lax.ppermute(jnp.where(even, head, tail), axis, second)  4.19 us
    transpose x2, local copies, waits for them, and re-layouts, leaf_pairs(): split = cells.reshape(lead, size_x, 2, LZ, PPL).transpose(0, 1, 3, 2, 4)  4.07 us
    ppermute x2, starting transfers between devices, extended(): inside = lax.ppermute(jnp.where(even, tail, head), axis, first)  3.93 us
    reshape x2, local copies, waits for them, and re-layouts, leaf_pairs(): return split.reshape(lead, size_x, LZ, LANES)  3.87 us
  transfers between devices with their start and end apart: 5, of which 1 were waited for; matrix products, arithmetic and copies ran while one was open for 22% of the time, Pallas kernels for 37%

profile of v2, /device:TPU:1, one launch (start us, length us, event | category | flops | bytes accessed | tf_op | source)
XLA Modules:
  0.0 114.6 jit_solution(3911716785985798916)
XLA Ops:
  0.0 0.9 broadcast_in_dim.12
  1.0 0.8 compare_select_fusion
  1.8 0.7 broadcast_select_fusion.7
  2.6 3.7 %collective-permute-start.1 = (f32[4,1,2,512]{3,2,1,0:T(2,128)S(1)}, f32[4,1,2,512]{3,2,1,0:T(2,128)S(1)}, u32[]{:S(2)}, u32[]{:S(2)}) collective-permute-start(f32[4,1,2,512]{3,2,1,0:T(2,128)S(1)} %broadcast_select_fusion.6), channel_id=1, source_target_pairs={{0,32},{32,0},{64,96},{96,64},{128,160},{160,128},{192,224},{224,1... | collective-permute-start | bytes 49160 | tf_op jit(solution)/shard_map/ppermute | solution.py:401
  7.0 0.9 slice_add_fusion.7
  8.7 1.0 slice_reduce_fusion
  10.4 0.7 broadcast_add_fusion
  11.2 4.1 %copy-done = f32[3,8,296,296]{3,2,1,0:T(8,128)S(1)} copy-done((f32[3,8,296,296]{3,2,1,0:T(8,128)S(1)}, f32[3,8,296,296]{3,2,1,0:T(8,128)}, u32[]{:S(2)}) %copy-start) | copy-done | bytes 8411160
  15.3 1.3 %copy-done.5 = f32[3,296,296]{2,1,0:T(8,128)S(1)} copy-done((f32[3,296,296]{2,1,0:T(8,128)S(1)}, f32[3,296,296]{2,1,0:T(8,128)}, u32[]{:S(2)}) %copy-start.5) | copy-done | bytes 1051416
  16.7 14.7 %send_panels.1 = f32[256,1,296]{2,1,0:T(1,128)} custom-call(s32[26]{0:T(128)S(1)} %concatenate.34.meta_ref, f32[24]{0:T(128)S(1)} %pad_maximum_fusion.6.sy_ref, f32[4,64,128]{2,1,0:T(8,128)S(1)} %reshape_reshape.8.p_ref, f32[3,296,296]{2,1,0:T(8,128)S(1)} %copy-done.5, f32[3,8,296,296]{3,2,1,0:T(8,128)S(1)} %copy-done, f32[2,2,296,296]{3,2,1,0:T(8,128)S(1)} %copy-done.4), custom_call_target="tpu_custom_call" | custom-call | tf_op jit(solution)/shard_map/send_panels/pallas_call | solution.py:188
  31.4 17.6 %all-to-all-start = ((f32[256,1,296]{2,1,0:T(1,128)}), f32[256,1,296]{2,1,0:T(1,128)S(1)}, u32[]{:S(2)}, u32[]{:S(2)}) async-start(f32[256,1,296]{2,1,0:T(1,128)} %send_panels.1), calls=%async_computation | async-start | bytes 786432 | tf_op jit(solution)/shard_map/all_to_all | solution.py:463
  50.1 1.1 maximum_maximum_fusion.column_ref
  51.5 0.7 reshape.169.held_ref
  52.4 3.5 %collective-permute-start.2 = (f32[4,10,1,512]{3,2,1,0:T(1,128)S(1)}, f32[4,10,1,512]{3,2,1,0:T(1,128)S(1)}, u32[]{:S(2)}, u32[]{:S(2)}) collective-permute-start(f32[4,10,1,512]{3,2,1,0:T(1,128)S(1)} %get-tuple-element.19), channel_id=1, source_target_pairs={{1,2},{2,1},{3,4},{4,3},{5,6},{6,5},{7,8},{8,7},{9,10},{10,9},{11,... | collective-permute-start | bytes 245768 | tf_op jit(solution)/shard_map/ppermute | solution.py:402
  56.3 3.0 %collective-permute-done.2 = f32[4,10,1,512]{3,2,1,0:T(1,128)S(1)} collective-permute-done((f32[4,10,1,512]{3,2,1,0:T(1,128)S(1)}, f32[4,10,1,512]{3,2,1,0:T(1,128)S(1)}, u32[]{:S(2)}, u32[]{:S(2)}) %collective-permute-start.2) | collective-permute-done | bytes 81952 | tf_op jit(solution)/shard_map/ppermute | solution.py:402
  60.7 1.0 reshape.161
  61.7 2.1 %copy.26 = f32[5,10,8,2,64]{4,3,2,1,0:T(2,128)} copy(f32[5,10,8,2,64]{4,2,3,1,0:T(8,128)} %bitcast.22) | data formatting | bytes 409600 | tf_op jit(solution)/shard_map/transpose | solution.py:436
  63.8 1.9 %reshape.162 = f32[5,10,8,128]{3,2,1,0:T(8,128)} reshape(f32[5,10,8,2,64]{4,3,2,1,0:T(2,128)} %copy.26) | data formatting | bytes 409600 | tf_op jit(solution)/shard_map/reshape | solution.py:437
  65.8 2.1 %fusion.2 = f32[5,10,2,512]{3,2,1,0:T(2,128)} fusion(f32[1,10,4,512]{3,2,1,0:T(4,128)} %copy-done.13, f32[1,10,4,512]{3,2,1,0:T(4,128)} %copy-done.14, f32[3,10,4,512]{3,2,1,0:T(4,128)} %copy-done.11), kind=kLoop, calls=%fused_computation.12 | loop fusion | flops 665600 | bytes 614400 | tf_op jit(solution)/shard_map/stack | solution.py:468
  67.9 1.9 %reshape.163 = f32[5,10,2,8,64]{4,3,2,1,0:T(8,128)} reshape(f32[5,10,2,512]{3,2,1,0:T(2,128)} %fusion.2) | data formatting | bytes 409600 | tf_op jit(solution)/shard_map/reshape | solution.py:436
  69.9 2.0 %copy.27 = f32[5,10,8,2,64]{4,3,2,1,0:T(2,128)} copy(f32[5,10,8,2,64]{4,2,3,1,0:T(8,128)} %bitcast.23) | data formatting | bytes 409600 | tf_op jit(solution)/shard_map/transpose | solution.py:436
  71.8 1.9 %reshape.164 = f32[5,10,8,128]{3,2,1,0:T(8,128)} reshape(f32[5,10,8,2,64]{4,3,2,1,0:T(2,128)} %copy.27) | data formatting | bytes 409600 | tf_op jit(solution)/shard_map/reshape | solution.py:437
  73.7 2.1 %fusion = f32[10,10,10,128]{3,2,1,0:T(8,128)} fusion(f32[5,10,8,128]{3,2,1,0:T(8,128)} %reshape.164, f32[5,10,8,128]{3,2,1,0:T(8,128)} %reshape.162, f32[10,10]{1,0:T(8,128)S(1)} %broadcast_multiply_fusion.1), kind=kLoop, calls=%fused_computation.3 | loop fusion | flops 896000 | bytes 922000 | tf_op jit(solution)/shard_map/add | solution.py:473
  75.8 2.0 %reshape.165.source_ref = f32[10,100,128]{2,1,0:T(8,128)} reshape(f32[10,10,10,128]{3,2,1,0:T(8,128)} %fusion) | data formatting | bytes 1024000 | tf_op jit(solution)/shard_map/reshape | solution.py:474
  77.8 1.0 copy-done.2
  78.9 1.0 copy-done.3
  79.9 27.3 %near_sums.1.near_ref = f32[64,128]{1,0:T(8,128)S(1)} custom-call(s32[128]{0:T(128)S(1)} %reshape.160.fill_ref, f32[10,100,128]{2,1,0:T(8,128)S(1)} %copy-done.2, f32[512,256]{1,0:T(8,128)S(1)} %copy-done.3, bf16[8,256,768]{2,1,0:T(8,128)(2,1)S(1)} %copy-done.1), custom_call_target="tpu_custom_call" | custom-call | tf_op jit(solution)/shard_map/near_sums/pallas_call | solution.py:378
  107.8 0.9 copy-done.7
  108.7 0.8 copy-done.9
  109.5 0.8 copy-done.10
  110.2 3.5 %far_and_sum.1 = f32[64,128]{1,0:T(8,128)S(1)} custom-call(f32[24]{0:T(128)S(1)} %pad_maximum_fusion.6.sy_ref, f32[4,64,128]{2,1,0:T(8,128)S(1)} %copy-done.7, f32[64,128]{1,0:T(8,128)S(1)} %copy-done.10, f32[64,128]{1,0:T(8,128)S(1)} %copy-done.9, f32[256,1,296]{2,1,0:T(1,128)S(1)} %all-to-all-done.parts_ref), custom_call_target="tpu_custom_call" | custom-call | tf_op jit(solution)/shard_map/far_and_sum/pallas_call | solution.py:249
  113.9 0.7 reshape.168
  (83 shorter events, 6.3 us)
Async XLA Ops:
  0.0 11.2 %copy-start.4 = (f32[2,2,296,296]{3,2,1,0:T(8,128)S(1)}, f32[2,2,296,296]{3,2,1,0:T(8,128)}, u32[]{:S(2)}) copy-start(f32[2,2,296,296]{3,2,1,0:T(8,128)} %down_hbm.1) | copy-start | bytes 4205572
  2.6 49.6 %collective-permute-start.1 = (f32[4,1,2,512]{3,2,1,0:T(2,128)S(1)}, f32[4,1,2,512]{3,2,1,0:T(2,128)S(1)}, u32[]{:S(2)}, u32[]{:S(2)}) collective-permute-start(f32[4,1,2,512]{3,2,1,0:T(2,128)S(1)} %broadcast_select_fusion.6), channel_id=1, source_target_pairs={{0,32},{32,0},{64,96},{96,64},{128,160},{160,128},{192,224},{224,1... | collective-permute-start | bytes 49160 | tf_op jit(solution)/shard_map/ppermute | solution.py:401
  6.2 46.0 %collective-permute-start = (f32[4,1,2,512]{3,2,1,0:T(2,128)S(1)}, f32[4,1,2,512]{3,2,1,0:T(2,128)S(1)}, u32[]{:S(2)}, u32[]{:S(2)}) collective-permute-start(f32[4,1,2,512]{3,2,1,0:T(2,128)S(1)} %get-tuple-element.8), channel_id=1, source_target_pairs={{32,64},{64,32},{96,128},{128,96},{160,192},{192,160},{33,65},{65,... | collective-permute-start | bytes 49160 | tf_op jit(solution)/shard_map/ppermute | solution.py:402
  8.7 22.7 %copy-start.6 = (f32[4,64,128]{2,1,0:T(8,128)}, f32[4,64,128]{2,1,0:T(8,128)S(1)}, u32[]{:S(2)}) copy-start(f32[4,64,128]{2,1,0:T(8,128)S(1)} %reshape_reshape.8.p_ref) | copy-start | bytes 393220
  11.2 4.1 %copy-start = (f32[3,8,296,296]{3,2,1,0:T(8,128)S(1)}, f32[3,8,296,296]{3,2,1,0:T(8,128)}, u32[]{:S(2)}) copy-start(f32[3,8,296,296]{3,2,1,0:T(8,128)} %m2l_hbm.1) | copy-start | bytes 25233412
  15.3 1.3 %copy-start.5 = (f32[3,296,296]{2,1,0:T(8,128)S(1)}, f32[3,296,296]{2,1,0:T(8,128)}, u32[]{:S(2)}) copy-start(f32[3,296,296]{2,1,0:T(8,128)} %up_hbm.1) | copy-start | bytes 3154180
  16.7 32.4 %copy-start.15 = (s32[8,2,8]{2,1,0:T(2,128)S(1)}, s32[8,2,8]{2,1,0:T(2,128)}, u32[]{:S(2)}) copy-start(s32[8,2,8]{2,1,0:T(2,128)} %param.11) | copy-start | bytes 1540
  31.4 20.8 %copy-start.12 = (f32[3,8,2,512]{3,2,1,0:T(2,128)S(1)}, f32[3,8,2,512]{3,2,1,0:T(2,128)}, u32[]{:S(2)}) copy-start(f32[3,8,2,512]{3,2,1,0:T(2,128)} %param.9) | copy-start | bytes 294916
  31.4 76.4 %all-to-all-start = ((f32[256,1,296]{2,1,0:T(1,128)}), f32[256,1,296]{2,1,0:T(1,128)S(1)}, u32[]{:S(2)}, u32[]{:S(2)}) async-start(f32[256,1,296]{2,1,0:T(1,128)} %send_panels.1), calls=%async_computation | async-start | bytes 786432 | tf_op jit(solution)/shard_map/all_to_all | solution.py:463
  52.4 6.8 %collective-permute-start.2 = (f32[4,10,1,512]{3,2,1,0:T(1,128)S(1)}, f32[4,10,1,512]{3,2,1,0:T(1,128)S(1)}, u32[]{:S(2)}, u32[]{:S(2)}) collective-permute-start(f32[4,10,1,512]{3,2,1,0:T(1,128)S(1)} %get-tuple-element.19), channel_id=1, source_target_pairs={{1,2},{2,1},{3,4},{4,3},{5,6},{6,5},{7,8},{8,7},{9,10},{10,9},{11,... | collective-permute-start | bytes 245768 | tf_op jit(solution)/shard_map/ppermute | solution.py:402
  56.0 3.3 %collective-permute-start.3 = (f32[4,10,1,512]{3,2,1,0:T(1,128)S(1)}, f32[4,10,1,512]{3,2,1,0:T(1,128)S(1)}, u32[]{:S(2)}, u32[]{:S(2)}) collective-permute-start(f32[4,10,1,512]{3,2,1,0:T(1,128)S(1)} %get-tuple-element.20), channel_id=1, source_target_pairs={{0,1},{1,0},{2,3},{3,2},{4,5},{5,4},{6,7},{7,6},{8,9},{9,8},{10,11... | collective-permute-start | bytes 245768 | tf_op jit(solution)/shard_map/ppermute | solution.py:401
  59.7 0.9 copy-start.13
  59.8 0.7 copy-start.11
  59.8 0.8 copy-start.14
  61.7 16.1 %copy-start.1 = (bf16[8,256,768]{2,1,0:T(8,128)(2,1)S(1)}, bf16[8,256,768]{2,1,0:T(8,128)(2,1)}, u32[]{:S(2)}) copy-start(bf16[8,256,768]{2,1,0:T(8,128)(2,1)} %constant.118.clone.choice_ref) | copy-start | bytes 9437188
  77.8 1.0 copy-start.2
  78.9 1.0 copy-start.3
  107.2 0.6 copy-start.8
  107.8 0.9 copy-start.7
  108.7 0.8 copy-start.9
  109.5 0.8 copy-start.10

commit v3 on v2

--- a/solution.py
+++ b/solution.py
@@ -42,21 +42,32 @@
     return pl.ds(64 + 8 + 2 * (b - 1) + (1 if c else 0), P_ORD - 2, stride=28)
 
 
+def lattice_y(h):
+    index_y = lax.axis_index("gy")
+    base = (((index_y >> h) << h) - index_y) * CYL
+    span = CYL * 2**h
+    return [
+        base.astype(jnp.float32)
+        + float(0.5 * span * (1.0 + SURFACE_REACH * LATTICE[b]) - 0.5 * CYL)
+        for b in range(P_ORD)
+    ]
+
+
 def wide(row):
     return jnp.broadcast_to(row, (8, LANES))
 
 
 def lattice_x(a):
-    return float(0.5 * CXL + SURFACE_REACH * 0.5 * CXL * LATTICE[a])
+    return float(SURFACE_REACH * 0.5 * CXL * LATTICE[a])
 
 
 def lattice_z(c):
-    return float(0.5 * LZ + SURFACE_REACH * 0.5 * LZ * LATTICE[c])
+    return float(SURFACE_REACH * 0.5 * LZ * LATTICE[c])
 
 
 def along_sublanes(half):
     steps = lax.broadcasted_iota(jnp.int32, (8, LANES), 0).astype(jnp.float32)
-    return half - SURFACE_REACH * half + steps * (SURFACE_REACH * half * 2.0 / (P_ORD - 1))
+    return steps * (SURFACE_REACH * half * 2.0 / (P_ORD - 1)) - SURFACE_REACH * half
 
 
 def square(value):
@@ -85,12 +96,12 @@
 
 
 def row_of(p_ref, r):
-    return [wide(p_ref[c, pl.ds(r, 1), :]) for c in range(4)]
+    return [wide(p_ref[c, pl.ds(r, 1), :]) for c in range(p_ref.shape[0])]
 
 
 def send_kernel(
-    span_x, span_y, meta_ref, sy_ref, p_ref, up_hbm, m2l_hbm, down_hbm, out_ref,
-    up_ref, m2l_ref, down_ref, check_ref, row_ref, column_ref, panel_ref, sems,
+    span_x, span_y, lists_ref, counts_ref, positions_ref, charges_ref, up_hbm, m2l_hbm, down_hbm,
+    out_ref, p_ref, up_ref, m2l_ref, down_ref, check_ref, row_ref, column_ref, panel_ref, sems,
 ):
     copies = [pltpu.make_async_copy(up_hbm, up_ref, sems.at[0])]
     copies += [
@@ -100,9 +111,31 @@
     for copy in copies:
         copy.start()
     row_ref[...] = jnp.zeros((8, 384), jnp.float32)
+    lane = lax.broadcasted_iota(jnp.int32, (CYL, LANES), 1)
+    upper = lane // PPL
+    slot = lane % PPL
+    along_y = lax.broadcasted_iota(jnp.int32, (CYL, LANES), 0)
+    for x in range(CXL):
+        for q in range(SLOTS // LANES):
+            here = slice(LANES * q, LANES * (q + 1))
+            rows = slice(8 * x + CYL * q, 8 * x + CYL * (q + 1))
+            place_z = (upper + (2 * q - LZ // 2)).astype(jnp.float32)
+            p_ref[0, rows, :] = positions_ref[0, x, :, here] + float(x - CXL // 2)
+            p_ref[1, rows, :] = positions_ref[1, x, :, here] + (along_y - 1).astype(jnp.float32)
+            p_ref[2, rows, :] = positions_ref[2, x, :, here] + place_z
+            held = [
+                jnp.where(
+                    upper == 0,
+                    counts_ref[(x * CYL + y) * LZ + 2 * q],
+                    counts_ref[(x * CYL + y) * LZ + 2 * q + 1],
+                )
+                for y in range(CYL)
+            ]
+            held = jnp.where(along_y == 0, held[0], held[1])
+            p_ref[3, rows, :] = jnp.where(slot < held, charges_ref[x, :, here], 0.0)
 
     for h in range(LEV):
-        ys = [sy_ref[8 * h + b] for b in range(P_ORD)]
+        ys = lattice_y(h + 1)
         for squares, tiles in ((a_squares, A_TILES), (bc_squares, B_TILES + C_TILES)):
 
             def gather(r, sums):
@@ -166,14 +199,15 @@
         for side in range(2)
     ]
     out_ref[...] = jnp.zeros(out_ref.shape, jnp.float32)
-    index_x = meta_ref[0]
-    index_y = meta_ref[1]
+    index_x = lax.axis_index("gx")
+    index_y = lax.axis_index("gy")
     for h in range(1, LEV + 1):
+        offset = span_x * (span_y - (span_y >> h - 1))
         across = span_y >> h
         bits = across.bit_length() - 1
         own_box = (index_x << bits) + (index_y >> h)
         for k in range(K):
-            box = (own_box - meta_ref[2 + (h - 1) * K + k]) & (span_x * across - 1)
+            box = (own_box - lists_ref[offset, k]) & (span_x * across - 1)
             first = (box >> bits) * span_y + ((box & (across - 1)) << h)
             for j in range(2**h):
                 if h == 1:
@@ -184,7 +218,7 @@
                 out_ref[first + j] += value
 
 
-def send_panels(meta, sy, points, up_ops, m2l_ops, down_ops, span_x, span_y):
+def send_panels(lists, counts, positions, charges, up_ops, m2l_ops, down_ops, span_x, span_y):
     return pl.pallas_call(
         functools.partial(send_kernel, span_x, span_y),
         out_shape=jax.ShapeDtypeStruct((span_x * span_y, 1, NE), jnp.float32),
@@ -192,12 +226,14 @@
             pl.BlockSpec(memory_space=pltpu.SMEM),
             pl.BlockSpec(memory_space=pltpu.SMEM),
             pl.BlockSpec(memory_space=pltpu.VMEM),
+            pl.BlockSpec(memory_space=pltpu.VMEM),
             pl.BlockSpec(memory_space=pltpu.HBM),
             pl.BlockSpec(memory_space=pltpu.HBM),
             pl.BlockSpec(memory_space=pltpu.HBM),
         ],
         out_specs=pl.BlockSpec(memory_space=pltpu.VMEM),
         scratch_shapes=[
+            pltpu.VMEM((4, ROWS, LANES), jnp.float32),
             pltpu.VMEM((LEV, NE, NE), jnp.float32),
             pltpu.VMEM((LEV, K, NE, NE), jnp.float32),
             pltpu.VMEM((LEV - 1, 2, NE, NE), jnp.float32),
@@ -207,14 +243,12 @@
             pltpu.VMEM((LEV, K, 8, NE), jnp.float32),
             pltpu.SemaphoreType.DMA((LEV + 2,)),
         ],
-        compiler_params=pltpu.CompilerParams(vmem_limit_bytes=18 * 2**20),
+        compiler_params=pltpu.CompilerParams(vmem_limit_bytes=46 * 2**20),
         name="send_panels",
-    )(meta, sy, points, up_ops, m2l_ops, down_ops)
-
-
-def far_kernel(
-    sy_ref, p_ref, held_ref, near_ref, parts_ref, out_ref, row_ref, column_ref, tile_ref,
-):
+    )(lists, counts, positions, charges, up_ops, m2l_ops, down_ops)
+
+
+def far_kernel(points_ref, near_ref, parts_ref, out_ref, row_ref, column_ref, tile_ref):
     row_ref[...] = jnp.zeros((8, 384), jnp.float32)
     row_ref[0:1, :NE] = jnp.sum(parts_ref[...], axis=0)
     flipped = jnp.transpose(row_ref[...])
@@ -225,10 +259,11 @@
         n += len(A_TILES + B_TILES)
         tile_ref[n] = jnp.zeros((8, LANES), jnp.float32)
         tile_ref[n, 1:7, :] = column_ref[strided_rows(*tile), :]
-    ys = [sy_ref[b] for b in range(P_ORD)]
-
-    def spread(r, carry):
-        x8, y8, z8, w8 = row_of(p_ref, r)
+    ys = lattice_y(1)
+    lower_half = lax.broadcasted_iota(jnp.int32, (1, LANES), 1) < PPL
+
+    def potential(r):
+        x8, y8, z8, held = row_of(points_ref, r)
         y_parts = [square(ys[b] - y8) for b in range(P_ORD)]
         totals = [jnp.zeros((8, LANES), jnp.float32) for _ in range(4)]
         n = 0
@@ -237,29 +272,36 @@
                 totals[n % 4] += tile_ref[n] * lax.rsqrt(d2)
                 n += 1
         far = jnp.sum(totals[0] + totals[1] + (totals[2] + totals[3]), axis=0, keepdims=True)
-        here = pl.ds(r, 1)
-        value = near_ref[here, :] + far
-        out_ref[here, :] = jnp.where(held_ref[here, :] > 0, value, 0.0)
+        return jnp.where(held[0:1] > 0, near_ref[pl.ds(r, 1), :] + far, 0.0)
+
+    def one_x(x, carry):
+        for q in range(LZ // 2):
+            first = potential(x * LZ + 2 * q)
+            second = potential(x * LZ + 2 * q + 1)
+            here = slice(LANES * q, LANES * (q + 1))
+            turned = pltpu.roll(second, PPL, 1)
+            out_ref[x, 0:1, here] = jnp.where(lower_half, first, turned)
+            turned = pltpu.roll(first, PPL, 1)
+            out_ref[x, 1:2, here] = jnp.where(lower_half, turned, second)
         return carry
 
-    lax.fori_loop(0, ROWS, spread, 0, unroll=2)
-
-
-def far_and_sum(sy, points, held, near, parts):
+    lax.fori_loop(0, CXL, one_x, 0)
+
+
+def far_and_sum(points, near, parts):
     return pl.pallas_call(
         far_kernel,
-        out_shape=jax.ShapeDtypeStruct((ROWS, LANES), jnp.float32),
-        in_specs=[pl.BlockSpec(memory_space=pltpu.SMEM)]
-        + [pl.BlockSpec(memory_space=pltpu.VMEM)] * 4,
+        out_shape=jax.ShapeDtypeStruct((CXL, CYL, SLOTS), jnp.float32),
+        in_specs=[pl.BlockSpec(memory_space=pltpu.VMEM)] * 3,
         out_specs=pl.BlockSpec(memory_space=pltpu.VMEM),
         scratch_shapes=[
             pltpu.VMEM((8, 384), jnp.float32),
             pltpu.VMEM((NE, LANES), jnp.float32),
             pltpu.VMEM((40, 8, LANES), jnp.float32),
         ],
-        compiler_params=pltpu.CompilerParams(vmem_limit_bytes=4 * 2**20),
+        compiler_params=pltpu.CompilerParams(vmem_limit_bytes=16 * 2**20),
         name="far_and_sum",
-    )(sy, points, held, near, parts)
+    )(points, near, parts)
 
 
 PAD_Z = LZ + 2
@@ -267,37 +309,74 @@
 STEP = 2
 TILES = PPL // 8
 LEAVES = CXL * LZ
-COLUMNS = 3 * CYL * LZ
-
-
-def choices():
-    chosen = np.zeros((LZ, 2 * LANES, 3 * CYL * LANES), np.float32)
-    for z in range(LZ):
-        for n in range(3 * CYL):
-            for part in range(3):
-                chosen[z, part * COLUMNS + n * LZ + z, n * LANES : (n + 1) * LANES] = 1.0
-    return jnp.asarray(chosen, dtype=jnp.bfloat16)
-
-
-def near_kernel(fill_ref, source_ref, column_ref, choice_ref, out_ref, sum_ref, place_ref):
+PARTS = 3
+CHOICE = 3 * LZ
+
+
+def near_kernel(
+    fill_ref, table_ref, out_ref, points_ref, source_ref, sum_ref, turn_ref, place_ref
+):
     lanes = lax.broadcasted_iota(jnp.int32, (8, LANES), 1)
     slots = lax.broadcasted_iota(jnp.int32, (8, LANES), 0)
     lower_half = lanes < PPL
-    rest = column_ref[...]
-    high_part = rest.astype(jnp.bfloat16)
-    rest = rest - high_part.astype(jnp.float32)
-    middle_part = rest.astype(jnp.bfloat16)
-    low_part = (rest - middle_part.astype(jnp.float32)).astype(jnp.bfloat16)
-    column = lax.broadcasted_iota(jnp.int32, rest.shape, 1)
-    split = jnp.where(
-        column < COLUMNS,
-        high_part.astype(jnp.float32),
-        jnp.where(
-            column < 2 * COLUMNS, middle_part.astype(jnp.float32), low_part.astype(jnp.float32)
-        ),
-    ).astype(jnp.bfloat16)
+    wide_x = CXL + 2
+    lane = lax.broadcasted_iota(jnp.int32, (wide_x, LANES), 1)
+    lower = lane < PPL
+    along_x = lax.broadcasted_iota(jnp.int32, (wide_x, LANES), 0)
+    along_x = (along_x - (1 + CXL // 2)).astype(jnp.float32)
+    for plane in range(2 * PLANES):
+        value = 1.0 if plane % PLANES == 3 else 0.0
+        source_ref[plane] = jnp.full(source_ref.shape[1:], value, jnp.float32)
+    for side, (first, second) in enumerate(((1, 2), (0, 3))):
+        along_y = jnp.where(lower, float(first - 2), float(second - 2))
+        for z in range(LZ):
+            here = slice(z // 2 * LANES, (z // 2 + 1) * LANES)
+
+            def both(c):
+                one = table_ref[first, c, :, here]
+                two = table_ref[second, c, :, here]
+                if z % 2:
+                    one = pltpu.roll(one, PPL, 1)
+                else:
+                    two = pltpu.roll(two, PPL, 1)
+                return jnp.where(lower, one, two)
+
+            held = jnp.where(
+                lower,
+                jnp.broadcast_to(table_ref[first, 4, :, z : z + 1], (wide_x, LANES)),
+                jnp.broadcast_to(table_ref[second, 4, :, z : z + 1], (wide_x, LANES)),
+            )
+            held = (lane % PPL).astype(jnp.float32) < held
+            coords = [both(0) + along_x, both(1) + along_y, both(2) + float(z - LZ // 2)]
+            norm = square(coords[0]) + square(coords[1]) + square(coords[2]) + SOFTENING
+            planes = [-2.0 * coord for coord in coords]
+            planes += [norm, jnp.where(held, both(3), 0.0)]
+            for n, plane in enumerate(planes):
+                source_ref[PLANES * side + n, pl.ds(z + 1, wide_x, stride=PAD_Z), :] = plane
+            if side == 0:
+                for n, plane in enumerate(coords + [held.astype(jnp.float32)]):
+                    points_ref[n, pl.ds(z, CXL, stride=LZ), :] = plane[1 : CXL + 1]
+
+    turn_ref[...] = jnp.zeros(turn_ref.shape, jnp.float32)
+    tables = [[], []]
+    for x in range(CXL):
+        rest = jnp.concatenate([points_ref[c, x * LZ : (x + 1) * LZ, :] for c in range(3)], axis=0)
+        for part in range(PARTS):
+            rounded = rest.astype(jnp.bfloat16).astype(jnp.float32)
+            turn_ref[CHOICE * part : CHOICE * (part + 1), :] = rounded
+            rest = rest - rounded
+        turned = jnp.transpose(turn_ref[...]).astype(jnp.bfloat16)
+        for y in range(CYL):
+            tables[y].append(turned[PPL * y : PPL * (y + 1)])
+    tables = [jnp.concatenate(table, axis=0) for table in tables]
+    row = lax.broadcasted_iota(jnp.int32, (LANES, LANES), 0)
+    row = jnp.where(row < PARTS * CHOICE, row % CHOICE, -1)
     for z in range(LZ):
-        place_ref[z] = jnp.dot(split, choice_ref[z], preferred_element_type=jnp.float32)
+        chosen = jnp.concatenate(
+            [(row == c * LZ + z).astype(jnp.float32) for c in range(3)], axis=1
+        ).astype(jnp.bfloat16)
+        for y in range(CYL):
+            place_ref[y, z] = jnp.dot(tables[y], chosen, preferred_element_type=jnp.float32)
 
     def add_tiles(leaf, step):
         x = leaf // LZ
@@ -307,10 +386,10 @@
             start = pl.multiple_of(x * PPL + 8 * (STEP * step + u), 8)
             low, high = [
                 [
-                    place_ref[z, pl.ds(start, 8), LANES * (2 * c + y) : LANES * (2 * c + y + 1)]
+                    place_ref[y, z, pl.ds(start, 8), LANES * c : LANES * (c + 1)]
                     for c in range(3)
                 ]
-                for y in range(2)
+                for y in range(CYL)
             ]
             for place in (low, high):
                 place.append(square(place[0]) + square(place[1]) + square(place[2]))
@@ -374,20 +453,30 @@
     lax.fori_loop(0, LEAVES // 8, finish, 0)
 
 
-def near_sums(fill, sources, columns):
+def near_sums(fill, table):
     return pl.pallas_call(
         near_kernel,
-        out_shape=jax.ShapeDtypeStruct((LEAVES, LANES), jnp.float32),
-        in_specs=[pl.BlockSpec(memory_space=pltpu.SMEM)]
-        + [pl.BlockSpec(memory_space=pltpu.VMEM)] * 3,
-        out_specs=pl.BlockSpec(memory_space=pltpu.VMEM),
+        out_shape=(
+            jax.ShapeDtypeStruct((LEAVES, LANES), jnp.float32),
+            jax.ShapeDtypeStruct((4, LEAVES, LANES), jnp.float32),
+        ),
+        in_specs=[
+            pl.BlockSpec(memory_space=pltpu.SMEM),
+            pl.BlockSpec(memory_space=pltpu.VMEM),
+        ],
+        out_specs=(
+            pl.BlockSpec(memory_space=pltpu.VMEM),
+            pl.BlockSpec(memory_space=pltpu.VMEM),
+        ),
         scratch_shapes=[
+            pltpu.VMEM((2 * PLANES, (CXL + 2) * PAD_Z, LANES), jnp.float32),
             pltpu.VMEM((LEAVES, LANES, LANES), jnp.float32),
-            pltpu.VMEM((LZ, CXL * PPL, 3 * CYL * LANES), jnp.float32),
+            pltpu.VMEM((LANES, LANES), jnp.float32),
+            pltpu.VMEM((CYL, LZ, CXL * PPL, 3 * LANES), jnp.float32),
         ],
-        compiler_params=pltpu.CompilerParams(vmem_limit_bytes=20 * 2**20),
+        compiler_params=pltpu.CompilerParams(vmem_limit_bytes=28 * 2**20),
         name="near_sums",
-    )(fill, sources, columns, choices())
+    )(fill, table)
 
 
 def extended(cells, sides, width):
@@ -406,81 +495,19 @@
     return cells
 
 
-def live_charges(charges, counts):
-    size_x, size_y = (counts.shape[0], counts.shape[1])
-    filled = jnp.broadcast_to(counts[..., None], (size_x, size_y, LZ, PPL)).reshape(
-        size_x, size_y, SLOTS
-    )
-    within = jnp.arange(SLOTS, dtype=jnp.int32) % PPL
-    occupied = within[None, None, :] < filled
-    return (jnp.where(occupied, charges, 0.0), occupied)
-
-
-def placed(rows, start_x, start_y, start_z):
-    size_x, size_y = rows.shape[1:3]
-    along_x = (start_x + jnp.arange(size_x)).astype(jnp.float32)
-    along_y = (start_y + jnp.arange(size_y)).astype(jnp.float32)
-    along_z = (start_z + jnp.arange(SLOTS) // PPL).astype(jnp.float32)
-    return jnp.stack(
-        [
-            rows[0] + along_x[:, None, None],
-            rows[1] + along_y[None, :, None],
-            rows[2] + along_z[None, None, :],
-            rows[3],
-        ]
-    )
-
-
-def leaf_pairs(cells):
-    lead, size_x = cells.shape[:2]
-    split = cells.reshape(lead, size_x, 2, LZ, PPL).transpose(0, 1, 3, 2, 4)
-    return split.reshape(lead, size_x, LZ, LANES)
-
-
 def per_device(positions, charges, counts, up_ops, m2l_ops, down_ops, box_lists):
-    index_x = lax.axis_index("gx")
-    index_y = lax.axis_index("gy")
     devices_x = lax.axis_size("gx")
     devices_y = lax.axis_size("gy")
-    weights, occupied = live_charges(charges, counts)
-    local_rows = jnp.concatenate([positions, weights[None]], axis=0)
-    padded = extended(local_rows, (("gx", 1), ("gy", 2)), 1)
-
-    own = placed(local_rows, 0, 0, 0)
-    points = leaf_pairs(own).reshape(4, ROWS, LANES)
-    held = leaf_pairs(occupied.astype(jnp.float32)[None]).reshape(ROWS, LANES)
-    offsets = [devices_x * (devices_y - (devices_y >> h - 1)) for h in range(1, LEV + 1)]
-    meta = jnp.concatenate([jnp.stack([index_x, index_y])] + [box_lists[o] for o in offsets])
-    lattice = jnp.asarray(LATTICE, dtype=jnp.float32)
-    sy = jnp.concatenate(
-        [
-            ((index_y >> h) * CYL * 2**h - index_y * CYL).astype(jnp.float32)
-            + (0.5 * CYL * 2**h) * (1.0 + SURFACE_REACH * lattice)
-            for h in range(1, LEV + 1)
-        ]
+    filled = jnp.pad(counts.astype(jnp.float32), ((0, 0), (0, 0), (0, SLOTS - LZ)))
+    rows = jnp.concatenate([positions, charges[None], filled[None]], axis=0)
+    padded = extended(rows, (("gx", 1), ("gy", 2)), 1)
+    fill = counts.reshape(-1)
+    sent = send_panels(
+        box_lists, fill, positions, charges, up_ops, m2l_ops, down_ops, devices_x, devices_y
     )
-    sent = send_panels(meta, sy, points, up_ops, m2l_ops, down_ops, devices_x, devices_y)
     parts = lax.all_to_all(sent, ("gx", "gy"), split_axis=0, concat_axis=0, tiled=True)
-
-    around = placed(padded, -1 - CXL // 2, -1 - CYL // 2, -(LZ // 2))
-    norm = jnp.sum(square(around[:3]), axis=0, keepdims=True) + SOFTENING
-    planes = jnp.concatenate([-2.0 * around[:3], norm, around[3:]])
-    sides = [planes[:, :, 1:3], jnp.stack([planes[:, :, 0], planes[:, :, 3]], axis=2)]
-    sources = jnp.concatenate([leaf_pairs(side) for side in sides])
-    sources = jnp.pad(sources, ((0, 0), (0, 0), (1, 1), (0, 0)), constant_values=0.0)
-    beyond = jnp.pad(jnp.zeros((LZ,), jnp.float32), (1, 1), constant_values=1.0)
-    is_norm = (jnp.arange(2 * PLANES) % PLANES == 3).astype(jnp.float32)
-    sources = sources + is_norm[:, None, None, None] * beyond[None, None, :, None]
-    sources = sources.reshape(2 * PLANES, (CXL + 2) * PAD_Z, LANES)
-    columns = placed(local_rows, -(CXL // 2), -(CYL // 2), -(LZ // 2))[:3]
-    columns = columns.reshape(3, CXL, CYL, LZ, PPL).transpose(1, 4, 0, 2, 3)
-    columns = columns.reshape(CXL * PPL, COLUMNS)
-    columns = jnp.concatenate([columns] * 3 + [jnp.zeros((CXL * PPL, 2 * LANES - 3 * COLUMNS))], 1)
-    fill = counts.reshape(-1)
-    near = near_sums(fill, sources, columns)
-    total = far_and_sum(sy, points, held, near, parts)
-    total = total.reshape(CXL, LZ, CYL, PPL).transpose(0, 2, 1, 3)
-    return total.reshape(CXL, CYL, SLOTS)
+    near, points = near_sums(fill, padded.transpose(2, 0, 1, 3))
+    return far_and_sum(points, near, parts)
 
 
 def solution(mesh):

time: 116 us -> 89.4 us (0.77)
  the two profiles are of different devices: /device:TPU:1 before, /device:TPU:107 now
where the time goes in v3:
time: 89.4 us; the launch traced here: 89.1 us
  Pallas kernels  47.4 us (53%)
  starting transfers between devices  25.4 us (28%)
  local copies, waits for them, and re-layouts  7.76 us (9%)
  waiting for transfers between devices  7.33 us (8%)
  other arithmetic  1 us (1%)
    pallas_call x1, Pallas kernels, near_sums(): pl.pallas_call(near_kernel, out_shape=(jax.ShapeDtypeStruct((LEAVES, LANE...  28.5 us
    all_to_all x1, starting transfers between devices, per_device(): lax.all_to_all(sent, ('gx', 'gy'), split_axis=0, concat_axis=0, tiled=True)  15.7 us
    pallas_call x1, Pallas kernels, send_panels(): pl.pallas_call(functools.partial(send_kernel, span_x, span_y), out_shape=...  15.1 us
    ppermute x2, starting transfers between devices, extended(): outside = lax.ppermute(jnp.where(even, head, tail), axis, second)  7.71 us
    ppermute x2, waiting for transfers between devices, extended(): outside = lax.ppermute(jnp.where(even, head, tail), axis, second)  7.32 us
    unnamed x10, local copies, waits for them, and re-layouts  6.2 us
    pallas_call x1, Pallas kernels, far_and_sum(): pl.pallas_call(far_kernel, out_shape=jax.ShapeDtypeStruct((CXL, CYL, SLOT...  3.79 us
    ppermute x2, starting transfers between devices, extended(): inside = lax.ppermute(jnp.where(even, tail, head), axis, first)  2.02 us
  transfers between devices with their start and end apart: 5, of which 1 were waited for; matrix products, arithmetic and copies ran while one was open for 2% of the time, Pallas kernels for 49%

profile of v3, /device:TPU:107, one launch (start us, length us, event | category | flops | bytes accessed | tf_op | source)
XLA Modules:
  0.0 89.1 jit_solution(8867726381060714880)
XLA Ops:
  0.0 0.7 copy_convert_fusion
  0.7 0.9 %copy.10 = f32[3,8,2,512]{3,1,0,2:T(8,128)S(1)} copy(f32[3,8,2,512]{3,2,1,0:T(2,128)} %positions_ref.1) | data formatting | bytes 196608 | tf_op args[0]
  1.6 0.8 copy_bitcast_fusion
  2.5 1.9 %collective-permute-start.1 = (f32[5,1,2,512]{3,1,0,2:T(1,128)S(1)}, f32[5,1,2,512]{3,1,0,2:T(1,128)S(1)}, u32[]{:S(2)}, u32[]{:S(2)}) collective-permute-start(f32[5,1,2,512]{3,1,0,2:T(1,128)S(1)} %broadcast_select_fusion.4), channel_id=1, source_target_pairs={{0,32},{32,0},{64,96},{96,64},{128,160},{160,128},{192,224},{224,1... | collective-permute-start | bytes 61448 | tf_op jit(solution)/shard_map/ppermute | solution.py:490
  4.4 2.9 %collective-permute-start = (f32[5,1,2,512]{3,1,0,2:T(1,128)S(1)}, f32[5,1,2,512]{3,1,0,2:T(1,128)S(1)}, u32[]{:S(2)}, u32[]{:S(2)}) collective-permute-start(f32[5,1,2,512]{3,1,0,2:T(1,128)S(1)} %get-tuple-element.9), channel_id=1, source_target_pairs={{32,64},{64,32},{96,128},{128,96},{160,192},{192,160},{33,65},{65,... | collective-permute-start | bytes 61448 | tf_op jit(solution)/shard_map/ppermute | solution.py:491
  7.3 0.8 reshape.3.fill_ref.counts_ref
  8.1 0.8 copy.11.lists_ref
  8.9 0.0 copy-start
  8.9 1.5 %copy-done = f32[2,2,296,296]{3,2,1,0:T(8,128)S(1)} copy-done((f32[2,2,296,296]{3,2,1,0:T(8,128)S(1)}, f32[2,2,296,296]{3,2,1,0:T(8,128)}, u32[]{:S(2)}) %copy-start) | copy-done | bytes 1401880
  10.4 0.0 copy-start.1
  10.4 1.3 %copy-done.1 = f32[3,296,296]{2,1,0:T(8,128)S(1)} copy-done((f32[3,296,296]{2,1,0:T(8,128)S(1)}, f32[3,296,296]{2,1,0:T(8,128)}, u32[]{:S(2)}) %copy-start.1) | copy-done | bytes 1051416
  11.8 0.0 copy-start.2
  11.8 0.9 copy-done.2
  12.7 0.0 copy-start.3
  12.7 0.8 copy-done.3
  13.4 15.1 %send_panels.1 = f32[256,1,296]{2,1,0:T(1,128)} custom-call(s32[224,8]{1,0:T(8,128)S(1)} %copy.11.lists_ref, s32[128]{0:T(128)S(1)} %reshape.3.fill_ref.counts_ref, f32[3,8,2,512]{3,2,1,0:T(2,128)S(1)} %copy-done.2, f32[8,2,512]{2,1,0:T(2,128)S(1)} %copy-done.3, f32[3,296,296]{2,1,0:T(8,128)S(1)} %copy-done.1, f32[3,8,296,296]{3,2,1,0:T(8,128)} %m2l_hbm.1, ...), custom_call_target="tpu_custom_call" | custom-call | tf_op jit(solution)/shard_map/send_panels/pallas_call | solution.py:222
  28.5 15.7 %all-to-all-start = ((f32[256,1,296]{2,1,0:T(1,128)}), f32[256,1,296]{2,1,0:T(1,128)S(1)}, u32[]{:S(2)}, u32[]{:S(2)}) async-start(f32[256,1,296]{2,1,0:T(1,128)} %send_panels.1), calls=%async_computation | async-start | bytes 786432 | tf_op jit(solution)/shard_map/all_to_all | solution.py:508
  44.2 0.0 collective-permute-done.1
  44.2 0.0 collective-permute-done
  44.3 0.1 pad_maximum_fusion
  44.4 4.8 %collective-permute-start.2 = (f32[5,10,1,512]{3,1,0,2:T(8,128)S(1)}, f32[5,10,1,512]{3,1,0,2:T(8,128)S(1)}, u32[]{:S(2)}, u32[]{:S(2)}) collective-permute-start(f32[5,10,1,512]{3,1,0,2:T(8,128)S(1)} %get-tuple-element.14), channel_id=1, source_target_pairs={{1,2},{2,1},{3,4},{4,3},{5,6},{6,5},{7,8},{8,7},{9,10},{10,9},{11,... | collective-permute-start | bytes 307208 | tf_op jit(solution)/shard_map/ppermute | solution.py:491
  49.2 0.1 collective-permute-start.3
  49.3 7.3 %collective-permute-done.2 = f32[5,10,1,512]{3,1,0,2:T(8,128)S(1)} collective-permute-done((f32[5,10,1,512]{3,1,0,2:T(8,128)S(1)}, f32[5,10,1,512]{3,1,0,2:T(8,128)S(1)}, u32[]{:S(2)}, u32[]{:S(2)}) %collective-permute-start.2) | collective-permute-done | bytes 102432 | tf_op jit(solution)/shard_map/ppermute | solution.py:491
  56.6 0.0 collective-permute-done.3
  56.6 0.1 maximum_bitcast_fusion.table_ref
  56.7 28.5 %near_sums.1 = (f32[64,128]{1,0:T(8,128)S(1)}, f32[4,64,128]{2,1,0:T(8,128)S(1)}) custom-call(s32[128]{0:T(128)S(1)} %reshape.3.fill_ref.counts_ref, f32[4,5,10,512]{3,2,1,0:T(8,128)S(1)} %maximum_bitcast_fusion.table_ref), custom_call_target="tpu_custom_call" | custom-call | tf_op jit(solution)/shard_map/near_sums/pallas_call | solution.py:457
  85.3 0.0 all-to-all-done.parts_ref
  85.3 3.8 %far_and_sum.1 = f32[8,2,512]{2,1,0:T(2,128)} custom-call(f32[4,64,128]{2,1,0:T(8,128)S(1)} %get-tuple-element.7.points_ref, f32[64,128]{1,0:T(8,128)S(1)} %get-tuple-element.8.near_ref, f32[256,1,296]{2,1,0:T(1,128)S(1)} %all-to-all-done.parts_ref), custom_call_target="tpu_custom_call" | custom-call | tf_op jit(solution)/shard_map/far_and_sum/pallas_call | solution.py:292
  (5 shorter events, 0.1 us)
Async XLA Ops:
  2.5 41.7 %collective-permute-start.1 = (f32[5,1,2,512]{3,1,0,2:T(1,128)S(1)}, f32[5,1,2,512]{3,1,0,2:T(1,128)S(1)}, u32[]{:S(2)}, u32[]{:S(2)}) collective-permute-start(f32[5,1,2,512]{3,1,0,2:T(1,128)S(1)} %broadcast_select_fusion.4), channel_id=1, source_target_pairs={{0,32},{32,0},{64,96},{96,64},{128,160},{160,128},{192,224},{224,1... | collective-permute-start | bytes 61448 | tf_op jit(solution)/shard_map/ppermute | solution.py:490
  4.4 39.8 %collective-permute-start = (f32[5,1,2,512]{3,1,0,2:T(1,128)S(1)}, f32[5,1,2,512]{3,1,0,2:T(1,128)S(1)}, u32[]{:S(2)}, u32[]{:S(2)}) collective-permute-start(f32[5,1,2,512]{3,1,0,2:T(1,128)S(1)} %get-tuple-element.9), channel_id=1, source_target_pairs={{32,64},{64,32},{96,128},{128,96},{160,192},{192,160},{33,65},{65,... | collective-permute-start | bytes 61448 | tf_op jit(solution)/shard_map/ppermute | solution.py:491
  8.9 1.5 %copy-start = (f32[2,2,296,296]{3,2,1,0:T(8,128)S(1)}, f32[2,2,296,296]{3,2,1,0:T(8,128)}, u32[]{:S(2)}) copy-start(f32[2,2,296,296]{3,2,1,0:T(8,128)} %down_hbm.1) | copy-start | bytes 4205572
  10.4 1.3 %copy-start.1 = (f32[3,296,296]{2,1,0:T(8,128)S(1)}, f32[3,296,296]{2,1,0:T(8,128)}, u32[]{:S(2)}) copy-start(f32[3,296,296]{2,1,0:T(8,128)} %up_hbm.1) | copy-start | bytes 3154180
  11.8 0.9 %copy-start.2 = (f32[3,8,2,512]{3,2,1,0:T(2,128)S(1)}, f32[3,8,2,512]{3,2,1,0:T(2,128)}, u32[]{:S(2)}) copy-start(f32[3,8,2,512]{3,2,1,0:T(2,128)} %positions_ref.1) | copy-start | bytes 294916
  12.7 0.8 copy-start.3
  28.5 56.8 %all-to-all-start = ((f32[256,1,296]{2,1,0:T(1,128)}), f32[256,1,296]{2,1,0:T(1,128)S(1)}, u32[]{:S(2)}, u32[]{:S(2)}) async-start(f32[256,1,296]{2,1,0:T(1,128)} %send_panels.1), calls=%async_computation | async-start | bytes 786432 | tf_op jit(solution)/shard_map/all_to_all | solution.py:508
  44.4 12.2 %collective-permute-start.2 = (f32[5,10,1,512]{3,1,0,2:T(8,128)S(1)}, f32[5,10,1,512]{3,1,0,2:T(8,128)S(1)}, u32[]{:S(2)}, u32[]{:S(2)}) collective-permute-start(f32[5,10,1,512]{3,1,0,2:T(8,128)S(1)} %get-tuple-element.14), channel_id=1, source_target_pairs={{1,2},{2,1},{3,4},{4,3},{5,6},{6,5},{7,8},{8,7},{9,10},{10,9},{11,... | collective-permute-start | bytes 307208 | tf_op jit(solution)/shard_map/ppermute | solution.py:491
  49.2 7.4 %collective-permute-start.3 = (f32[5,10,1,512]{3,1,0,2:T(8,128)S(1)}, f32[5,10,1,512]{3,1,0,2:T(8,128)S(1)}, u32[]{:S(2)}, u32[]{:S(2)}) collective-permute-start(f32[5,10,1,512]{3,1,0,2:T(8,128)S(1)} %get-tuple-element.15), channel_id=1, source_target_pairs={{0,1},{1,0},{2,3},{3,2},{4,5},{5,4},{6,7},{7,6},{8,9},{9,8},{10,11... | collective-permute-start | bytes 307208 | tf_op jit(solution)/shard_map/ppermute | solution.py:490

commit v4 on v3

--- a/solution.py
+++ b/solution.py
@@ -17,6 +17,7 @@
 NE = 296
 SLOTS = LZ * PPL
 LANES = 128
+GRANT = 58
 ROWS = CXL * CYL * SLOTS // LANES
 SOFTENING = 0.01
 SURFACE_REACH = 1.05
@@ -99,8 +100,70 @@
     return [wide(p_ref[c, pl.ds(r, 1), :]) for c in range(p_ref.shape[0])]
 
 
+def fill_points(own_ref, p_ref):
+    lane = lax.broadcasted_iota(jnp.int32, (CXL, LANES), 1)
+    upper = lane // PPL
+    slot = (lane % PPL).astype(jnp.float32)
+    along_x = lax.broadcasted_iota(jnp.int32, (CXL, LANES), 0) - CXL // 2
+    for y in range(CYL):
+        for q in range(SLOTS // LANES):
+            here = slice(LANES * q, LANES * (q + 1))
+            rows = slice(CXL * (4 * y + q), CXL * (4 * y + q + 1))
+            place_z = (upper + (2 * q - LZ // 2)).astype(jnp.float32)
+            p_ref[0, rows, :] = own_ref[y, 0, :, here] + along_x.astype(jnp.float32)
+            p_ref[1, rows, :] = own_ref[y, 1, :, here] + float(y - CYL // 2)
+            p_ref[2, rows, :] = own_ref[y, 2, :, here] + place_z
+            held = [
+                jnp.broadcast_to(own_ref[y, 4, :, z : z + 1], (CXL, LANES))
+                for z in (2 * q, 2 * q + 1)
+            ]
+            held = jnp.where(upper == 0, held[0], held[1])
+            p_ref[3, rows, :] = jnp.where(slot < held, own_ref[y, 3, :, here], 0.0)
+
+
+def add_checks(levels, p_ref, check_ref):
+    for n, h in enumerate(levels):
+        ys = lattice_y(h)
+        for squares, tiles in ((a_squares, A_TILES), (bc_squares, B_TILES + C_TILES)):
+
+            def gather(r, sums):
+                x8, y8, z8, w8 = row_of(p_ref, r)
+                y_parts = [square(ys[b] - y8) for b in range(P_ORD)]
+                return [
+                    total + w8 * lax.rsqrt(d2)
+                    for total, d2 in zip(sums, squares(x8, z8, y_parts))
+                ]
+
+            sums = lax.fori_loop(
+                0, ROWS, gather, [jnp.zeros((8, LANES), jnp.float32) for _ in tiles], unroll=2
+            )
+            for i, (total, tile) in enumerate(zip(sums, tiles)):
+                filled = jnp.broadcast_to(jnp.sum(total, axis=1, keepdims=True), (8, LANES))
+                if squares is bc_squares and i >= len(B_TILES):
+                    check_ref[n, strided_rows(*tile), :] = filled[1:7]
+                else:
+                    check_ref[n, pl.ds(first_row(*tile), 8), :] = filled
+
+
+def check_kernel(h, own_ref, check_ref, p_ref):
+    fill_points(own_ref, p_ref)
+    add_checks([h], p_ref, check_ref)
+
+
+def one_check(h, own):
+    return pl.pallas_call(
+        functools.partial(check_kernel, h),
+        out_shape=jax.ShapeDtypeStruct((1, NE, LANES), jnp.float32),
+        in_specs=[pl.BlockSpec(memory_space=pltpu.VMEM)],
+        out_specs=pl.BlockSpec(memory_space=pltpu.VMEM),
+        scratch_shapes=[pltpu.VMEM((4, ROWS, LANES), jnp.float32)],
+        compiler_params=pltpu.CompilerParams(vmem_limit_bytes=4 * 2**20),
+        name="one_check",
+    )(own)
+
+
 def send_kernel(
-    span_x, span_y, lists_ref, counts_ref, positions_ref, charges_ref, up_hbm, m2l_hbm, down_hbm,
+    span_x, span_y, lists_ref, first_ref, second_ref, own_ref, up_hbm, m2l_hbm, down_hbm,
     out_ref, p_ref, up_ref, m2l_ref, down_ref, check_ref, row_ref, column_ref, panel_ref, sems,
 ):
     copies = [pltpu.make_async_copy(up_hbm, up_ref, sems.at[0])]
@@ -111,57 +174,15 @@
     for copy in copies:
         copy.start()
     row_ref[...] = jnp.zeros((8, 384), jnp.float32)
-    lane = lax.broadcasted_iota(jnp.int32, (CYL, LANES), 1)
-    upper = lane // PPL
-    slot = lane % PPL
-    along_y = lax.broadcasted_iota(jnp.int32, (CYL, LANES), 0)
-    for x in range(CXL):
-        for q in range(SLOTS // LANES):
-            here = slice(LANES * q, LANES * (q + 1))
-            rows = slice(8 * x + CYL * q, 8 * x + CYL * (q + 1))
-            place_z = (upper + (2 * q - LZ // 2)).astype(jnp.float32)
-            p_ref[0, rows, :] = positions_ref[0, x, :, here] + float(x - CXL // 2)
-            p_ref[1, rows, :] = positions_ref[1, x, :, here] + (along_y - 1).astype(jnp.float32)
-            p_ref[2, rows, :] = positions_ref[2, x, :, here] + place_z
-            held = [
-                jnp.where(
-                    upper == 0,
-                    counts_ref[(x * CYL + y) * LZ + 2 * q],
-                    counts_ref[(x * CYL + y) * LZ + 2 * q + 1],
-                )
-                for y in range(CYL)
-            ]
-            held = jnp.where(along_y == 0, held[0], held[1])
-            p_ref[3, rows, :] = jnp.where(slot < held, charges_ref[x, :, here], 0.0)
-
-    for h in range(LEV):
-        ys = lattice_y(h + 1)
-        for squares, tiles in ((a_squares, A_TILES), (bc_squares, B_TILES + C_TILES)):
-
-            def gather(r, sums):
-                x8, y8, z8, w8 = row_of(p_ref, r)
-                y_parts = [square(ys[b] - y8) for b in range(P_ORD)]
-                return [
-                    total + w8 * lax.rsqrt(d2)
-                    for total, d2 in zip(sums, squares(x8, z8, y_parts))
-                ]
-
-            sums = lax.fori_loop(
-                0, ROWS, gather, [jnp.zeros((8, LANES), jnp.float32) for _ in tiles], unroll=2
-            )
-            for n, (total, tile) in enumerate(zip(sums, tiles)):
-                filled = jnp.broadcast_to(jnp.sum(total, axis=1, keepdims=True), (8, LANES))
-                if squares is bc_squares and n >= len(B_TILES):
-                    check_ref[h, strided_rows(*tile), :] = filled[1:7]
-                else:
-                    check_ref[h, pl.ds(first_row(*tile), 8), :] = filled
-
+    fill_points(own_ref, p_ref)
+    add_checks([LEV], p_ref, check_ref)
     copies[0].wait()
     for h in range(LEV):
         for low, high in CHUNKS:
             total = jnp.zeros((8, high - low), jnp.float32)
             for i in range(0, NE, 8):
-                total += check_ref[h, i : i + 8, : high - low] * up_ref[h, i : i + 8, low:high]
+                check = (first_ref, second_ref, check_ref)[h][0, i : i + 8, : high - low]
+                total += check * up_ref[h, i : i + 8, low:high]
             row_ref[h : h + 1, low:high] = jnp.sum(total, axis=0, keepdims=True)
     flipped = jnp.transpose(row_ref[...])
     for h in range(LEV):
@@ -207,7 +228,7 @@
         bits = across.bit_length() - 1
         own_box = (index_x << bits) + (index_y >> h)
         for k in range(K):
-            box = (own_box - lists_ref[offset, k]) & (span_x * across - 1)
+            box = (own_box - lists_ref[k, offset]) & (span_x * across - 1)
             first = (box >> bits) * span_y + ((box & (across - 1)) << h)
             for j in range(2**h):
                 if h == 1:
@@ -218,13 +239,13 @@
                 out_ref[first + j] += value
 
 
-def send_panels(lists, counts, positions, charges, up_ops, m2l_ops, down_ops, span_x, span_y):
+def send_panels(lists, first, second, own, up_ops, m2l_ops, down_ops, span_x, span_y):
     return pl.pallas_call(
         functools.partial(send_kernel, span_x, span_y),
         out_shape=jax.ShapeDtypeStruct((span_x * span_y, 1, NE), jnp.float32),
         in_specs=[
             pl.BlockSpec(memory_space=pltpu.SMEM),
-            pl.BlockSpec(memory_space=pltpu.SMEM),
+            pl.BlockSpec(memory_space=pltpu.VMEM),
             pl.BlockSpec(memory_space=pltpu.VMEM),
             pl.BlockSpec(memory_space=pltpu.VMEM),
             pl.BlockSpec(memory_space=pltpu.HBM),
@@ -237,15 +258,15 @@
             pltpu.VMEM((LEV, NE, NE), jnp.float32),
             pltpu.VMEM((LEV, K, NE, NE), jnp.float32),
             pltpu.VMEM((LEV - 1, 2, NE, NE), jnp.float32),
-            pltpu.VMEM((LEV, NE, LANES), jnp.float32),
+            pltpu.VMEM((1, NE, LANES), jnp.float32),
             pltpu.VMEM((8, 384), jnp.float32),
             pltpu.VMEM((LEV, NE, LANES), jnp.float32),
             pltpu.VMEM((LEV, K, 8, NE), jnp.float32),
             pltpu.SemaphoreType.DMA((LEV + 2,)),
         ],
-        compiler_params=pltpu.CompilerParams(vmem_limit_bytes=46 * 2**20),
+        compiler_params=pltpu.CompilerParams(vmem_limit_bytes=GRANT * 2**20),
         name="send_panels",
-    )(lists, counts, positions, charges, up_ops, m2l_ops, down_ops)
+    )(lists, first, second, own, up_ops, m2l_ops, down_ops)
 
 
 def far_kernel(points_ref, near_ref, parts_ref, out_ref, row_ref, column_ref, tile_ref):
@@ -422,7 +443,7 @@
     def one_leaf_pair(leaf, carry):
         x = leaf // LZ
         z = leaf % LZ
-        held = jnp.maximum(fill_ref[x * 2 * LZ + z], fill_ref[(x * 2 + 1) * LZ + z])
+        held = jnp.maximum(fill_ref[x, 0, z], fill_ref[x, 1, z])
 
         def more(step, inner):
             add_tiles(leaf, step)
@@ -479,34 +500,33 @@
     )(fill, table)
 
 
-def extended(cells, sides, width):
-    for axis, dim in sides:
-        count = lax.axis_size(axis)
-        even = lax.axis_index(axis) % 2 == 0
-        head = lax.slice_in_dim(cells, 0, width, axis=dim)
-        tail = lax.slice_in_dim(cells, cells.shape[dim] - width, cells.shape[dim], axis=dim)
-        first = [(i, i ^ 1) for i in range(count)]
-        second = [(i, i + 1 if i % 2 else i - 1) for i in range(1, count - 1)]
-        inside = lax.ppermute(jnp.where(even, tail, head), axis, first)
-        outside = lax.ppermute(jnp.where(even, head, tail), axis, second)
-        cells = jnp.concatenate(
-            [jnp.where(even, outside, inside), cells, jnp.where(even, inside, outside)], axis=dim
-        )
-    return cells
+def swapped(axis, head, tail):
+    count = lax.axis_size(axis)
+    even = lax.axis_index(axis) & 1 == 0
+    first = [(i, i ^ 1) for i in range(count)]
+    second = [(i, i + 1 if i % 2 else i - 1) for i in range(1, count - 1)]
+    outside = lax.ppermute(jnp.where(even, head, tail), axis, second)
+    inside = lax.ppermute(jnp.where(even, tail, head), axis, first)
+    return jnp.where(even, outside, inside), jnp.where(even, inside, outside)
 
 
 def per_device(positions, charges, counts, up_ops, m2l_ops, down_ops, box_lists):
     devices_x = lax.axis_size("gx")
     devices_y = lax.axis_size("gy")
     filled = jnp.pad(counts.astype(jnp.float32), ((0, 0), (0, 0), (0, SLOTS - LZ)))
-    rows = jnp.concatenate([positions, charges[None], filled[None]], axis=0)
-    padded = extended(rows, (("gx", 1), ("gy", 2)), 1)
-    fill = counts.reshape(-1)
+    own = jnp.concatenate([positions, charges[None], filled[None]], axis=0).transpose(2, 0, 1, 3)
+    before, after = swapped("gx", own[:, :, :1], own[:, :, -1:])
+    first = one_check(1, own)
+    middle = jnp.concatenate([before, own, after], axis=2)
+    middle, first, own = lax.optimization_barrier((middle, first, own))
+    below, above = swapped("gy", middle[:1], middle[1:])
+    second = one_check(2, own)
+    below, above, second, own = lax.optimization_barrier((below, above, second, own))
     sent = send_panels(
-        box_lists, fill, positions, charges, up_ops, m2l_ops, down_ops, devices_x, devices_y
+        box_lists.T, first, second, own, up_ops, m2l_ops, down_ops, devices_x, devices_y
     )
     parts = lax.all_to_all(sent, ("gx", "gy"), split_axis=0, concat_axis=0, tiled=True)
-    near, points = near_sums(fill, padded.transpose(2, 0, 1, 3))
+    near, points = near_sums(counts, jnp.concatenate([below, middle, above], axis=0))
     return far_and_sum(points, near, parts)
 
 

time: 89.4 us -> 76.4 us (0.85)
  the two profiles are of different devices: /device:TPU:107 before, /device:TPU:1 now
where the time goes in v4:
time: 76.4 us; the launch traced here: 75 us
  Pallas kernels  44.5 us (58%)
  starting transfers between devices  26 us (34%)
  local copies, waits for them, and re-layouts  3.02 us (4%)
  other arithmetic  0.93 us (1%)
    pallas_call x1, Pallas kernels, near_sums(): pl.pallas_call(near_kernel, out_shape=(jax.ShapeDtypeStruct((LEAVES, LANE...  26.9 us
    all_to_all x1, starting transfers between devices, per_device(): lax.all_to_all(sent, ('gx', 'gy'), split_axis=0, concat_axis=0, tiled=True)  14.9 us
    pallas_call x1, Pallas kernels, send_panels(): pl.pallas_call(functools.partial(send_kernel, span_x, span_y), out_shape=...  8.15 us
    ppermute x2, starting transfers between devices, swapped(): inside = lax.ppermute(jnp.where(even, tail, head), axis, first)  6.24 us
    pallas_call x2, Pallas kernels, one_check(): pl.pallas_call(functools.partial(check_kernel, h), out_shape=jax.ShapeDty...  5.64 us
    ppermute x2, starting transfers between devices, swapped(): outside = lax.ppermute(jnp.where(even, head, tail), axis, second)  4.9 us
    pallas_call x1, Pallas kernels, far_and_sum(): pl.pallas_call(far_kernel, out_shape=jax.ShapeDtypeStruct((CXL, CYL, SLOT...  3.79 us
    unnamed x9, local copies, waits for them, and re-layouts  2.24 us
  transfers between devices with their start and end apart: 5, of which 1 were waited for; matrix products, arithmetic and copies ran while one was open for 0% of the time, Pallas kernels for 43%

profile of v4, /device:TPU:1, one launch (start us, length us, event | category | flops | bytes accessed | tf_op | source)
XLA Modules:
  0.0 75.0 jit_solution(4444125886615730395)
XLA Ops:
  0.0 0.7 copy_convert_fusion
  0.7 0.9 %copy.10 = f32[3,8,2,512]{3,1,0,2:T(8,128)S(1)} copy(f32[3,8,2,512]{3,2,1,0:T(2,128)} %param.7) | data formatting | bytes 196608 | tf_op args[0]
  1.6 0.8 %copy_bitcast_fusion = (f32[1,8,2,512]{3,1,0,2:T(8,128)S(1)}, f32[1,8,2,512]{3,1,0,2:T(8,128)S(1)}) fusion(f32[8,2,512]{2,1,0:T(2,128)} %param.8, f32[8,2,8]{2,0,1:T(8,128)S(1)} %copy_convert_fusion), kind=kLoop, calls=%fused_computation.11 | loop fusion | bytes 98816 | tf_op jit(solution)/shard_map/broadcast_in_dim | solution.py:517
  2.4 0.0 copy-start
  2.5 0.7 collective-permute-start
  3.1 6.1 %collective-permute-start.1 = (f32[2,5,1,512]{3,2,1,0:T(1,128)S(1)}, f32[2,5,1,512]{3,2,1,0:T(1,128)S(1)}, u32[]{:S(2)}, u32[]{:S(2)}) collective-permute-start(f32[2,5,1,512]{3,2,1,0:T(1,128)S(1)} %get-tuple-element.28), channel_id=1, source_target_pairs={{0,32},{32,0},{64,96},{96,64},{128,160},{160,128},{192,224},{224,1... | collective-permute-start | bytes 61448 | tf_op jit(solution)/shard_map/ppermute | solution.py:509
  9.3 2.8 %one_check.2.first_ref = f32[1,296,128]{2,1,0:T(8,128)S(1)} custom-call(f32[2,5,8,512]{3,2,1,0:T(8,128)S(1)} %maximum_bitcast_fusion.own_ref), custom_call_target="tpu_custom_call" | custom-call | tf_op jit(solution)/shard_map/one_check/pallas_call | solution.py:154
  12.1 0.0 copy-start.1
  12.1 0.7 copy-done.1
  12.8 0.0 collective-permute-done
  12.8 0.0 collective-permute-done.1
  12.8 0.1 pad_maximum_fusion.1
  12.9 4.2 %collective-permute-start.2 = (f32[1,5,10,512]{3,2,1,0:T(8,128)S(1)}, f32[1,5,10,512]{3,2,1,0:T(8,128)S(1)}, u32[]{:S(2)}, u32[]{:S(2)}) collective-permute-start(f32[1,5,10,512]{3,2,1,0:T(8,128)S(1)} %get-tuple-element.26), channel_id=1, source_target_pairs={{1,2},{2,1},{3,4},{4,3},{5,6},{6,5},{7,8},{8,7},{9,10},{10,9},{11,... | collective-permute-start | bytes 307208 | tf_op jit(solution)/shard_map/ppermute | solution.py:508
  17.2 0.1 collective-permute-start.3
  17.3 2.8 %one_check.3.second_ref = f32[1,296,128]{2,1,0:T(8,128)S(1)} custom-call(f32[2,5,8,512]{3,2,1,0:T(8,128)S(1)} %maximum_bitcast_fusion.own_ref), custom_call_target="tpu_custom_call" | custom-call | tf_op jit(solution)/shard_map/one_check/pallas_call | solution.py:154
  20.1 0.0 copy-start.2
  20.1 0.7 copy-done.2
  20.8 0.4 collective-permute-done.2
  21.2 0.0 collective-permute-done.3
  21.2 0.0 copy-done
  21.2 8.2 %send_panels.1 = f32[256,1,296]{2,1,0:T(1,128)} custom-call(s32[8,224]{1,0:T(8,128)} %bitcast.7, f32[1,296,128]{2,1,0:T(8,128)} %copy-done.1, f32[1,296,128]{2,1,0:T(8,128)} %copy-done.2, f32[2,5,8,512]{3,2,1,0:T(8,128)} %copy-done, f32[3,296,296]{2,1,0:T(8,128)} %up_hbm.1, f32[3,8,296,296]{3,2,1,0:T(8,128)} %m2l_hbm.1, f32[2,2,296,296]{3,2,1,0:T(8,128)} %down_hbm.1), custom_call_target="tpu_custom_call" | custom-call | tf_op jit(solution)/shard_map/send_panels/pallas_call | solution.py:243
  29.4 0.0 copy-start.3
  29.4 14.9 %all-to-all-start = ((f32[256,1,296]{2,1,0:T(1,128)}), f32[256,1,296]{2,1,0:T(1,128)S(1)}, u32[]{:S(2)}, u32[]{:S(2)}) async-start(f32[256,1,296]{2,1,0:T(1,128)} %send_panels.1), calls=%async_computation | async-start | bytes 786432 | tf_op jit(solution)/shard_map/all_to_all | solution.py:528
  44.3 0.0 copy-done.3
  44.3 26.9 %near_sums.1 = (f32[64,128]{1,0:T(8,128)S(1)}, f32[4,64,128]{2,1,0:T(8,128)S(1)}) custom-call(s32[8,2,8]{2,1,0:T(2,128)S(1)} %copy-done.3, f32[4,5,10,512]{3,2,1,0:T(8,128)S(1)} %pad_maximum_fusion.table_ref), custom_call_target="tpu_custom_call" | custom-call | tf_op jit(solution)/shard_map/near_sums/pallas_call | solution.py:478
  71.2 0.0 all-to-all-done.parts_ref
  71.2 3.8 %far_and_sum.1 = f32[8,2,512]{2,1,0:T(2,128)} custom-call(f32[4,64,128]{2,1,0:T(8,128)S(1)} %get-tuple-element.18.points_ref, f32[64,128]{1,0:T(8,128)S(1)} %get-tuple-element.19.near_ref, f32[256,1,296]{2,1,0:T(1,128)S(1)} %all-to-all-done.parts_ref), custom_call_target="tpu_custom_call" | custom-call | tf_op jit(solution)/shard_map/far_and_sum/pallas_call | solution.py:313
  (6 shorter events, 0.2 us)
Async XLA Ops:
  2.4 18.8 %copy-start = (f32[2,5,8,512]{3,2,1,0:T(8,128)}, f32[2,5,8,512]{3,2,1,0:T(8,128)S(1)}, u32[]{:S(2)}) copy-start(f32[2,5,8,512]{3,2,1,0:T(8,128)S(1)} %maximum_bitcast_fusion.own_ref) | copy-start | bytes 491524
  2.5 10.3 %collective-permute-start = (f32[2,5,1,512]{3,2,1,0:T(1,128)S(1)}, f32[2,5,1,512]{3,2,1,0:T(1,128)S(1)}, u32[]{:S(2)}, u32[]{:S(2)}) collective-permute-start(f32[2,5,1,512]{3,2,1,0:T(1,128)S(1)} %get-tuple-element.27), channel_id=1, source_target_pairs={{32,64},{64,32},{96,128},{128,96},{160,192},{192,160},{33,65},{65,... | collective-permute-start | bytes 61448 | tf_op jit(solution)/shard_map/ppermute | solution.py:508
  3.1 9.6 %collective-permute-start.1 = (f32[2,5,1,512]{3,2,1,0:T(1,128)S(1)}, f32[2,5,1,512]{3,2,1,0:T(1,128)S(1)}, u32[]{:S(2)}, u32[]{:S(2)}) collective-permute-start(f32[2,5,1,512]{3,2,1,0:T(1,128)S(1)} %get-tuple-element.28), channel_id=1, source_target_pairs={{0,32},{32,0},{64,96},{96,64},{128,160},{160,128},{192,224},{224,1... | collective-permute-start | bytes 61448 | tf_op jit(solution)/shard_map/ppermute | solution.py:509
  12.1 0.7 copy-start.1
  12.9 8.2 %collective-permute-start.2 = (f32[1,5,10,512]{3,2,1,0:T(8,128)S(1)}, f32[1,5,10,512]{3,2,1,0:T(8,128)S(1)}, u32[]{:S(2)}, u32[]{:S(2)}) collective-permute-start(f32[1,5,10,512]{3,2,1,0:T(8,128)S(1)} %get-tuple-element.26), channel_id=1, source_target_pairs={{1,2},{2,1},{3,4},{4,3},{5,6},{6,5},{7,8},{8,7},{9,10},{10,9},{11,... | collective-permute-start | bytes 307208 | tf_op jit(solution)/shard_map/ppermute | solution.py:508
  17.2 4.0 %collective-permute-start.3 = (f32[1,5,10,512]{3,2,1,0:T(8,128)S(1)}, f32[1,5,10,512]{3,2,1,0:T(8,128)S(1)}, u32[]{:S(2)}, u32[]{:S(2)}) collective-permute-start(f32[1,5,10,512]{3,2,1,0:T(8,128)S(1)} %get-tuple-element.25), channel_id=1, source_target_pairs={{0,1},{1,0},{2,3},{3,2},{4,5},{5,4},{6,7},{7,6},{8,9},{9,8},{10,11... | collective-permute-start | bytes 307208 | tf_op jit(solution)/shard_map/ppermute | solution.py:509
  20.1 0.7 copy-start.2
  29.4 15.0 %copy-start.3 = (s32[8,2,8]{2,1,0:T(2,128)S(1)}, s32[8,2,8]{2,1,0:T(2,128)}, u32[]{:S(2)}) copy-start(s32[8,2,8]{2,1,0:T(2,128)} %fill_ref.1) | copy-start | bytes 1540
  29.4 41.8 %all-to-all-start = ((f32[256,1,296]{2,1,0:T(1,128)}), f32[256,1,296]{2,1,0:T(1,128)S(1)}, u32[]{:S(2)}, u32[]{:S(2)}) async-start(f32[256,1,296]{2,1,0:T(1,128)} %send_panels.1), calls=%async_computation | async-start | bytes 786432 | tf_op jit(solution)/shard_map/all_to_all | solution.py:528

commit v5 on v4

--- a/solution.py
+++ b/solution.py
@@ -17,7 +17,8 @@
 NE = 296
 SLOTS = LZ * PPL
 LANES = 128
-GRANT = 58
+GRANT = 52
+UNROLL = 4
 ROWS = CXL * CYL * SLOTS // LANES
 SOFTENING = 0.01
 SURFACE_REACH = 1.05
@@ -124,25 +125,23 @@
 def add_checks(levels, p_ref, check_ref):
     for n, h in enumerate(levels):
         ys = lattice_y(h)
-        for squares, tiles in ((a_squares, A_TILES), (bc_squares, B_TILES + C_TILES)):
-
-            def gather(r, sums):
-                x8, y8, z8, w8 = row_of(p_ref, r)
-                y_parts = [square(ys[b] - y8) for b in range(P_ORD)]
-                return [
-                    total + w8 * lax.rsqrt(d2)
-                    for total, d2 in zip(sums, squares(x8, z8, y_parts))
-                ]
-
-            sums = lax.fori_loop(
-                0, ROWS, gather, [jnp.zeros((8, LANES), jnp.float32) for _ in tiles], unroll=2
-            )
-            for i, (total, tile) in enumerate(zip(sums, tiles)):
-                filled = jnp.broadcast_to(jnp.sum(total, axis=1, keepdims=True), (8, LANES))
-                if squares is bc_squares and i >= len(B_TILES):
-                    check_ref[n, strided_rows(*tile), :] = filled[1:7]
-                else:
-                    check_ref[n, pl.ds(first_row(*tile), 8), :] = filled
+        tiles = A_TILES + B_TILES + C_TILES
+
+        def gather(r, sums):
+            x8, y8, z8, w8 = row_of(p_ref, r)
+            y_parts = [square(ys[b] - y8) for b in range(P_ORD)]
+            gaps = list(a_squares(x8, z8, y_parts)) + list(bc_squares(x8, z8, y_parts))
+            return [total + w8 * lax.rsqrt(d2) for total, d2 in zip(sums, gaps)]
+
+        sums = lax.fori_loop(
+            0, ROWS, gather, [jnp.zeros((8, LANES), jnp.float32) for _ in tiles], unroll=UNROLL
+        )
+        for i, (total, tile) in enumerate(zip(sums, tiles)):
+            filled = jnp.broadcast_to(jnp.sum(total, axis=1, keepdims=True), (8, LANES))
+            if i >= len(A_TILES + B_TILES):
+                check_ref[n, strided_rows(*tile), :] = filled[1:7]
+            else:
+                check_ref[n, pl.ds(first_row(*tile), 8), :] = filled
 
 
 def check_kernel(h, own_ref, check_ref, p_ref):
@@ -162,21 +161,39 @@
     )(own)
 
 
+def halves(value):
+    coarse = value.astype(jnp.bfloat16)
+    return coarse, (value - coarse.astype(jnp.float32)).astype(jnp.bfloat16)
+
+
+def product(rows, matrix):
+    coarse, fine = halves(rows)
+    count = rows.shape[0]
+    wide_part, narrow_part = halves(matrix)
+    both = jnp.concatenate([coarse.astype(jnp.float32), fine.astype(jnp.float32)], axis=0)
+    both = jnp.dot(
+        both.astype(jnp.bfloat16), wide_part, preferred_element_type=jnp.float32
+    )
+    rest = jnp.dot(coarse, narrow_part, preferred_element_type=jnp.float32)
+    return both[:count] + (both[count:] + rest)
+
+
 def send_kernel(
     span_x, span_y, lists_ref, first_ref, second_ref, own_ref, up_hbm, m2l_hbm, down_hbm,
     out_ref, p_ref, up_ref, m2l_ref, down_ref, check_ref, row_ref, column_ref, panel_ref, sems,
 ):
-    copies = [pltpu.make_async_copy(up_hbm, up_ref, sems.at[0])]
-    copies += [
-        pltpu.make_async_copy(m2l_hbm.at[h], m2l_ref.at[h], sems.at[1 + h]) for h in range(LEV)
+    up_copy = pltpu.make_async_copy(up_hbm, up_ref, sems.at[0])
+    down_copy = pltpu.make_async_copy(down_hbm, down_ref, sems.at[1])
+    level_copies = [
+        pltpu.make_async_copy(m2l_hbm.at[h], m2l_ref.at[h], sems.at[2 + h]) for h in range(LEV)
     ]
-    copies.append(pltpu.make_async_copy(down_hbm, down_ref, sems.at[1 + LEV]))
+    copies = [up_copy, level_copies[2], down_copy, level_copies[1], level_copies[0]]
     for copy in copies:
         copy.start()
     row_ref[...] = jnp.zeros((8, 384), jnp.float32)
     fill_points(own_ref, p_ref)
     add_checks([LEV], p_ref, check_ref)
-    copies[0].wait()
+    up_copy.wait()
     for h in range(LEV):
         for low, high in CHUNKS:
             total = jnp.zeros((8, high - low), jnp.float32)
@@ -188,8 +205,12 @@
     for h in range(LEV):
         column_ref[h] = jnp.broadcast_to(flipped[:NE, h : h + 1], (NE, LANES))
 
-    for h in range(LEV):
-        copies[1 + h].wait()
+    out_ref[...] = jnp.zeros(out_ref.shape, jnp.float32)
+    index_x = lax.axis_index("gx")
+    index_y = lax.axis_index("gy")
+
+    def translated(h):
+        level_copies[h].wait()
 
         def translate(k, carry):
             for low, high in CHUNKS:
@@ -203,26 +224,9 @@
             return carry
 
         lax.fori_loop(0, K, translate, 0)
-
-    copies[1 + LEV].wait()
-    panels = [jnp.sum(panel_ref[h], axis=1) for h in range(LEV)]
-    top = panels[2]
-    middle = jnp.concatenate(
-        [panels[1]]
-        + [
-            jnp.dot(top, down_ref[1, side], precision=PRECISE, preferred_element_type=jnp.float32)
-            for side in range(2)
-        ],
-        axis=0,
-    )
-    lower = [
-        jnp.dot(middle, down_ref[0, side], precision=PRECISE, preferred_element_type=jnp.float32)
-        for side in range(2)
-    ]
-    out_ref[...] = jnp.zeros(out_ref.shape, jnp.float32)
-    index_x = lax.axis_index("gx")
-    index_y = lax.axis_index("gy")
-    for h in range(1, LEV + 1):
+        return jnp.sum(panel_ref[h], axis=1)
+
+    def spread(h, row_for):
         offset = span_x * (span_y - (span_y >> h - 1))
         across = span_y >> h
         bits = across.bit_length() - 1
@@ -231,12 +235,25 @@
             box = (own_box - lists_ref[k, offset]) & (span_x * across - 1)
             first = (box >> bits) * span_y + ((box & (across - 1)) << h)
             for j in range(2**h):
-                if h == 1:
-                    value = panels[0][k : k + 1]
-                else:
-                    start = 8 * (h - 2 + j // 4) + k
-                    value = lower[j // 2 % 2][start : start + 1]
-                out_ref[first + j] += value
+                out_ref[first + j] += row_for(k, j)
+
+    top = translated(2)
+    down_copy.wait()
+    top = [product(top, down_ref[1, side]) for side in range(2)]
+    middle = jnp.concatenate([translated(1)] + top, axis=0)
+    lower = [product(middle, down_ref[0, side]) for side in range(2)]
+
+    def second_row(k, j):
+        return lower[j // 2][k : k + 1]
+
+    def third_row(k, j):
+        start = K * (1 + j // 4) + k
+        return lower[j // 2 % 2][start : start + 1]
+
+    spread(3, third_row)
+    spread(2, second_row)
+    low_panel = translated(0)
+    spread(1, lambda k, j: low_panel[k : k + 1])
 
 
 def send_panels(lists, first, second, own, up_ops, m2l_ops, down_ops, span_x, span_y):
@@ -462,6 +479,9 @@
         rows = []
         for n in range(8):
             whole = sum_ref[8 * group + n]
+            if n % 2:
+                rows.append(jnp.sum(jnp.transpose(whole), axis=0, keepdims=True))
+                continue
             coarse = whole.astype(jnp.bfloat16)
             fine = (whole - coarse.astype(jnp.float32)).astype(jnp.bfloat16)
             added = jnp.dot(

time: 76.4 us -> 74.7 us (0.978)
  Pallas kernels: 44.5 us -> 42.3 us
  local copies, waits for them, and re-layouts: 3.02 us -> 1.69 us
  waiting for transfers between devices: 0.41 us -> 1.69 us
  starting transfers between devices: 26 us -> 26.9 us
    unnamed x9 -> x5, local copies, waits for them, and re-layouts: 2.24 us -> 0.92 us
    ppermute x2, waiting for transfers between devices: 0.4 us -> 1.68 us  [swapped(): outside = lax.ppermute(jnp.where(even, head, tail), axis, second)]
    pallas_call x2, Pallas kernels: 5.64 us -> 4.42 us  [one_check(): pl.pallas_call(functools.partial(check_kernel, h), out_shape=jax.ShapeDty...]
    pallas_call x1, Pallas kernels: 8.15 us -> 7.07 us  [send_panels(): pl.pallas_call(functools.partial(send_kernel, span_x, span_y), out_shape=...]
    all_to_all x1, starting transfers between devices: 14.9 us -> 15.7 us  [per_device(): lax.all_to_all(sent, ('gx', 'gy'), split_axis=0, concat_axis=0, tiled=True)]
where the time goes in v5:
time: 74.7 us; the launch traced here: 73.7 us
  Pallas kernels  42.3 us (57%)
  starting transfers between devices  26.9 us (36%)
  local copies, waits for them, and re-layouts  1.69 us (2%)
  waiting for transfers between devices  1.69 us (2%)
  other arithmetic  0.95 us (1%)
    pallas_call x1, Pallas kernels, near_sums(): pl.pallas_call(near_kernel, out_shape=(jax.ShapeDtypeStruct((LEAVES, LANE...  27 us
    all_to_all x1, starting transfers between devices, per_device(): lax.all_to_all(sent, ('gx', 'gy'), split_axis=0, concat_axis=0, tiled=True)  15.7 us
    pallas_call x1, Pallas kernels, send_panels(): pl.pallas_call(functools.partial(send_kernel, span_x, span_y), out_shape=...  7.07 us
    ppermute x2, starting transfers between devices, swapped(): inside = lax.ppermute(jnp.where(even, tail, head), axis, first)  6.24 us
    ppermute x2, starting transfers between devices, swapped(): outside = lax.ppermute(jnp.where(even, head, tail), axis, second)  4.9 us
    pallas_call x2, Pallas kernels, one_check(): pl.pallas_call(functools.partial(check_kernel, h), out_shape=jax.ShapeDty...  4.42 us
    pallas_call x1, Pallas kernels, far_and_sum(): pl.pallas_call(far_kernel, out_shape=jax.ShapeDtypeStruct((CXL, CYL, SLOT...  3.79 us
    ppermute x2, waiting for transfers between devices, swapped(): outside = lax.ppermute(jnp.where(even, head, tail), axis, second)  1.68 us
  transfers between devices with their start and end apart: 5, of which 1 were waited for; matrix products, arithmetic and copies ran while one was open for 0% of the time, Pallas kernels for 43%

profile of v5, /device:TPU:1, one launch (start us, length us, event | category | flops | bytes accessed | tf_op | source)
XLA Modules:
  0.0 73.7 jit_solution(7015257208092308368)
XLA Ops:
  0.0 0.0 copy-start.1
  0.0 0.7 copy_convert_fusion
  0.7 0.9 %copy.10 = f32[3,8,2,512]{3,1,0,2:T(8,128)S(1)} copy(f32[3,8,2,512]{3,2,1,0:T(2,128)} %param.7) | data formatting | bytes 196608 | tf_op args[0]
  1.6 0.8 %copy_bitcast_fusion = (f32[1,8,2,512]{3,1,0,2:T(8,128)S(1)}, f32[1,8,2,512]{3,1,0,2:T(8,128)S(1)}) fusion(f32[8,2,512]{2,1,0:T(2,128)} %param.8, f32[8,2,8]{2,0,1:T(8,128)S(1)} %copy_convert_fusion), kind=kLoop, calls=%fused_computation.11 | loop fusion | bytes 98816 | tf_op jit(solution)/shard_map/broadcast_in_dim | solution.py:537
  2.5 0.7 collective-permute-start
  3.1 6.1 %collective-permute-start.1 = (f32[2,5,1,512]{3,2,1,0:T(1,128)S(1)}, f32[2,5,1,512]{3,2,1,0:T(1,128)S(1)}, u32[]{:S(2)}, u32[]{:S(2)}) collective-permute-start(f32[2,5,1,512]{3,2,1,0:T(1,128)S(1)} %get-tuple-element.28), channel_id=1, source_target_pairs={{0,32},{32,0},{64,96},{96,64},{128,160},{160,128},{192,224},{224,1... | collective-permute-start | bytes 61448 | tf_op jit(solution)/shard_map/ppermute | solution.py:529
  9.3 2.2 %one_check.2.first_ref = f32[1,296,128]{2,1,0:T(8,128)S(1)} custom-call(f32[2,5,8,512]{3,2,1,0:T(8,128)S(1)} %maximum_bitcast_fusion.own_ref), custom_call_target="tpu_custom_call" | custom-call | tf_op jit(solution)/shard_map/one_check/pallas_call | solution.py:153
  11.5 0.0 collective-permute-done
  11.5 0.0 collective-permute-done.1
  11.6 0.1 pad_maximum_fusion.1
  11.7 4.2 %collective-permute-start.2 = (f32[1,5,10,512]{3,2,1,0:T(8,128)S(1)}, f32[1,5,10,512]{3,2,1,0:T(8,128)S(1)}, u32[]{:S(2)}, u32[]{:S(2)}) collective-permute-start(f32[1,5,10,512]{3,2,1,0:T(8,128)S(1)} %get-tuple-element.26), channel_id=1, source_target_pairs={{1,2},{2,1},{3,4},{4,3},{5,6},{6,5},{7,8},{8,7},{9,10},{10,9},{11,... | collective-permute-start | bytes 307208 | tf_op jit(solution)/shard_map/ppermute | solution.py:528
  15.9 0.1 collective-permute-start.3
  16.0 2.2 %one_check.3.second_ref = f32[1,296,128]{2,1,0:T(8,128)S(1)} custom-call(f32[2,5,8,512]{3,2,1,0:T(8,128)S(1)} %maximum_bitcast_fusion.own_ref), custom_call_target="tpu_custom_call" | custom-call | tf_op jit(solution)/shard_map/one_check/pallas_call | solution.py:153
  18.2 1.7 %collective-permute-done.2 = f32[1,5,10,512]{3,2,1,0:T(8,128)S(1)} collective-permute-done((f32[1,5,10,512]{3,2,1,0:T(8,128)S(1)}, f32[1,5,10,512]{3,2,1,0:T(8,128)S(1)}, u32[]{:S(2)}, u32[]{:S(2)}) %collective-permute-start.2) | collective-permute-done | bytes 102432 | tf_op jit(solution)/shard_map/ppermute | solution.py:528
  19.9 0.0 collective-permute-done.3
  20.0 0.0 copy-done.1
  20.0 7.1 %send_panels.1 = f32[256,1,296]{2,1,0:T(1,128)} custom-call(s32[8,224]{1,0:T(8,128)S(1)} %bitcast.7, f32[1,296,128]{2,1,0:T(8,128)S(1)} %one_check.2.first_ref, f32[1,296,128]{2,1,0:T(8,128)S(1)} %one_check.3.second_ref, f32[2,5,8,512]{3,2,1,0:T(8,128)S(1)} %maximum_bitcast_fusion.own_ref, f32[3,296,296]{2,1,0:T(8,128)} %up_hbm.1, ...), custom_call_target="tpu_custom_call" | custom-call | tf_op jit(solution)/shard_map/send_panels/pallas_call | solution.py:260
  27.0 0.0 copy-start
  27.1 15.7 %all-to-all-start = ((f32[256,1,296]{2,1,0:T(1,128)}), f32[256,1,296]{2,1,0:T(1,128)S(1)}, u32[]{:S(2)}, u32[]{:S(2)}) async-start(f32[256,1,296]{2,1,0:T(1,128)} %send_panels.1), calls=%async_computation | async-start | bytes 786432 | tf_op jit(solution)/shard_map/all_to_all | solution.py:548
  42.8 0.0 copy-done
  42.9 27.0 %near_sums.1 = (f32[64,128]{1,0:T(8,128)S(1)}, f32[4,64,128]{2,1,0:T(8,128)S(1)}) custom-call(s32[8,2,8]{2,1,0:T(2,128)S(1)} %copy-done, f32[4,5,10,512]{3,2,1,0:T(8,128)S(1)} %pad_maximum_fusion.table_ref), custom_call_target="tpu_custom_call" | custom-call | tf_op jit(solution)/shard_map/near_sums/pallas_call | solution.py:498
  69.9 0.0 all-to-all-done.parts_ref
  69.9 3.8 %far_and_sum.1 = f32[8,2,512]{2,1,0:T(2,128)} custom-call(f32[4,64,128]{2,1,0:T(8,128)S(1)} %get-tuple-element.18.points_ref, f32[64,128]{1,0:T(8,128)S(1)} %get-tuple-element.19.near_ref, f32[256,1,296]{2,1,0:T(1,128)S(1)} %all-to-all-done.parts_ref), custom_call_target="tpu_custom_call" | custom-call | tf_op jit(solution)/shard_map/far_and_sum/pallas_call | solution.py:330
  (6 shorter events, 0.2 us)
Async XLA Ops:
  0.0 20.0 %copy-start.1 = (s32[224,8]{0,1:T(8,128)S(1)}, s32[224,8]{0,1:T(8,128)}, u32[]{:S(2)}) copy-start(s32[224,8]{0,1:T(8,128)} %param.13) | copy-start | bytes 21508
  2.5 9.0 %collective-permute-start = (f32[2,5,1,512]{3,2,1,0:T(1,128)S(1)}, f32[2,5,1,512]{3,2,1,0:T(1,128)S(1)}, u32[]{:S(2)}, u32[]{:S(2)}) collective-permute-start(f32[2,5,1,512]{3,2,1,0:T(1,128)S(1)} %get-tuple-element.27), channel_id=1, source_target_pairs={{32,64},{64,32},{96,128},{128,96},{160,192},{192,160},{33,65},{65,... | collective-permute-start | bytes 61448 | tf_op jit(solution)/shard_map/ppermute | solution.py:528
  3.1 8.4 %collective-permute-start.1 = (f32[2,5,1,512]{3,2,1,0:T(1,128)S(1)}, f32[2,5,1,512]{3,2,1,0:T(1,128)S(1)}, u32[]{:S(2)}, u32[]{:S(2)}) collective-permute-start(f32[2,5,1,512]{3,2,1,0:T(1,128)S(1)} %get-tuple-element.28), channel_id=1, source_target_pairs={{0,32},{32,0},{64,96},{96,64},{128,160},{160,128},{192,224},{224,1... | collective-permute-start | bytes 61448 | tf_op jit(solution)/shard_map/ppermute | solution.py:529
  11.7 8.2 %collective-permute-start.2 = (f32[1,5,10,512]{3,2,1,0:T(8,128)S(1)}, f32[1,5,10,512]{3,2,1,0:T(8,128)S(1)}, u32[]{:S(2)}, u32[]{:S(2)}) collective-permute-start(f32[1,5,10,512]{3,2,1,0:T(8,128)S(1)} %get-tuple-element.26), channel_id=1, source_target_pairs={{1,2},{2,1},{3,4},{4,3},{5,6},{6,5},{7,8},{8,7},{9,10},{10,9},{11,... | collective-permute-start | bytes 307208 | tf_op jit(solution)/shard_map/ppermute | solution.py:528
  15.9 4.0 %collective-permute-start.3 = (f32[1,5,10,512]{3,2,1,0:T(8,128)S(1)}, f32[1,5,10,512]{3,2,1,0:T(8,128)S(1)}, u32[]{:S(2)}, u32[]{:S(2)}) collective-permute-start(f32[1,5,10,512]{3,2,1,0:T(8,128)S(1)} %get-tuple-element.25), channel_id=1, source_target_pairs={{0,1},{1,0},{2,3},{3,2},{4,5},{5,4},{6,7},{7,6},{8,9},{9,8},{10,11... | collective-permute-start | bytes 307208 | tf_op jit(solution)/shard_map/ppermute | solution.py:529
  27.0 15.8 %copy-start = (s32[8,2,8]{2,1,0:T(2,128)S(1)}, s32[8,2,8]{2,1,0:T(2,128)}, u32[]{:S(2)}) copy-start(s32[8,2,8]{2,1,0:T(2,128)} %fill_ref.1) | copy-start | bytes 1540
  27.1 42.8 %all-to-all-start = ((f32[256,1,296]{2,1,0:T(1,128)}), f32[256,1,296]{2,1,0:T(1,128)S(1)}, u32[]{:S(2)}, u32[]{:S(2)}) async-start(f32[256,1,296]{2,1,0:T(1,128)} %send_panels.1), calls=%async_computation | async-start | bytes 786432 | tf_op jit(solution)/shard_map/all_to_all | solution.py:548

commit v6 on v5

--- a/solution.py
+++ b/solution.py
@@ -348,11 +348,12 @@
 TILES = PPL // 8
 LEAVES = CXL * LZ
 PARTS = 3
-CHOICE = 3 * LZ
+PLACES = 4
+CHOICE = PLACES * LZ
 
 
 def near_kernel(
-    fill_ref, table_ref, out_ref, points_ref, source_ref, sum_ref, turn_ref, place_ref
+    fill_ref, table_ref, out_ref, points_ref, source_ref, sum_ref, turn_ref, place_ref, back_ref
 ):
     lanes = lax.broadcasted_iota(jnp.int32, (8, LANES), 1)
     slots = lax.broadcasted_iota(jnp.int32, (8, LANES), 0)
@@ -396,9 +397,15 @@
                     points_ref[n, pl.ds(z, CXL, stride=LZ), :] = plane[1 : CXL + 1]
 
     turn_ref[...] = jnp.zeros(turn_ref.shape, jnp.float32)
+    back_ref[...] = jnp.zeros(back_ref.shape, jnp.float32)
     tables = [[], []]
     for x in range(CXL):
-        rest = jnp.concatenate([points_ref[c, x * LZ : (x + 1) * LZ, :] for c in range(3)], axis=0)
+        first = (x + 1) * PAD_Z + 1
+        rest = jnp.concatenate(
+            [points_ref[c, x * LZ : (x + 1) * LZ, :] for c in range(3)]
+            + [source_ref[4, first : first + LZ, :]],
+            axis=0,
+        )
         for part in range(PARTS):
             rounded = rest.astype(jnp.bfloat16).astype(jnp.float32)
             turn_ref[CHOICE * part : CHOICE * (part + 1), :] = rounded
@@ -411,84 +418,87 @@
     row = jnp.where(row < PARTS * CHOICE, row % CHOICE, -1)
     for z in range(LZ):
         chosen = jnp.concatenate(
-            [(row == c * LZ + z).astype(jnp.float32) for c in range(3)], axis=1
+            [(row == c * LZ + z).astype(jnp.float32) for c in range(PLACES)], axis=1
         ).astype(jnp.bfloat16)
         for y in range(CYL):
             place_ref[y, z] = jnp.dot(tables[y], chosen, preferred_element_type=jnp.float32)
 
-    def add_tiles(leaf, step):
+    def add_tiles(leaf, step, at_edge):
         x = leaf // LZ
         z = leaf % LZ
         targets = []
+        own_weights = []
         for u in range(STEP):
             start = pl.multiple_of(x * PPL + 8 * (STEP * step + u), 8)
             low, high = [
                 [
                     place_ref[y, z, pl.ds(start, 8), LANES * c : LANES * (c + 1)]
-                    for c in range(3)
+                    for c in range(PLACES)
                 ]
                 for y in range(CYL)
             ]
+            own_weights.append([place.pop() for place in (low, high)])
             for place in (low, high):
                 place.append(square(place[0]) + square(place[1]) + square(place[2]))
             mixed = [jnp.where(lower_half, l, h) for l, h in zip(low, high)]
             targets.append((low, high, mixed))
         sums = [[None] * 3 for _ in range(STEP)]
+
+        def plus(old, value):
+            return value if old is None else old + value
+
         for shift_x in range(3):
             for shift_z in range(3):
                 row = (x + shift_x) * PAD_Z + z + shift_z
+                middle = shift_x == 1 and shift_z == 1
+                forward = 3 * shift_x + shift_z > 4
                 for side in range(2):
+                    if side == 0 and not (middle or forward or (at_edge and shift_x == 0)):
+                        continue
                     mx, my, mz, norm, weight = [
                         wide(source_ref[PLANES * side + c, pl.ds(row, 1), :]) for c in range(PLANES)
                     ]
+                    back = None
                     for u in range(STEP):
                         for n in (0, 1) if side == 0 else (2,):
                             tx, ty, tz, own_norm = targets[u][n]
                             d2 = (own_norm + norm) + tx * mx + ty * my + tz * mz
-                            value = weight * lax.rsqrt(d2)
-                            if side == 0 and shift_x == 1 and shift_z == 1:
+                            strength = lax.rsqrt(d2)
+                            if side == 0 and middle:
                                 itself = lanes == slots + (8 * (STEP * step + u) + PPL * n)
-                                value = jnp.where(itself, 0.0, value)
-                            old = sums[u][n]
-                            sums[u][n] = value if old is None else old + value
+                                strength = jnp.where(itself, 0.0, strength)
+                            sums[u][n] = plus(sums[u][n], weight * strength)
+                            if side == 0 and forward:
+                                back = plus(back, own_weights[u][n] * strength)
+                    if back is not None:
+                        back_ref[row] += back
         for u in range(STEP):
             low, high, mixed = sums[u]
             start = pl.multiple_of(8 * (STEP * step + u), 8)
             sum_ref[leaf, pl.ds(start, 8), :] = low + jnp.where(lower_half, mixed, 0.0)
             sum_ref[leaf, pl.ds(PPL + start, 8), :] = high + jnp.where(lower_half, 0.0, mixed)
 
-    def one_leaf_pair(leaf, carry):
+    def one_leaf_pair(at_edge, leaf, carry):
         x = leaf // LZ
         z = leaf % LZ
         held = jnp.maximum(fill_ref[x, 0, z], fill_ref[x, 1, z])
 
         def more(step, inner):
-            add_tiles(leaf, step)
+            add_tiles(leaf, step, at_edge)
             return inner
 
         lax.fori_loop(0, (held + 8 * STEP - 1) // (8 * STEP), more, 0)
         return carry
 
-    lax.fori_loop(0, LEAVES, one_leaf_pair, 0)
-    ones = jnp.ones((2 * LANES, LANES), jnp.bfloat16)
-    diagonal = lax.broadcasted_iota(jnp.int32, (LANES, LANES), 0) == lax.broadcasted_iota(
-        jnp.int32, (LANES, LANES), 1
-    )
-
+    lax.fori_loop(0, LZ, functools.partial(one_leaf_pair, True), 0)
+    lax.fori_loop(LZ, LEAVES, functools.partial(one_leaf_pair, False), 0)
     def finish(group, carry):
-        rows = []
-        for n in range(8):
-            whole = sum_ref[8 * group + n]
-            if n % 2:
-                rows.append(jnp.sum(jnp.transpose(whole), axis=0, keepdims=True))
-                continue
-            coarse = whole.astype(jnp.bfloat16)
-            fine = (whole - coarse.astype(jnp.float32)).astype(jnp.bfloat16)
-            added = jnp.dot(
-                jnp.concatenate([coarse, fine], axis=1), ones, preferred_element_type=jnp.float32
-            )
-            rows.append(jnp.sum(jnp.where(diagonal, added, 0.0), axis=0, keepdims=True))
-        out_ref[pl.ds(pl.multiple_of(8 * group, 8), 8), :] = jnp.concatenate(rows, axis=0)
+        rows = [
+            jnp.sum(jnp.transpose(sum_ref[8 * group + n]), axis=0, keepdims=True)
+            for n in range(8)
+        ]
+        back = jnp.sum(back_ref[pl.ds((group + 1) * PAD_Z + 1, LZ)], axis=1)
+        out_ref[pl.ds(pl.multiple_of(8 * group, 8), 8), :] = jnp.concatenate(rows, axis=0) + back
         return carry
 
     lax.fori_loop(0, LEAVES // 8, finish, 0)
@@ -513,7 +523,8 @@
             pltpu.VMEM((2 * PLANES, (CXL + 2) * PAD_Z, LANES), jnp.float32),
             pltpu.VMEM((LEAVES, LANES, LANES), jnp.float32),
             pltpu.VMEM((LANES, LANES), jnp.float32),
-            pltpu.VMEM((CYL, LZ, CXL * PPL, 3 * LANES), jnp.float32),
+            pltpu.VMEM((CYL, LZ, CXL * PPL, PLACES * LANES), jnp.float32),
+            pltpu.VMEM(((CXL + 2) * PAD_Z, 8, LANES), jnp.float32),
         ],
         compiler_params=pltpu.CompilerParams(vmem_limit_bytes=28 * 2**20),
         name="near_sums",

time: 74.7 us -> 71.5 us (0.957)
  Pallas kernels: 42.3 us -> 39.8 us
    pallas_call x1, Pallas kernels: 27 us -> 24.5 us  [near_sums(): pl.pallas_call(near_kernel, out_shape=(jax.ShapeDtypeStruct((LEAVES, LANE...]
  transfers between devices with their start and end apart: 5 -> 5, of which waited for: 1 -> 1; matrix products, arithmetic and copies ran while one was open for 0% -> 0% of each run, Pallas kernels for 43% -> 41%
where the time goes in v6:
time: 71.5 us; the launch traced here: 71.1 us
  Pallas kernels  39.8 us (56%)
  starting transfers between devices  26.9 us (38%)
  local copies, waits for them, and re-layouts  1.69 us (2%)
  waiting for transfers between devices  1.69 us (2%)
  other arithmetic  0.95 us (1%)
    pallas_call x1, Pallas kernels, near_sums(): pl.pallas_call(near_kernel, out_shape=(jax.ShapeDtypeStruct((LEAVES, LANE...  24.5 us
    all_to_all x1, starting transfers between devices, per_device(): lax.all_to_all(sent, ('gx', 'gy'), split_axis=0, concat_axis=0, tiled=True)  15.7 us
    pallas_call x1, Pallas kernels, send_panels(): pl.pallas_call(functools.partial(send_kernel, span_x, span_y), out_shape=...  7.07 us
    ppermute x2, starting transfers between devices, swapped(): inside = lax.ppermute(jnp.where(even, tail, head), axis, first)  6.24 us
    ppermute x2, starting transfers between devices, swapped(): outside = lax.ppermute(jnp.where(even, head, tail), axis, second)  4.9 us
    pallas_call x2, Pallas kernels, one_check(): pl.pallas_call(functools.partial(check_kernel, h), out_shape=jax.ShapeDty...  4.42 us
    pallas_call x1, Pallas kernels, far_and_sum(): pl.pallas_call(far_kernel, out_shape=jax.ShapeDtypeStruct((CXL, CYL, SLOT...  3.79 us
    ppermute x2, waiting for transfers between devices, swapped(): outside = lax.ppermute(jnp.where(even, head, tail), axis, second)  1.68 us
  transfers between devices with their start and end apart: 5, of which 1 were waited for; matrix products, arithmetic and copies ran while one was open for 0% of the time, Pallas kernels for 41%

profile of v6, /device:TPU:1, one launch (start us, length us, event | category | flops | bytes accessed | tf_op | source)
XLA Modules:
  0.0 71.1 jit_solution(8774774077074795104)
XLA Ops:
  0.0 0.0 copy-start.1
  0.0 0.7 %copy_convert_fusion = f32[8,2,8]{2,0,1:T(8,128)S(1)} fusion(s32[8,2,8]{2,1,0:T(2,128)} %fill_ref.1), kind=kLoop, calls=%fused_computation.13 | loop fusion | flops 128 | bytes 1024 | tf_op jit(solution)/shard_map/convert_element_type | solution.py:547
  0.7 0.9 %copy.10 = f32[3,8,2,512]{3,1,0,2:T(8,128)S(1)} copy(f32[3,8,2,512]{3,2,1,0:T(2,128)} %param.7) | data formatting | bytes 196608 | tf_op args[0]
  1.6 0.8 %copy_bitcast_fusion = (f32[1,8,2,512]{3,1,0,2:T(8,128)S(1)}, f32[1,8,2,512]{3,1,0,2:T(8,128)S(1)}) fusion(f32[8,2,512]{2,1,0:T(2,128)} %param.8, f32[8,2,8]{2,0,1:T(8,128)S(1)} %copy_convert_fusion), kind=kLoop, calls=%fused_computation.11 | loop fusion | bytes 98816 | tf_op jit(solution)/shard_map/broadcast_in_dim | solution.py:548
  2.5 0.7 collective-permute-start
  3.1 6.1 %collective-permute-start.1 = (f32[2,5,1,512]{3,2,1,0:T(1,128)S(1)}, f32[2,5,1,512]{3,2,1,0:T(1,128)S(1)}, u32[]{:S(2)}, u32[]{:S(2)}) collective-permute-start(f32[2,5,1,512]{3,2,1,0:T(1,128)S(1)} %get-tuple-element.28), channel_id=1, source_target_pairs={{0,32},{32,0},{64,96},{96,64},{128,160},{160,128},{192,224},{224,1... | collective-permute-start | bytes 61448 | tf_op jit(solution)/shard_map/ppermute | solution.py:540
  9.3 2.2 %one_check.2.first_ref = f32[1,296,128]{2,1,0:T(8,128)S(1)} custom-call(f32[2,5,8,512]{3,2,1,0:T(8,128)S(1)} %maximum_bitcast_fusion.own_ref), custom_call_target="tpu_custom_call" | custom-call | tf_op jit(solution)/shard_map/one_check/pallas_call | solution.py:153
  11.5 0.0 collective-permute-done
  11.5 0.0 collective-permute-done.1
  11.6 0.1 pad_maximum_fusion.1
  11.7 4.2 %collective-permute-start.2 = (f32[1,5,10,512]{3,2,1,0:T(8,128)S(1)}, f32[1,5,10,512]{3,2,1,0:T(8,128)S(1)}, u32[]{:S(2)}, u32[]{:S(2)}) collective-permute-start(f32[1,5,10,512]{3,2,1,0:T(8,128)S(1)} %get-tuple-element.26), channel_id=1, source_target_pairs={{1,2},{2,1},{3,4},{4,3},{5,6},{6,5},{7,8},{8,7},{9,10},{10,9},{11,... | collective-permute-start | bytes 307208 | tf_op jit(solution)/shard_map/ppermute | solution.py:539
  15.9 0.1 collective-permute-start.3
  16.0 2.2 %one_check.3.second_ref = f32[1,296,128]{2,1,0:T(8,128)S(1)} custom-call(f32[2,5,8,512]{3,2,1,0:T(8,128)S(1)} %maximum_bitcast_fusion.own_ref), custom_call_target="tpu_custom_call" | custom-call | tf_op jit(solution)/shard_map/one_check/pallas_call | solution.py:153
  18.2 1.7 %collective-permute-done.2 = f32[1,5,10,512]{3,2,1,0:T(8,128)S(1)} collective-permute-done((f32[1,5,10,512]{3,2,1,0:T(8,128)S(1)}, f32[1,5,10,512]{3,2,1,0:T(8,128)S(1)}, u32[]{:S(2)}, u32[]{:S(2)}) %collective-permute-start.2) | collective-permute-done | bytes 102432 | tf_op jit(solution)/shard_map/ppermute | solution.py:539
  19.9 0.0 collective-permute-done.3
  20.0 0.0 copy-done.1
  20.0 7.1 %send_panels.1 = f32[256,1,296]{2,1,0:T(1,128)} custom-call(s32[8,224]{1,0:T(8,128)S(1)} %bitcast.7, f32[1,296,128]{2,1,0:T(8,128)S(1)} %one_check.2.first_ref, f32[1,296,128]{2,1,0:T(8,128)S(1)} %one_check.3.second_ref, f32[2,5,8,512]{3,2,1,0:T(8,128)S(1)} %maximum_bitcast_fusion.own_ref, f32[3,296,296]{2,1,0:T(8,128)} %up_hbm.1, ...), custom_call_target="tpu_custom_call" | custom-call | tf_op jit(solution)/shard_map/send_panels/pallas_call | solution.py:260
  27.0 0.0 copy-start
  27.1 15.7 %all-to-all-start = ((f32[256,1,296]{2,1,0:T(1,128)}), f32[256,1,296]{2,1,0:T(1,128)S(1)}, u32[]{:S(2)}, u32[]{:S(2)}) async-start(f32[256,1,296]{2,1,0:T(1,128)} %send_panels.1), calls=%async_computation | async-start | bytes 786432 | tf_op jit(solution)/shard_map/all_to_all | solution.py:559
  42.8 0.0 copy-done
  42.9 24.5 %near_sums.1 = (f32[64,128]{1,0:T(8,128)S(1)}, f32[4,64,128]{2,1,0:T(8,128)S(1)}) custom-call(s32[8,2,8]{2,1,0:T(2,128)S(1)} %copy-done, f32[4,5,10,512]{3,2,1,0:T(8,128)S(1)} %pad_maximum_fusion.table_ref), custom_call_target="tpu_custom_call" | custom-call | tf_op jit(solution)/shard_map/near_sums/pallas_call | solution.py:508
  67.3 0.0 all-to-all-done.parts_ref
  67.3 3.8 %far_and_sum.1 = f32[8,2,512]{2,1,0:T(2,128)} custom-call(f32[4,64,128]{2,1,0:T(8,128)S(1)} %get-tuple-element.18.points_ref, f32[64,128]{1,0:T(8,128)S(1)} %get-tuple-element.19.near_ref, f32[256,1,296]{2,1,0:T(1,128)S(1)} %all-to-all-done.parts_ref), custom_call_target="tpu_custom_call" | custom-call | tf_op jit(solution)/shard_map/far_and_sum/pallas_call | solution.py:330
  (6 shorter events, 0.2 us)
Async XLA Ops:
  0.0 20.0 %copy-start.1 = (s32[224,8]{0,1:T(8,128)S(1)}, s32[224,8]{0,1:T(8,128)}, u32[]{:S(2)}) copy-start(s32[224,8]{0,1:T(8,128)} %param.13) | copy-start | bytes 21508
  2.5 9.0 %collective-permute-start = (f32[2,5,1,512]{3,2,1,0:T(1,128)S(1)}, f32[2,5,1,512]{3,2,1,0:T(1,128)S(1)}, u32[]{:S(2)}, u32[]{:S(2)}) collective-permute-start(f32[2,5,1,512]{3,2,1,0:T(1,128)S(1)} %get-tuple-element.27), channel_id=1, source_target_pairs={{32,64},{64,32},{96,128},{128,96},{160,192},{192,160},{33,65},{65,... | collective-permute-start | bytes 61448 | tf_op jit(solution)/shard_map/ppermute | solution.py:539
  3.1 8.4 %collective-permute-start.1 = (f32[2,5,1,512]{3,2,1,0:T(1,128)S(1)}, f32[2,5,1,512]{3,2,1,0:T(1,128)S(1)}, u32[]{:S(2)}, u32[]{:S(2)}) collective-permute-start(f32[2,5,1,512]{3,2,1,0:T(1,128)S(1)} %get-tuple-element.28), channel_id=1, source_target_pairs={{0,32},{32,0},{64,96},{96,64},{128,160},{160,128},{192,224},{224,1... | collective-permute-start | bytes 61448 | tf_op jit(solution)/shard_map/ppermute | solution.py:540
  11.7 8.2 %collective-permute-start.2 = (f32[1,5,10,512]{3,2,1,0:T(8,128)S(1)}, f32[1,5,10,512]{3,2,1,0:T(8,128)S(1)}, u32[]{:S(2)}, u32[]{:S(2)}) collective-permute-start(f32[1,5,10,512]{3,2,1,0:T(8,128)S(1)} %get-tuple-element.26), channel_id=1, source_target_pairs={{1,2},{2,1},{3,4},{4,3},{5,6},{6,5},{7,8},{8,7},{9,10},{10,9},{11,... | collective-permute-start | bytes 307208 | tf_op jit(solution)/shard_map/ppermute | solution.py:539
  15.9 4.0 %collective-permute-start.3 = (f32[1,5,10,512]{3,2,1,0:T(8,128)S(1)}, f32[1,5,10,512]{3,2,1,0:T(8,128)S(1)}, u32[]{:S(2)}, u32[]{:S(2)}) collective-permute-start(f32[1,5,10,512]{3,2,1,0:T(8,128)S(1)} %get-tuple-element.25), channel_id=1, source_target_pairs={{0,1},{1,0},{2,3},{3,2},{4,5},{5,4},{6,7},{7,6},{8,9},{9,8},{10,11... | collective-permute-start | bytes 307208 | tf_op jit(solution)/shard_map/ppermute | solution.py:540
  27.0 15.8 %copy-start = (s32[8,2,8]{2,1,0:T(2,128)S(1)}, s32[8,2,8]{2,1,0:T(2,128)}, u32[]{:S(2)}) copy-start(s32[8,2,8]{2,1,0:T(2,128)} %fill_ref.1) | copy-start | bytes 1540
  27.1 40.3 %all-to-all-start = ((f32[256,1,296]{2,1,0:T(1,128)}), f32[256,1,296]{2,1,0:T(1,128)S(1)}, u32[]{:S(2)}, u32[]{:S(2)}) async-start(f32[256,1,296]{2,1,0:T(1,128)} %send_panels.1), calls=%async_computation | async-start | bytes 786432 | tf_op jit(solution)/shard_map/all_to_all | solution.py:559

commit v7 on v6

--- a/solution.py
+++ b/solution.py
@@ -18,6 +18,7 @@
 SLOTS = LZ * PPL
 LANES = 128
 GRANT = 52
+WHOLE = 60
 UNROLL = 4
 ROWS = CXL * CYL * SLOTS // LANES
 SOFTENING = 0.01
@@ -99,6 +100,51 @@
 
 def row_of(p_ref, r):
     return [wide(p_ref[c, pl.ds(r, 1), :]) for c in range(p_ref.shape[0])]
+
+
+def collect_kernel(
+    positions_hbm, charges_hbm, counts_hbm, own_ref, first_ref, second_ref,
+    positions_ref, charges_ref, counts_ref, sems,
+):
+    even = lax.axis_index("gx") & 1 == 0
+    copies = [
+        pltpu.make_async_copy(positions_hbm, positions_ref, sems.at[0]),
+        pltpu.make_async_copy(charges_hbm, charges_ref, sems.at[1]),
+        pltpu.make_async_copy(counts_hbm, counts_ref, sems.at[2]),
+    ]
+    for copy in copies:
+        copy.start()
+    for copy in copies:
+        copy.wait()
+    for y in range(CYL):
+        own_ref[y, 4] = jnp.zeros((CXL, SLOTS), jnp.float32)
+        own_ref[y, 4, :, :LZ] = counts_ref[:, y, :].astype(jnp.float32)
+        own_ref[y, 3] = charges_ref[:, y, :]
+        for c in range(3):
+            own_ref[y, c] = positions_ref[c, :, y, :]
+        for c in range(5):
+            head = own_ref[y, c, 0:1, :]
+            tail = own_ref[y, c, CXL - 1 : CXL, :]
+            first_ref[y, c] = jnp.where(even, tail, head)
+            second_ref[y, c] = jnp.where(even, head, tail)
+
+
+def collect(positions, charges, counts):
+    face = jax.ShapeDtypeStruct((CYL, 5, 1, SLOTS), jnp.float32)
+    return pl.pallas_call(
+        collect_kernel,
+        out_shape=(jax.ShapeDtypeStruct((CYL, 5, CXL, SLOTS), jnp.float32), face, face),
+        in_specs=[pl.BlockSpec(memory_space=pltpu.HBM)] * 3,
+        out_specs=(pl.BlockSpec(memory_space=pltpu.VMEM),) * 3,
+        scratch_shapes=[
+            pltpu.VMEM((3, CXL, CYL, SLOTS), jnp.float32),
+            pltpu.VMEM((CXL, CYL, SLOTS), jnp.float32),
+            pltpu.VMEM((CXL, CYL, LZ), jnp.int32),
+            pltpu.SemaphoreType.DMA((3,)),
+        ],
+        compiler_params=pltpu.CompilerParams(vmem_limit_bytes=WHOLE * 2**20),
+        name="collect",
+    )(positions, charges, counts)
 
 
 def fill_points(own_ref, p_ref):
@@ -531,33 +577,36 @@
     )(fill, table)
 
 
-def swapped(axis, head, tail):
+def swapped(axis, for_first, for_second):
     count = lax.axis_size(axis)
     even = lax.axis_index(axis) & 1 == 0
     first = [(i, i ^ 1) for i in range(count)]
     second = [(i, i + 1 if i % 2 else i - 1) for i in range(1, count - 1)]
-    outside = lax.ppermute(jnp.where(even, head, tail), axis, second)
-    inside = lax.ppermute(jnp.where(even, tail, head), axis, first)
+    inside = lax.ppermute(for_first, axis, first)
+    outside = lax.ppermute(for_second, axis, second)
     return jnp.where(even, outside, inside), jnp.where(even, inside, outside)
 
 
 def per_device(positions, charges, counts, up_ops, m2l_ops, down_ops, box_lists):
     devices_x = lax.axis_size("gx")
     devices_y = lax.axis_size("gy")
-    filled = jnp.pad(counts.astype(jnp.float32), ((0, 0), (0, 0), (0, SLOTS - LZ)))
-    own = jnp.concatenate([positions, charges[None], filled[None]], axis=0).transpose(2, 0, 1, 3)
-    before, after = swapped("gx", own[:, :, :1], own[:, :, -1:])
+    own, for_first, for_second = collect(positions, charges, counts)
+    before, after = swapped("gx", for_first, for_second)
     first = one_check(1, own)
-    middle = jnp.concatenate([before, own, after], axis=2)
-    middle, first, own = lax.optimization_barrier((middle, first, own))
-    below, above = swapped("gy", middle[:1], middle[1:])
+    before, after, first, own = lax.optimization_barrier((before, after, first, own))
+    even = lax.axis_index("gy") & 1 == 0
+    head, tail = [
+        jnp.concatenate([side[y : y + 1] for side in (before, own, after)], axis=2)
+        for y in range(CYL)
+    ]
+    below, above = swapped("gy", jnp.where(even, tail, head), jnp.where(even, head, tail))
     second = one_check(2, own)
     below, above, second, own = lax.optimization_barrier((below, above, second, own))
     sent = send_panels(
         box_lists.T, first, second, own, up_ops, m2l_ops, down_ops, devices_x, devices_y
     )
     parts = lax.all_to_all(sent, ("gx", "gy"), split_axis=0, concat_axis=0, tiled=True)
-    near, points = near_sums(counts, jnp.concatenate([below, middle, above], axis=0))
+    near, points = near_sums(counts, jnp.concatenate([below, head, tail, above], axis=0))
     return far_and_sum(points, near, parts)
 
 

time: 71.5 us -> 72.2 us (level)
  Pallas kernels: 39.8 us -> 41.5 us
  local copies, waits for them, and re-layouts: 1.69 us -> 2.78 us
  waiting for transfers between devices: 1.69 us -> 0.77 us
  starting transfers between devices: 26.9 us -> 26.1 us
  other arithmetic: 0.95 us -> 0.22 us
    pallas_call x0 -> x1, Pallas kernels: none -> 1.65 us  [collect(): pl.pallas_call(collect_kernel, out_shape=(jax.ShapeDtypeStruct((CYL, 5, C...]
    slice x0 -> x2, local copies, waits for them, and re-layouts: none -> 0.95 us  [per_device(): side[y:y + 1]]
    ppermute x4, waiting for transfers between devices: 1.69 us -> 0.77 us  [the longest x2 0.76 us: swapped(): outside = lax.ppermute(for_second, axis, second)]
    unnamed x5 -> x10, local copies, waits for them, and re-layouts: 0.92 us -> 1.84 us
    broadcast_in_dim x1 -> x0, local copies, waits for them, and re-layouts: 0.77 us -> none  [per_device(): charges[None]]
  transfers between devices with their start and end apart: 5 -> 5, of which waited for: 1 -> 1; matrix products, arithmetic and copies ran while one was open for 0% -> 0% of each run, Pallas kernels for 41% -> 40%
where the time goes in v7:
time: 72.2 us; the launch traced here: 71.7 us
  Pallas kernels  41.5 us (57%)
  starting transfers between devices  26.1 us (36%)
  local copies, waits for them, and re-layouts  2.78 us (4%)
  waiting for transfers between devices  0.77 us (1%)
    pallas_call x1, Pallas kernels, near_sums(): pl.pallas_call(near_kernel, out_shape=(jax.ShapeDtypeStruct((LEAVES, LANE...  24.6 us
    all_to_all x1, starting transfers between devices, per_device(): lax.all_to_all(sent, ('gx', 'gy'), split_axis=0, concat_axis=0, tiled=True)  15 us
    pallas_call x1, Pallas kernels, send_panels(): pl.pallas_call(functools.partial(send_kernel, span_x, span_y), out_shape=...  7.09 us
    ppermute x2, starting transfers between devices, swapped(): inside = lax.ppermute(for_first, axis, first)  6.24 us
    ppermute x2, starting transfers between devices, swapped(): outside = lax.ppermute(for_second, axis, second)  4.9 us
    pallas_call x2, Pallas kernels, one_check(): pl.pallas_call(functools.partial(check_kernel, h), out_shape=jax.ShapeDty...  4.42 us
    pallas_call x1, Pallas kernels, far_and_sum(): pl.pallas_call(far_kernel, out_shape=jax.ShapeDtypeStruct((CXL, CYL, SLOT...  3.79 us
    unnamed x10, local copies, waits for them, and re-layouts  1.84 us
  transfers between devices with their start and end apart: 5, of which 1 were waited for; matrix products, arithmetic and copies ran while one was open for 0% of the time, Pallas kernels for 40%

profile of v7, /device:TPU:1, one launch (start us, length us, event | category | flops | bytes accessed | tf_op | source)
XLA Modules:
  0.0 71.7 jit_solution(9616324567556287978)
XLA Ops:
  0.0 0.0 copy-start.4
  0.0 1.6 %collect.1 = (f32[2,5,8,512]{3,2,1,0:T(8,128)}, f32[2,5,1,512]{3,2,1,0:T(1,128)}, f32[2,5,1,512]{3,2,1,0:T(1,128)}) custom-call(f32[3,8,2,512]{3,2,1,0:T(2,128)} %positions_hbm.1, f32[8,2,512]{2,1,0:T(2,128)} %charges_hbm.1, s32[8,2,8]{2,1,0:T(2,128)} %fill_ref.1), custom_call_target="tpu_custom_call" | custom-call | tf_op jit(solution)/shard_map/collect/pallas_call | solution.py:134
  1.7 0.7 collective-permute-start
  2.3 6.1 %collective-permute-start.1 = (f32[2,5,1,512]{3,2,1,0:T(1,128)}, f32[2,5,1,512]{3,2,1,0:T(1,128)S(1)}, u32[]{:S(2)}, u32[]{:S(2)}) collective-permute-start(f32[2,5,1,512]{3,2,1,0:T(1,128)} %get-tuple-element.19), channel_id=1, source_target_pairs={{0,32},{32,0},{64,96},{96,64},{128,160},{160,128},{192,224},{224,1... | collective-permute-start | bytes 61448 | tf_op jit(solution)/shard_map/ppermute | solution.py:585
  8.5 0.0 copy-start
  8.5 0.9 %copy-done = f32[2,5,8,512]{3,2,1,0:T(8,128)S(1)} copy-done((f32[2,5,8,512]{3,2,1,0:T(8,128)S(1)}, f32[2,5,8,512]{3,2,1,0:T(8,128)}, u32[]{:S(2)}) %copy-start) | copy-done | bytes 163864
  9.4 0.0 copy-start.2
  9.4 2.2 %one_check.2.first_ref = f32[1,296,128]{2,1,0:T(8,128)S(1)} custom-call(f32[2,5,8,512]{3,2,1,0:T(8,128)S(1)} %copy-done), custom_call_target="tpu_custom_call" | custom-call | tf_op jit(solution)/shard_map/one_check/pallas_call | solution.py:199
  11.6 0.0 collective-permute-done
  11.6 0.0 collective-permute-done.1
  11.7 0.9 %fusion.2 = (f32[1,5,8,512]{3,2,1,0:T(8,128)S(1)}, f32[1,5,8,512]{3,2,1,0:T(8,128)S(1)}) fusion(f32[2,5,8,512]{3,2,1,0:T(8,128)} %get-tuple-element.30.own_ref), kind=kLoop, calls=%fused_computation.9 | loop fusion | bytes 327680 | tf_op jit(solution)/shard_map/slice | solution.py:599
  12.6 0.1 fusion
  12.7 4.2 %collective-permute-start.2 = (f32[1,5,10,512]{3,2,1,0:T(8,128)S(1)}, f32[1,5,10,512]{3,2,1,0:T(8,128)S(1)}, u32[]{:S(2)}, u32[]{:S(2)}) collective-permute-start(f32[1,5,10,512]{3,2,1,0:T(8,128)S(1)} %get-tuple-element.34), channel_id=1, source_target_pairs={{1,2},{2,1},{3,4},{4,3},{5,6},{6,5},{7,8},{8,7},{9,10},{10,9},{11,... | collective-permute-start | bytes 307208 | tf_op jit(solution)/shard_map/ppermute | solution.py:586
  17.0 0.1 collective-permute-start.3
  17.1 0.0 copy-start.1
  17.1 0.9 %copy-done.1 = f32[2,5,8,512]{3,2,1,0:T(8,128)S(1)} copy-done((f32[2,5,8,512]{3,2,1,0:T(8,128)S(1)}, f32[2,5,8,512]{3,2,1,0:T(8,128)}, u32[]{:S(2)}) %copy-start.1) | copy-done | bytes 163864
  18.0 2.2 %one_check.3.second_ref = f32[1,296,128]{2,1,0:T(8,128)S(1)} custom-call(f32[2,5,8,512]{3,2,1,0:T(8,128)S(1)} %copy-done.1), custom_call_target="tpu_custom_call" | custom-call | tf_op jit(solution)/shard_map/one_check/pallas_call | solution.py:199
  20.2 0.8 %collective-permute-done.2 = f32[1,5,10,512]{3,2,1,0:T(8,128)S(1)} collective-permute-done((f32[1,5,10,512]{3,2,1,0:T(8,128)S(1)}, f32[1,5,10,512]{3,2,1,0:T(8,128)S(1)}, u32[]{:S(2)}, u32[]{:S(2)}) %collective-permute-start.2) | collective-permute-done | bytes 102432 | tf_op jit(solution)/shard_map/ppermute | solution.py:586
  21.0 0.0 collective-permute-done.3
  21.0 0.0 copy-done.4
  21.0 0.0 copy-done.2
  21.0 7.1 %send_panels.1 = f32[256,1,296]{2,1,0:T(1,128)} custom-call(s32[8,224]{1,0:T(8,128)S(1)} %bitcast.1, f32[1,296,128]{2,1,0:T(8,128)S(1)} %one_check.2.first_ref, f32[1,296,128]{2,1,0:T(8,128)S(1)} %one_check.3.second_ref, f32[2,5,8,512]{3,2,1,0:T(8,128)S(1)} %copy-done.2, f32[3,296,296]{2,1,0:T(8,128)} %up_hbm.1, f32[3,8,296,296]{3,2,1,0:T(8,128)} %m2l_hbm.1, ...), custom_call_target="tpu_custom_call" | custom-call | tf_op jit(solution)/shard_map/send_panels/pallas_call | solution.py:306
  28.1 0.0 copy-start.3
  28.1 15.0 %all-to-all-start = ((f32[256,1,296]{2,1,0:T(1,128)}), f32[256,1,296]{2,1,0:T(1,128)S(1)}, u32[]{:S(2)}, u32[]{:S(2)}) async-start(f32[256,1,296]{2,1,0:T(1,128)} %send_panels.1), calls=%async_computation | async-start | bytes 786432 | tf_op jit(solution)/shard_map/all_to_all | solution.py:608
  43.1 0.1 pad_maximum_fusion.table_ref
  43.2 0.0 copy-done.3
  43.2 24.6 %near_sums.1 = (f32[64,128]{1,0:T(8,128)S(1)}, f32[4,64,128]{2,1,0:T(8,128)S(1)}) custom-call(s32[8,2,8]{2,1,0:T(2,128)S(1)} %copy-done.3, f32[4,5,10,512]{3,2,1,0:T(8,128)S(1)} %pad_maximum_fusion.table_ref), custom_call_target="tpu_custom_call" | custom-call | tf_op jit(solution)/shard_map/near_sums/pallas_call | solution.py:554
  67.8 0.0 all-to-all-done.parts_ref
  67.9 3.8 %far_and_sum.1 = f32[8,2,512]{2,1,0:T(2,128)} custom-call(f32[4,64,128]{2,1,0:T(8,128)S(1)} %get-tuple-element.26.points_ref, f32[64,128]{1,0:T(8,128)S(1)} %get-tuple-element.27.near_ref, f32[256,1,296]{2,1,0:T(1,128)S(1)} %all-to-all-done.parts_ref), custom_call_target="tpu_custom_call" | custom-call | tf_op jit(solution)/shard_map/far_and_sum/pallas_call | solution.py:376
  (3 shorter events, 0.1 us)
Async XLA Ops:
  0.0 21.0 %copy-start.4 = (s32[224,8]{0,1:T(8,128)S(1)}, s32[224,8]{0,1:T(8,128)}, u32[]{:S(2)}) copy-start(s32[224,8]{0,1:T(8,128)} %param.13) | copy-start | bytes 21508
  1.7 10.0 %collective-permute-start = (f32[2,5,1,512]{3,2,1,0:T(1,128)}, f32[2,5,1,512]{3,2,1,0:T(1,128)S(1)}, u32[]{:S(2)}, u32[]{:S(2)}) collective-permute-start(f32[2,5,1,512]{3,2,1,0:T(1,128)} %get-tuple-element.18), channel_id=1, source_target_pairs={{32,64},{64,32},{96,128},{128,96},{160,192},{192,160},{33,65},{65,... | collective-permute-start | bytes 61448 | tf_op jit(solution)/shard_map/ppermute | solution.py:586
  2.3 9.3 %collective-permute-start.1 = (f32[2,5,1,512]{3,2,1,0:T(1,128)}, f32[2,5,1,512]{3,2,1,0:T(1,128)S(1)}, u32[]{:S(2)}, u32[]{:S(2)}) collective-permute-start(f32[2,5,1,512]{3,2,1,0:T(1,128)} %get-tuple-element.19), channel_id=1, source_target_pairs={{0,32},{32,0},{64,96},{96,64},{128,160},{160,128},{192,224},{224,1... | collective-permute-start | bytes 61448 | tf_op jit(solution)/shard_map/ppermute | solution.py:585
  8.5 0.9 %copy-start = (f32[2,5,8,512]{3,2,1,0:T(8,128)S(1)}, f32[2,5,8,512]{3,2,1,0:T(8,128)}, u32[]{:S(2)}) copy-start(f32[2,5,8,512]{3,2,1,0:T(8,128)} %get-tuple-element.30.own_ref) | copy-start | bytes 491524
  9.4 11.6 %copy-start.2 = (f32[2,5,8,512]{3,2,1,0:T(8,128)S(1)}, f32[2,5,8,512]{3,2,1,0:T(8,128)}, u32[]{:S(2)}) copy-start(f32[2,5,8,512]{3,2,1,0:T(8,128)} %get-tuple-element.30.own_ref) | copy-start | bytes 491524
  12.7 8.2 %collective-permute-start.2 = (f32[1,5,10,512]{3,2,1,0:T(8,128)S(1)}, f32[1,5,10,512]{3,2,1,0:T(8,128)S(1)}, u32[]{:S(2)}, u32[]{:S(2)}) collective-permute-start(f32[1,5,10,512]{3,2,1,0:T(8,128)S(1)} %get-tuple-element.34), channel_id=1, source_target_pairs={{1,2},{2,1},{3,4},{4,3},{5,6},{6,5},{7,8},{8,7},{9,10},{10,9},{11,... | collective-permute-start | bytes 307208 | tf_op jit(solution)/shard_map/ppermute | solution.py:586
  17.0 4.0 %collective-permute-start.3 = (f32[1,5,10,512]{3,2,1,0:T(8,128)S(1)}, f32[1,5,10,512]{3,2,1,0:T(8,128)S(1)}, u32[]{:S(2)}, u32[]{:S(2)}) collective-permute-start(f32[1,5,10,512]{3,2,1,0:T(8,128)S(1)} %get-tuple-element.33), channel_id=1, source_target_pairs={{0,1},{1,0},{2,3},{3,2},{4,5},{5,4},{6,7},{7,6},{8,9},{9,8},{10,11... | collective-permute-start | bytes 307208 | tf_op jit(solution)/shard_map/ppermute | solution.py:585
  17.1 0.9 %copy-start.1 = (f32[2,5,8,512]{3,2,1,0:T(8,128)S(1)}, f32[2,5,8,512]{3,2,1,0:T(8,128)}, u32[]{:S(2)}) copy-start(f32[2,5,8,512]{3,2,1,0:T(8,128)} %get-tuple-element.30.own_ref) | copy-start | bytes 491524
  28.1 15.1 %copy-start.3 = (s32[8,2,8]{2,1,0:T(2,128)S(1)}, s32[8,2,8]{2,1,0:T(2,128)}, u32[]{:S(2)}) copy-start(s32[8,2,8]{2,1,0:T(2,128)} %fill_ref.1) | copy-start | bytes 1540
  28.1 39.7 %all-to-all-start = ((f32[256,1,296]{2,1,0:T(1,128)}), f32[256,1,296]{2,1,0:T(1,128)S(1)}, u32[]{:S(2)}, u32[]{:S(2)}) async-start(f32[256,1,296]{2,1,0:T(1,128)} %send_panels.1), calls=%async_computation | async-start | bytes 786432 | tf_op jit(solution)/shard_map/all_to_all | solution.py:608
